TPU v7x, 256 devices: a whole 4x4x8 slice. The times are simulated.
256 devices in a mesh: slab: 64 (over x, z, core), quad: 4 (over y).
Axes of the slice: x: 4, y: 4, z: 8, core: 2. Of those that a mesh axis runs over, the one named last changes fastest.
Arguments:
- right_side: float32 [256, 64, 1024], P('slab', 'quad'), may hold values from -16 to 16
- phase_label: int32 [256, 64, 1024], P('slab', 'quad'), may hold values 0 or 1
- density_gain: float32 [256, 64, 1024], P('slab', 'quad'), may hold values from 0.25 to 1.75
- subdomain: int32 [256, 64, 1024], P('slab', 'quad'), may hold values from 0 to 63, as said below
- block_factor: float32 [64, 256, 256], P('slab', 'quad'), may hold values from -0.03125 to 0.03125
- coupling: float32 [64, 256, 64], P('slab', 'quad'), may hold values from -0.75 to 0.75
Outputs:
- solution_field: float32 [256, 64, 1024], P('slab', 'quad')
- residual: float32 [256, 64, 1024], P('slab', 'quad')
Inputs may be any that keep to these rules, and one draw needn't show every extreme that they name: `subdomain`: within each device the subdomains are 8 x 8 contiguous tiles with jagged edges, each spanning the device's z-planes.
All inputs are finite; a program needn't handle non-finite values. No bound on the sum of `phase_label` on one device may be relied on, other than what follows from the above.
Results may differ from a plain program's by a relative error of at most 0.0075.
Values sent between devices are 32-bit elements; how exact they have to be, the bound alone decides.
No kernel may reach another device: no remote copies, remote signals or barrier semaphores. Data moves between devices by JAX's collectives and lax.ppermute only.
A program may use at most 64 MiB of HBM per device.

v0:
```python
import jax
import jax.numpy as jnp
from jax import lax
from jax.sharding import PartitionSpec as P

LINE = 4
ITERS = 2


HIGH = lax.Precision.HIGHEST


def with_halo(value, sides, width):
    for axis, dim in sides:
        size, length = (lax.axis_size(axis), value.shape[dim])
        up = [(i, (i + 1) % size) for i in range(size - 1)]
        down = [(j, i) for i, j in up]
        last = lax.slice_in_dim(value, length - width, length, axis=dim)
        initial = lax.slice_in_dim(value, 0, width, axis=dim)
        before = lax.ppermute(last, axis, up)
        after = lax.ppermute(initial, axis, down)
        value = jnp.concatenate([before, value, after], axis=dim)
    return value


def prefix(value, axis, combine, identity, reverse):
    length, mine = (lax.axis_size(axis), lax.axis_index(axis))
    everything = jax.tree.map(lambda part: lax.all_gather(part, axis), value)
    start = jax.tree.map(
        lambda part, zero: jnp.broadcast_to(jnp.asarray(zero, part.dtype), part.shape),
        value,
        identity,
    )

    def turn(k, before):
        at = length - 1 - k if reverse else k
        reached = at > mine if reverse else at < mine
        new = combine(before, jax.tree.map(lambda part: part[at], everything))
        return jax.tree.map(lambda a, b: jnp.where(reached, a, b), new, before)

    return lax.fori_loop(0, length, turn, start)


def harmonic(here, there):
    return jnp.where(there > 0, 2.0 * here * there / (here + there), here)


def solve_along_line(diag, lower, upper, rhs):
    shape = rhs.shape
    dd = diag.reshape(-1, LINE, shape[1], shape[2])
    lo = lower.reshape(-1, LINE, shape[1], shape[2])
    up = upper.reshape(-1, LINE, shape[1], shape[2])
    rr = rhs.reshape(-1, LINE, shape[1], shape[2])
    gammas = []
    rhos = []
    denom = dd[:, 0]
    gammas.append(-up[:, 0] / denom)
    rhos.append(rr[:, 0] / denom)
    for j in range(1, LINE):
        denom = dd[:, j] + lo[:, j] * gammas[j - 1]
        gammas.append(-up[:, j] / denom)
        rhos.append((rr[:, j] + lo[:, j] * rhos[j - 1]) / denom)
    values = [None] * LINE
    values[LINE - 1] = rhos[LINE - 1]
    for j in range(LINE - 2, -1, -1):
        values[j] = rhos[j] - gammas[j] * values[j + 1]
    return jnp.stack(values, axis=1).reshape(shape)


def adjacent_cells(center, extended):
    xpad = jnp.pad(center, ((0, 0), (0, 0), (1, 1)))
    return (
        extended[:-2, 1:-1],
        extended[2:, 1:-1],
        extended[1:-1, :-2],
        extended[1:-1, 2:],
        xpad[:, :, :-2],
        xpad[:, :, 2:],
    )


def compose(earlier, later):
    return (
        jnp.dot(later[0], earlier[0], precision=HIGH),
        jnp.dot(later[0], earlier[1], precision=HIGH) + later[1],
    )


def restrict(subdomain, field, count):
    labels = lax.broadcasted_iota(jnp.int32, (count, 1), 0)

    def restrict_plane(total, pair):
        sub_plane, field_plane = pair
        onehot = (sub_plane.reshape(1, -1) == labels).astype(jnp.float32)
        return (total + jnp.dot(onehot, field_plane.reshape(-1), precision=HIGH), None)

    total, unused = lax.scan(restrict_plane, jnp.zeros((count,), jnp.float32), (subdomain, field))
    return total


def interpolate_coarse(subdomain, values):
    count = values.shape[0]
    labels = lax.broadcasted_iota(jnp.int32, (count, 1), 0)

    def interpolate_plane(sub_plane):
        onehot = (sub_plane.reshape(1, -1) == labels).astype(jnp.float32)
        return jnp.dot(values, onehot, precision=HIGH).reshape(sub_plane.shape)

    return lax.map(interpolate_plane, subdomain)


def body(right_side, phase_label, density_gain, subdomain, block_factor, coupling):
    mobility = 1.0 / (density_gain * (0.001 + 0.999 * phase_label.astype(jnp.float32)))
    mext = with_halo(mobility, (("slab", 0), ("quad", 1)), 1)
    near = adjacent_cells(mobility, mext)
    kz_lo = harmonic(mobility, near[0])
    kz_hi = harmonic(mobility, near[1])
    ky_lo = harmonic(mobility, near[2])
    ky_hi = harmonic(mobility, near[3])
    kx_lo = harmonic(mobility, near[4])
    kx_hi = harmonic(mobility, near[5])
    diag = kz_lo + kz_hi + ky_lo + ky_hi + kx_lo + kx_hi
    factor = block_factor[0]
    couple = coupling[0]
    count = couple.shape[0]

    def coarse_solve(coarse_rhs):
        eye = jnp.eye(count, dtype=jnp.float32)
        blank = jnp.zeros((count,), jnp.float32)
        before = prefix((couple, coarse_rhs), "slab", compose, (eye, blank), False)
        u_own = jnp.dot(couple, before[1], precision=HIGH) + coarse_rhs
        flipped = couple.T
        after = prefix(
            (flipped, jnp.dot(flipped, u_own, precision=HIGH)), "slab", compose, (eye, blank), True
        )
        w_own = u_own + after[1]
        return (u_own, w_own)

    def precondition(resid):
        block_part = solve_along_line(diag, kz_lo, kz_hi, resid)
        coarse_in = restrict(subdomain, resid, count)
        coarse_all = lax.all_gather(coarse_in, "quad", axis=0, tiled=True)
        coarse_rhs = jnp.dot(factor, coarse_all, precision=HIGH)
        u_own, w_own = coarse_solve(coarse_rhs)
        coarse_out = lax.psum_scatter(
            jnp.dot(factor.T, w_own, precision=HIGH), "quad", scatter_dimension=0, tiled=True
        )
        precond = block_part + interpolate_coarse(subdomain, coarse_out)
        rz_total = lax.psum(jnp.sum(resid * precond), ("slab", "quad"))
        return (precond, rz_total)

    solution_field = jnp.zeros_like(right_side)
    residual = right_side
    precond, rz = precondition(residual)
    search_direction = precond
    for step in range(ITERS):
        vector_with_halo = with_halo(search_direction, (("slab", 0), ("quad", 1)), 1)
        vector_neighbour = adjacent_cells(search_direction, vector_with_halo)
        image = (
            diag * search_direction
            - kz_lo * vector_neighbour[0]
            - kz_hi * vector_neighbour[1]
            - ky_lo * vector_neighbour[2]
            - ky_hi * vector_neighbour[3]
            - kx_lo * vector_neighbour[4]
            - kx_hi * vector_neighbour[5]
        )
        alpha = rz / lax.psum(jnp.sum(search_direction * image), ("slab", "quad"))
        solution_field = solution_field + alpha * search_direction
        residual = residual - alpha * image
        if step + 1 < ITERS:
            precond, residual_precond_next = precondition(residual)
            search_direction = precond + residual_precond_next / rz * search_direction
            rz = residual_precond_next
    return (solution_field, residual)


def solution(mesh):
    in_specs = (
        P("slab", "quad", None),
        P("slab", "quad", None),
        P("slab", "quad", None),
        P("slab", "quad", None),
        P("slab", "quad", None),
        P("slab", "quad", None),
    )
    out_specs = (P("slab", "quad", None), P("slab", "quad", None))
    return jax.shard_map(body, mesh=mesh, in_specs=in_specs, out_specs=out_specs, check_vma=False)
```

profile of v0, /device:TPU:1, one launch (start us, length us, event | category | flops | bytes accessed | tf_op | source)
XLA Modules:
  0.0 1597.4 jit_solution(9286723559896746589)
XLA Ops:
  9.1 4.9 collective-permute-start
  17.5 15.6 while.106
  19.3 2.1 fusion.154
  23.1 2.1 fusion.154
  27.0 2.1 fusion.154
  30.9 2.1 fusion.154
  34.6 9.5 all-reduce.3
  48.6 247.1 %all-reduce.4 = f32[4096]{0:T(1024)S(1)} all-reduce(f32[4096]{0:T(1024)S(1)} %dynamic-update-slice.1), channel_id=2, replica_groups=mesh['slab'=64,'quad'=4] {'slab'}, use_global_device_ids=true, to_apply=%add.4 | all-reduce | flops 4096 | bytes 32768
  298.0 60.1 %while.107 = (s32[]{:T(128)}, f32[64]{0:T(128)S(1)}, s32[]{:T(128)}, f32[64,64,64]{2,1,0:T(8,128)}, f32[64,64]{1,0:T(8,128)S(1)}, /*index=5*/s32[]{:T(128)}, s32[]{:T(128)}) while((s32[]{:T(128)}, f32[64]{0:T(128)S(1)}, s32[]{:T(128)}, f32[64,64,64]{2,1,0:T(8,128)}, f32[64,64]{1,0:T(8,128)S(1)}, /*index=5*/s32[]{:T(128)}, ...), condition=%wide.region_3.4_spmd.clone, body=%wide.region_2.3_spmd.clone.sunk | while | flops 49412 | bytes 37727 | solution.py:41
  358.7 246.1 %all-reduce.5 = f32[4096]{0:T(1024)S(1)} all-reduce(f32[4096]{0:T(1024)S(1)} %dynamic-update-slice.2), channel_id=4, replica_groups=mesh['slab'=64,'quad'=4] {'slab'}, use_global_device_ids=true, to_apply=%add.5 | all-reduce | flops 4096 | bytes 32768
  604.9 60.1 %while.108 = (s32[]{:T(128)}, f32[64]{0:T(128)S(1)}, s32[]{:T(128)}, f32[64,64,64]{2,1,0:T(8,128)}, f32[64,64]{1,0:T(8,128)S(1)}, /*index=5*/s32[]{:T(128)}, s32[]{:T(128)}, s32[]{:T(128)}, s32[]{:T(128)}) while((s32[]{:T(128)}, f32[64]{0:T(128)S(1)}, s32[]{:T(128)}, f32[64,64,64]{2,1,0:T(8,128)}, f32[64,64]{1,0:T(8,128)S(1)}, ...), condition=%wide.region_5.6_spmd.clone, body=%wide.region_4.5_spmd.clone.sunk | while | flops 49416 | bytes 37789 | solution.py:41
  665.1 8.4 all-reduce.9
  673.7 5.9 while.104
  679.6 5.6 collective-permute-start.4
  685.3 5.2 collective-permute-start.5
  694.5 3.2 collective-permute-done.7
  699.1 72.8 %all-reduce.11 = (f32[]{:T(128)}, f32[]{:T(128)}) all-reduce(f32[]{:T(128)} %get-tuple-element.697, f32[]{:T(128)} %get-tuple-element.696), channel_id=1, replica_groups=mesh['slab'=64,'quad'=4] {'slab','quad'}, use_global_device_ids=true, to_apply=%region_10.11 | all-reduce | flops 2 | bytes 16 | tf_op jit(solution)/shard_map/psum | solution.py:149
  773.2 9.0 while.109
  773.3 2.1 fusion.162
  775.6 2.1 fusion.162
  782.4 8.0 all-reduce.6
  790.8 243.2 %all-reduce.7 = f32[4096]{0:T(1024)S(1)} all-reduce(f32[4096]{0:T(1024)S(1)} %dynamic-update-slice.4), channel_id=5, replica_groups=mesh['slab'=64,'quad'=4] {'slab'}, use_global_device_ids=true, to_apply=%add.7 | all-reduce | flops 4096 | bytes 32768
  1034.0 60.1 %while.110 = (s32[]{:T(128)}, f32[64]{0:T(128)S(1)}, s32[]{:T(128)}, f32[64,64,64]{2,1,0:T(8,128)}, f32[64,64]{1,0:T(8,128)S(1)}, /*index=5*/s32[]{:T(128)}, s32[]{:T(128)}) while((s32[]{:T(128)}, f32[64]{0:T(128)S(1)}, s32[]{:T(128)}, f32[64,64,64]{2,1,0:T(8,128)}, f32[64,64]{1,0:T(8,128)S(1)}, /*index=5*/s32[]{:T(128)}, ...), condition=%wide.region_16.17_spmd.clone, body=%wide.region_15.16_spmd.clone.sunk | while | flops 49412 | bytes 37727 | solution.py:41
  1094.7 246.3 %all-reduce.8 = f32[4096]{0:T(1024)S(1)} all-reduce(f32[4096]{0:T(1024)S(1)} %dynamic-update-slice.5), channel_id=6, replica_groups=mesh['slab'=64,'quad'=4] {'slab'}, use_global_device_ids=true, to_apply=%add.8 | all-reduce | flops 4096 | bytes 32768
  1341.1 60.1 %while.111 = (s32[]{:T(128)}, f32[64]{0:T(128)S(1)}, s32[]{:T(128)}, f32[64,64,64]{2,1,0:T(8,128)}, f32[64,64]{1,0:T(8,128)S(1)}, /*index=5*/s32[]{:T(128)}, s32[]{:T(128)}, s32[]{:T(128)}, s32[]{:T(128)}) while((s32[]{:T(128)}, f32[64]{0:T(128)S(1)}, s32[]{:T(128)}, f32[64,64,64]{2,1,0:T(8,128)}, f32[64,64]{1,0:T(8,128)S(1)}, ...), condition=%wide.region_18.19_spmd.clone, body=%wide.region_17.18_spmd.clone.sunk | while | flops 49416 | bytes 37789 | solution.py:41
  1401.3 6.6 all-reduce.10
  1408.0 5.9 while.105
  1414.6 79.4 %psum.30 = f32[]{:T(128)} all-reduce(f32[]{:T(128)} %multiply_reduce_fusion.1), channel_id=1, replica_groups=mesh['slab'=64,'quad'=4] {'slab','quad'}, use_global_device_ids=true, to_apply=%region_23.24 | all-reduce | flops 1 | bytes 8 | tf_op jit(solution)/shard_map/psum | solution.py:149
  1495.4 4.2 collective-permute-start.8
  1501.6 3.6 collective-permute-done.9
  1508.5 3.3 collective-permute-done.11
  1513.0 75.3 %psum.31 = f32[]{:T(128)} all-reduce(f32[]{:T(128)} %get-tuple-element.772), channel_id=1, replica_groups=mesh['slab'=64,'quad'=4] {'slab','quad'}, use_global_device_ids=true, to_apply=%region_25.26 | all-reduce | flops 1 | bytes 8 | tf_op jit(solution)/shard_map/psum | solution.py:168
  (679 shorter events, 290.8 us)
Async XLA Ops:
  7.2 39.6 %copy-start = (f32[1,64,256]{2,1,0:T(8,128)S(1)}, f32[1,64,256]{2,1,0:T(8,128)}, u32[]{:S(2)}) copy-start(f32[1,64,256]{2,1,0:T(8,128)} %param.26) | copy-start | bytes 196612
  7.2 290.8 %all-gather.8.cloned.1.call-start = ((), (), s32[]{:S(2)}) async-start(), calls=%async_computation | async-start | bytes 2129920 | tf_op jit(solution)/shard_map/all_gather | solution.py:28
  7.9 597.0 %all-gather.10.cloned.1.call-start = ((), (), s32[]{:S(2)}) async-start(), calls=%async_computation.1 | async-start | bytes 2129920 | tf_op jit(solution)/shard_map/all_gather | solution.py:28
  9.1 35.1 %collective-permute-start = (f32[1,16,1024]{2,1,0:T(8,128)S(1)}, f32[1,16,1024]{2,1,0:T(8,128)S(1)}, u32[]{:S(2)}, u32[]{:S(2)}) collective-permute-start(f32[1,16,1024]{2,1,0:T(8,128)S(1)} %get-tuple-element.803), channel_id=1, source_target_pairs={{0,4},{4,8},{8,12},{12,16},{16,20},{20,24},{24,28},{28,32},{32,36}... | collective-permute-start | bytes 196616 | tf_op jit(solution)/shard_map/ppermute | solution.py:20
  14.0 30.1 %collective-permute-start.1 = (f32[1,16,1024]{2,1,0:T(8,128)S(1)}, f32[1,16,1024]{2,1,0:T(8,128)S(1)}, u32[]{:S(2)}, u32[]{:S(2)}) collective-permute-start(f32[1,16,1024]{2,1,0:T(8,128)S(1)} %get-tuple-element.804), channel_id=1, source_target_pairs={{4,0},{8,4},{12,8},{16,12},{20,16},{24,20},{28,24},{32,28},{36,32}... | collective-permute-start | bytes 196616 | tf_op jit(solution)/shard_map/ppermute | solution.py:21
  17.4 15.6 copy-start.5
  17.4 29.5 %copy-start.6 = (u32[256]{0:T(256)S(1)}, u32[256]{0:T(256)}, u32[]{:S(2)}) copy-start(u32[256]{0:T(256)} %constant.199) | copy-start | bytes 3076
  33.0 264.8 %copy-start.2 = (f32[4,16,1024]{2,1,0:T(8,128)S(1)}, f32[4,16,1024]{2,1,0:T(8,128)}, u32[]{:S(2)}) copy-start(f32[4,16,1024]{2,1,0:T(8,128)} %get-tuple-element.1201) | copy-start | bytes 786436
  44.1 313.9 %copy-start.3 = (f32[1,64,64]{2,1,0:T(8,128)S(1)}, f32[1,64,64]{2,1,0:T(8,128)}, u32[]{:S(2)}) copy-start(f32[1,64,64]{2,1,0:T(8,128)} %param.27) | copy-start | bytes 49156
  44.1 314.1 %copy-start.4 = (f32[1,64,64]{1,2,0:T(8,128)S(1)}, f32[1,64,64]{1,2,0:T(8,128)}, u32[]{:S(2)}) copy-start(f32[1,64,64]{1,2,0:T(8,128)} %copy.9) | copy-start | bytes 49156
  44.2 252.2 %collective-permute-start.2 = (f32[6,1,1024]{2,1,0:T(1,128)S(1)}, f32[6,1,1024]{2,1,0:T(1,128)S(1)}, u32[]{:S(2)}, u32[]{:S(2)}) collective-permute-start(f32[6,1,1024]{2,1,0:T(1,128)S(1)} %get-tuple-element.795), channel_id=1, source_target_pairs={{0,1},{1,2},{2,3},{4,5},{5,6},{6,7},{8,9},{9,10},{10,11},{12,13},{... | collective-permute-start | bytes 73736 | tf_op jit(solution)/shard_map/ppermute | solution.py:20
  45.5 250.9 %collective-permute-start.3 = (f32[6,1,1024]{2,1,0:T(1,128)S(1)}, f32[6,1,1024]{2,1,0:T(1,128)S(1)}, u32[]{:S(2)}, u32[]{:S(2)}) collective-permute-start(f32[6,1,1024]{2,1,0:T(1,128)S(1)} %get-tuple-element.794), channel_id=1, source_target_pairs={{1,0},{2,1},{3,2},{5,4},{6,5},{7,6},{9,8},{10,9},{11,10},{13,12},{... | collective-permute-start | bytes 73736 | tf_op jit(solution)/shard_map/ppermute | solution.py:21
  296.4 377.2 %copy-start.1 = (s32[4,16,1024]{2,1,0:T(8,128)S(1)}, s32[4,16,1024]{2,1,0:T(8,128)}, u32[]{:S(2)}) copy-start(s32[4,16,1024]{2,1,0:T(8,128)} %get-tuple-element.1198) | copy-start | bytes 786436
  679.6 10.9 collective-permute-start.4
  685.3 6.1 collective-permute-start.5
  691.4 3.0 collective-permute-start.6
  693.1 4.6 collective-permute-start.7
  1495.4 6.2 collective-permute-start.8
  1499.6 5.6 collective-permute-start.9
  1505.2 3.2 collective-permute-start.10
  1507.2 4.6 collective-permute-start.11
Sparse Core Ops, SparseCore 0:
  10.8 81.4 all-gather.7
  95.6 74.9 all-gather.9
where the time goes:
time: 1620 us; the launch traced here: 1600 us
  blocking collectives  1240 us (77%)
  matrix products  268 us (17%)
  starting transfers between devices  32.7 us (2%)
  between operations  20.4 us (1%)
    unnamed x8, blocking collectives  1020 us
    dot_general x256, matrix products, compose(): jnp.dot(later[0], earlier[1], precision=HIGH) + later[1]  239 us
    psum x2, blocking collectives, precondition(): rz_total = lax.psum(jnp.sum(resid * precond), ('slab', 'quad'))  152 us
    psum x1, blocking collectives, body(): alpha = rz / lax.psum(jnp.sum(search_direction * image), ('slab', 'quad'))  75.3 us
  transfers between devices with their start and end apart: 14, of which 4 were waited for; matrix products, arithmetic and copies ran while one was open for 5% of the time, Pallas kernels for 0%

commit v1 on v0

v1 whole, which is shorter than its diff:
```python
import jax
import jax.numpy as jnp
from jax import lax
from jax.experimental import pallas as pl
from jax.experimental.pallas import tpu as pltpu
from jax.sharding import PartitionSpec as P

F32 = jnp.float32
HIGH = lax.Precision.HIGHEST
BOTH = ("slab", "quad")


def sds(*shape):
    return jax.ShapeDtypeStruct(shape, F32)


def call(kernel, outs, scratch=()):
    return pl.pallas_call(kernel, out_shape=outs, scratch_shapes=list(scratch), name=kernel.__name__)


def harmonic(here, there):
    return jnp.where(there > 0, 2.0 * here * there / (here + there), here)


def x_before(plane):
    lane = lax.broadcasted_iota(jnp.int32, plane.shape, 1)
    return jnp.where(lane == 0, 0.0, pltpu.roll(plane, 1, 1))


def x_after(plane):
    width = plane.shape[1]
    lane = lax.broadcasted_iota(jnp.int32, plane.shape, 1)
    return jnp.where(lane == width - 1, 0.0, pltpu.roll(plane, width - 1, 1))


def y_before(plane, halo):
    row = lax.broadcasted_iota(jnp.int32, plane.shape, 0)
    return jnp.where(row == 0, halo, pltpu.roll(plane, 1, 0))


def y_after(plane, halo):
    height = plane.shape[0]
    row = lax.broadcasted_iota(jnp.int32, plane.shape, 0)
    return jnp.where(row == height - 1, halo, pltpu.roll(plane, height - 1, 0))


def lane_of(shape):
    return lax.broadcasted_iota(jnp.int32, shape, len(shape) - 1)


def restrict(sub_ref, field_ref, rows_ref):
    def group(g, unused):
        def tile(t, totals):
            rows = pl.ds(pl.multiple_of((t % 2) * 8, 8), 8)
            sub = sub_ref[t // 2, rows, :]
            field = field_ref[t // 2, rows, :]
            out = []
            for label in range(8):
                picked = jnp.where(sub == g * 8 + label, field, 0.0)
                total = totals[label]
                for j in range(8):
                    total = total + picked[:, j * 128 : (j + 1) * 128]
                out.append(total)
            return tuple(out)

        totals = lax.fori_loop(0, 8, tile, tuple(jnp.zeros((8, 128), F32) for _ in range(8)))
        stacked = jnp.concatenate([jnp.sum(t, axis=0, keepdims=True) for t in totals], axis=0)
        rows_ref[pl.ds(pl.multiple_of(g * 8, 8), 8), :] = stacked
        return unused

    lax.fori_loop(0, 8, group, 0)
    return jnp.sum(rows_ref[...].T, axis=0, keepdims=True)


def look_up(table, index):
    wide = jnp.broadcast_to(table, (8, 128))
    rows = []
    for r in range(index.shape[0] // 8):
        parts = []
        for c in range(index.shape[1] // 128):
            part = index[r * 8 : (r + 1) * 8, c * 128 : (c + 1) * 128]
            parts.append(jnp.take_along_axis(wide, part, axis=1, mode="promise_in_bounds"))
        rows.append(jnp.concatenate(parts, axis=1))
    return jnp.concatenate(rows, axis=0)


def solve_lines(kz, inv, gam, rhs):
    rho = [rhs[0] * inv[0]]
    for j in range(1, 4):
        rho.append((rhs[j] + kz[j] * rho[j - 1]) * inv[j])
    out = [None] * 4
    out[3] = rho[3]
    for j in (2, 1, 0):
        out[j] = rho[j] - gam[j] * out[j + 1]
    return out


def begin(rs, ph, gain, sub, fac, mob, zup, zdn, yup, ydn, pay, rows):
    for z in range(4):
        m = 1.0 / (gain[z] * (0.001 + 0.999 * ph[z].astype(F32)))
        s = (sub[z] + 1).astype(F32)
        mob[z] = m
        yup[z : z + 1, :] = m[15:16, :]
        yup[z + 4 : z + 5, :] = s[15:16, :]
        ydn[z : z + 1, :] = m[0:1, :]
        ydn[z + 4 : z + 5, :] = s[0:1, :]
        if z == 0:
            zdn[0] = m
            zdn[1] = s
        if z == 3:
            zup[0] = m
            zup[1] = s
    cin = restrict(sub, rs, rows)
    both = jnp.concatenate([cin, cin], axis=1)
    lane = lane_of((64, 128))
    row = lax.broadcasted_iota(jnp.int32, (64, 128), 0)
    tail = jnp.where(row == 0, both, 0.0)
    for q in range(4):
        block = fac[:, (q // 2) * 128 : (q // 2 + 1) * 128]
        if q % 2:
            block = pltpu.roll(block, 64, 1)
        pay[q] = jnp.where(lane < 64, block, tail)


def setup(rs, mob, zlo, zhi, ylo, yhi, fac, cou, got, kz, kyl, kyh, kxl, kxh, diag, inv, gam, bj, bzu, bzd, byu, byd, pay):
    odd = lax.axis_index("slab") % 2
    planes = [mob[z] for z in range(4)]
    below = [zlo[0]] + planes[:3]
    above = planes[1:] + [zhi[0]]
    faces = [harmonic(planes[z], below[z]) for z in range(4)]
    faces.append(harmonic(planes[3], above[3]))
    for z in range(5):
        kz[z] = faces[z]
    diags = []
    for z in range(4):
        m = planes[z]
        a = harmonic(m, y_before(m, ylo[z : z + 1, :]))
        b = harmonic(m, y_after(m, yhi[z : z + 1, :]))
        c = harmonic(m, x_before(m))
        d = harmonic(m, x_after(m))
        kyl[z] = a
        kyh[z] = b
        kxl[z] = c
        kxh[z] = d
        total = faces[z] + faces[z + 1] + a + b + c + d
        diag[z] = total
        diags.append(total)
    invs = [1.0 / diags[0]]
    gams = [-faces[1] * invs[0]]
    for j in range(1, 4):
        invs.append(1.0 / (diags[j] + faces[j] * gams[j - 1]))
        gams.append(-faces[j + 1] * invs[j])
    for j in range(4):
        inv[j] = invs[j]
    for j in range(3):
        gam[j] = gams[j]
    out = solve_lines(faces, invs, gams, [rs[z] for z in range(4)])
    for z in range(4):
        bj[z] = out[z]
        byu[z : z + 1, :] = out[z][15:16, :]
        byd[z : z + 1, :] = out[z][0:1, :]
    bzu[0] = out[3]
    bzd[0] = out[0]
    cins = [pltpu.roll(got[q][0:8, :], 64, 1)[0:1, :64] for q in range(4)]
    cin = jnp.concatenate(cins, axis=1)
    rhs = lax.dot_general(
        jnp.broadcast_to(cin, (8, 256)), fac[...], (((1,), (1,)), ((), ())), precision=HIGH, preferred_element_type=F32
    )
    flag = jnp.broadcast_to(odd, (64, 64)) == 1
    mat = jnp.where(flag, cou[...], cou[...].T)
    packed = jnp.concatenate([mat[:32, :], mat[32:, :]], axis=1)
    tail = jnp.concatenate([rhs, rhs], axis=1)
    for m in range(32):
        pay[m, 0:32, :] = packed
        pay[m, 32:40, :] = tail


def chain(own, other, rhs_ref, fac, facm, facp, out, mats, us, uc, ws, wc, core):
    odd = lax.axis_index("slab") % 2
    lane = lane_of((32, 128))
    low = lane < 64
    for m in range(32):
        for j, src in ((0, own), (1, other)):
            packed = src[m, 0:32, :]
            at = 2 * m + (odd if j == 0 else 1 - odd)
            mats[at, 0:32, :] = jnp.where(low, packed, 0.0)
            mats[at, 32:64, :] = jnp.where(low, pltpu.roll(packed, 64, 1), 0.0)
    cols = rhs_ref[...].T
    row = rhs_ref[0:1, :]
    us[0:1, :] = row
    col = None
    for k in range(1, 64):
        if k % 2:
            col = jnp.sum(mats[k] * row, axis=1, keepdims=True) + cols[:64, k : k + 1]
            uc[k] = jnp.broadcast_to(col, (64, 128))
        else:
            row = jnp.sum(mats[k] * col, axis=0, keepdims=True) + rhs_ref[k : k + 1, :]
            us[k : k + 1, :] = row
    ws[0:8, :] = jnp.zeros((8, 128), F32)
    wc[0] = jnp.zeros((64, 128), F32)
    wc[65] = jnp.zeros((64, 128), F32)
    wc[64] = jnp.broadcast_to(col, (64, 128))
    for k in range(63, 0, -1):
        if k % 2:
            row = jnp.sum(mats[k] * col, axis=0, keepdims=True) + us[k - 1 : k, :]
            ws[k : k + 1, :] = row
        else:
            col = jnp.sum(mats[k] * row, axis=1, keepdims=True) + uc[k - 1][:, 0:1]
            wc[k] = jnp.broadcast_to(col, (64, 128))
    slab = lax.axis_index("slab")
    for j, (shift, table) in enumerate(((0, fac), (-1, facm), (1, facp))):
        at = slab + shift + 1
        from_row = ws[pl.ds(jnp.minimum(at, 63), 1), :]
        from_col = wc[at].T[0:1, :]
        is_row = jnp.broadcast_to(at % 2, (1, 64)) == 1
        w = jnp.where(is_row, from_row[:, :64], from_col)
        part = jnp.dot(jnp.broadcast_to(w, (8, 64)), table[...], precision=HIGH, preferred_element_type=F32)
        for q in range(4):
            out[q, 2 * j : 2 * j + 1, :] = part[0:1, :128]
            out[q, 2 * j + 1 : 2 * j + 2, :] = part[0:1, 128:]
    for q in range(4):
        out[q, 6:8, :] = jnp.zeros((2, 128), F32)


def chain_first(own, other, fac, facm, facp, out, mats, us, uc, ws, wc, rhs):
    odd = lax.axis_index("slab") % 2
    lane = lane_of((1, 128))
    for m in range(32):
        for j, src in ((0, own), (1, other)):
            at = 2 * m + (odd if j == 0 else 1 - odd)
            rhs[pl.ds(at, 1), :] = jnp.where(lane < 64, src[m, 32:33, :], 0.0)
    chain(own, other, rhs, fac, facm, facp, out, mats, us, uc, ws, wc, None)


def chain_second(own, other, got, fac, facm, facp, out, dots, mats, us, uc, ws, wc, rhs):
    total = got[pl.ds(0, 64, 4), :]
    for q in range(1, 4):
        total = total + got[pl.ds(q, 64, 4), :]
    rhs[...] = jnp.where(lane_of((64, 128)) < 64, total, 0.0)
    dots[...] = jnp.broadcast_to(jnp.sum(total, axis=0, keepdims=True), (8, 128))
    chain(own, other, rhs, fac, facm, facp, out, mats, us, uc, ws, wc, None)


def tables(got):
    quad = lax.axis_index("quad")
    total = got[0] + got[1] + got[2] + got[3]
    near = pltpu.roll(total, 1, 1)
    far = pltpu.roll(total, 65, 1)
    lane = lane_of((1, 128))
    valid = (lane >= 1) & (lane <= 64)

    def table(base, q):
        first = jnp.where(jnp.broadcast_to(q % 2, (1, 128)) == 1, far[base : base + 1, :], near[base : base + 1, :])
        second = jnp.where(
            jnp.broadcast_to(q % 2, (1, 128)) == 1, far[base + 1 : base + 2, :], near[base + 1 : base + 2, :]
        )
        picked = jnp.where(jnp.broadcast_to(q, (1, 128)) >= 2, second, first)
        return jnp.where(valid, picked, 0.0)

    return (
        table(0, quad),
        table(0, jnp.maximum(quad - 1, 0)),
        table(0, jnp.minimum(quad + 1, 3)),
        table(2, quad),
        table(4, quad),
    )


def apply(got, bj, zlo, zhi, ylo, yhi, bzl, bzh, byl, byh, sub, kz, kyl, kyh, kxl, kxh, diag):
    own, t_yl, t_yh, t_zl, t_zh = tables(got)
    planes = [bj[z] + look_up(own, sub[z] + 1) for z in range(4)]
    below = bzl[0] + look_up(t_zl, zlo[1].astype(jnp.int32))
    above = bzh[0] + look_up(t_zh, zhi[1].astype(jnp.int32))
    before = byl[...] + look_up(t_yl, jnp.minimum(ylo[...], 64.0).astype(jnp.int32))[4:8, :]
    after = byh[...] + look_up(t_yh, jnp.minimum(yhi[...], 64.0).astype(jnp.int32))[4:8, :]
    lower = [below] + planes[:3]
    upper = planes[1:] + [above]
    images = []
    for z in range(4):
        v = planes[z]
        images.append(
            diag[z] * v
            - kz[z] * lower[z]
            - kz[z + 1] * upper[z]
            - kyl[z] * y_before(v, before[z : z + 1, :])
            - kyh[z] * y_after(v, after[z : z + 1, :])
            - kxl[z] * x_before(v)
            - kxh[z] * x_after(v)
        )
    return planes, images


def total_of(lefts, rights):
    acc = lefts[0] * rights[0]
    for a, b in zip(lefts[1:], rights[1:]):
        acc = acc + a * b
    return jnp.sum(jnp.sum(acc, axis=0, keepdims=True), axis=1, keepdims=True)


def first(
    got, bj, zlo, zhi, ylo, yhi, bzl, bzh, byl, byh, sub, kz, kyl, kyh, kxl, kxh, diag, rs, inv, gam, cols,
    z_out, q_out, bj_out, bzu, bzd, byu, byd, pay, rows,
):
    planes, images = apply(got, bj, zlo, zhi, ylo, yhi, bzl, bzh, byl, byh, sub, kz, kyl, kyh, kxl, kxh, diag)
    for z in range(4):
        z_out[z] = planes[z]
        q_out[z] = images[z]
    rz = total_of([rs[z] for z in range(4)], planes)
    pq = total_of(planes, images)
    out = solve_lines([kz[z] for z in range(4)], [inv[z] for z in range(4)], [gam[z] for z in range(3)], images)
    for z in range(4):
        bj_out[z] = out[z]
        byu[z : z + 1, :] = out[z][15:16, :]
        byd[z : z + 1, :] = out[z][0:1, :]
    bzu[0] = out[3]
    bzd[0] = out[0]
    cin = jnp.broadcast_to(restrict(sub, q_out, rows), (8, 64))
    lane = lane_of((1, 128))
    parts = []
    for q in range(4):
        part = lax.dot_general(
            cin, cols[q][:, :64], (((1,), (1,)), ((), ())), precision=HIGH, preferred_element_type=F32
        )[0:1, :]
        part = jnp.concatenate([part, part], axis=1)
        parts.append(jnp.where(lane < 64, part, jnp.where(lane == 64, rz, jnp.where(lane == 65, pq, 0.0))))
    tile = jnp.concatenate(parts + parts, axis=0)
    for j in range(32):
        pay[j * 8 : (j + 1) * 8, :] = tile


def second(
    got, bj, zlo, zhi, ylo, yhi, bzl, bzh, byl, byh, sub, kz, kyl, kyh, kxl, kxh, diag, rs, z0, q0, dots,
    z_out, g_out, r_out, pay,
):
    planes, images = apply(got, bj, zlo, zhi, ylo, yhi, bzl, bzh, byl, byh, sub, kz, kyl, kyh, kxl, kxh, diag)
    alpha = dots[0:1, 64:65] / dots[0:1, 65:66]
    zs, gs, rr = [], [], []
    for z in range(4):
        rr.append(rs[z] - alpha * q0[z])
        zs.append(z0[z] - alpha * planes[z])
        gs.append(q0[z] - alpha * images[z])
        z_out[z] = zs[z]
        g_out[z] = gs[z]
        r_out[z] = rr[z]
    new = total_of(rr, zs)
    own = total_of(zs, gs)
    cross = total_of([z0[z] for z in range(4)], gs)
    lane = lane_of((8, 128))
    tile = jnp.where(lane == 0, new, jnp.where(lane == 1, own, jnp.where(lane == 2, cross, 0.0)))
    for j in range(32):
        pay[j * 8 : (j + 1) * 8, :] = tile


def last(got, dots, z0, q0, z1, g1, r1, x_out, r_out):
    total = jnp.sum(got[...], axis=0, keepdims=True)
    new, own, cross = total[:, 0:1], total[:, 1:2], total[:, 2:3]
    rz, pq = dots[0:1, 64:65], dots[0:1, 65:66]
    alpha = rz / pq
    beta = new / rz
    step = new / (own + 2.0 * beta * cross + beta * beta * pq)
    for z in range(4):
        x_out[z] = alpha * z0[z] + step * (z1[z] + beta * z0[z])
        r_out[z] = r1[z] - step * (g1[z] + beta * q0[z])


def body(right_side, phase_label, density_gain, subdomain, block_factor, coupling):
    slabs, quads = lax.axis_size("slab"), lax.axis_size("quad")
    fac, cou = block_factor[0], coupling[0]
    grid = sds(4, 16, 1024)
    up = [(i, i + 1) for i in range(slabs - 1)]
    down = [(j, i) for i, j in up]
    forth = [(i, i + 1) for i in range(quads - 1)]
    back = [(j, i) for i, j in forth]
    cores = [[i for i in range(slabs) if i % 2 == c] for c in range(2)]

    def exchange(value, axis, groups=None):
        return lax.all_to_all(value, axis, 0, 0, tiled=True, axis_index_groups=groups)

    def halo(zu, zd, yu, yd):
        return (
            lax.ppermute(zu, "slab", up),
            lax.ppermute(zd, "slab", down),
            lax.ppermute(yu, "quad", forth),
            lax.ppermute(yd, "quad", back),
        )

    facm = lax.ppermute(fac, "slab", up)
    facp = lax.ppermute(fac, "slab", down)
    mob, *faces, pay = call(
        begin,
        (grid, sds(2, 16, 1024), sds(2, 16, 1024), sds(8, 1024), sds(8, 1024), sds(4, 64, 128)),
        [pltpu.VMEM((64, 128), F32)],
    )(right_side, phase_label, density_gain, subdomain, fac)
    sides = halo(*faces)
    got = exchange(pay, "quad")
    kz, kyl, kyh, kxl, kxh, diag, inv, gam, bj, *ends, pay = call(
        setup,
        (sds(5, 16, 1024), grid, grid, grid, grid, grid, grid, sds(3, 16, 1024), grid)
        + (sds(1, 16, 1024), sds(1, 16, 1024), sds(4, 1024), sds(4, 1024), sds(32, 40, 128)),
    )(right_side, mob, *sides, fac, cou, got)
    bjs = halo(*ends)
    own = exchange(pay, "slab", cores)
    other = lax.ppermute(own, "slab", [(i, i ^ 1) for i in range(slabs)])
    work = [
        pltpu.VMEM((64, 64, 128), F32),
        pltpu.VMEM((64, 128), F32),
        pltpu.VMEM((64, 64, 128), F32),
        pltpu.VMEM((64, 128), F32),
        pltpu.VMEM((66, 64, 128), F32),
        pltpu.VMEM((64, 128), F32),
    ]
    part = call(chain_first, sds(4, 8, 128), work)(own, other, fac, facm, facp)
    coarse = exchange(part, "quad")
    stencil = (kz, kyl, kyh, kxl, kxh, diag)
    z0, q0, bj1, *ends, pay = call(
        first,
        (grid, grid, grid, sds(1, 16, 1024), sds(1, 16, 1024), sds(4, 1024), sds(4, 1024), sds(256, 128)),
        [pltpu.VMEM((64, 128), F32)],
    )(coarse, bj, *sides, *bjs, subdomain, *stencil, right_side, inv, gam, got)
    bjs = halo(*ends)
    everyone = exchange(pay.reshape(256, 1, 128), BOTH).reshape(256, 128)
    part, dots = call(chain_second, (sds(4, 8, 128), sds(8, 128)), work)(own, other, everyone, fac, facm, facp)
    coarse = exchange(part, "quad")
    z1, g1, r1, pay = call(second, (grid, grid, grid, sds(256, 128)))(
        coarse, bj1, *sides, *bjs, subdomain, *stencil, right_side, z0, q0, dots
    )
    everyone = exchange(pay.reshape(256, 1, 128), BOTH).reshape(256, 128)
    return tuple(call(last, (grid, grid))(everyone, dots, z0, q0, z1, g1, r1))


def solution(mesh):
    spec = P("slab", "quad", None)
    return jax.shard_map(body, mesh=mesh, in_specs=(spec,) * 6, out_specs=(spec, spec), check_vma=False)
```

time: 1620 us -> 185 us (0.11); the launches traced: 1600 us -> 184 us
  blocking collectives: 1240 us -> 51.7 us
  matrix products: 268 us -> 0 us
  Pallas kernels: 0 us -> 47.2 us
  starting transfers between devices: 32.7 us -> 66.4 us
  between operations: 20.4 us -> 1.18 us
    unnamed x8 -> x0, blocking collectives: 1020 us -> none
    dot_general x280 -> x0, matrix products: 268 us -> none  [the longest x256 239 us: compose(): jnp.dot(later[0], earlier[1], precision=HIGH) + later[1]]
    psum x3 -> x0, blocking collectives: 227 us -> none  [the longest x2 152 us: precondition(): rz_total = lax.psum(jnp.sum(resid * precond), ('slab', 'quad'))]
    all_to_all x0 -> x2, blocking collectives: none -> 51.7 us  [exchange(): lax.all_to_all(value, axis, 0, 0, tiled=True, axis_index_groups=groups)]
    pallas_call x0 -> x7, Pallas kernels: none -> 47.2 us  [the longest x1 13.2 us: body(): call(chain_second, (sds(4, 8, 128), sds(8, 128)), work)]
    all_to_all x0 -> x4, starting transfers between devices: none -> 23.3 us  [exchange(): lax.all_to_all(value, axis, 0, 0, tiled=True, axis_index_groups=groups)]
    ppermute x12 -> x15, starting transfers between devices: 32.7 us -> 43.1 us  [the longest x3 11 us: halo(): lax.ppermute(zu, 'slab', up)]
  transfers between devices with their start and end apart: 14 -> 19, of which waited for: 4 -> 4; matrix products, arithmetic and copies ran while one was open for 5% -> 0% of each run, Pallas kernels for 0% -> 14%
where the time goes in v1:
time: 185 us; the launch traced here: 184 us
  starting transfers between devices  66.4 us (36%)
  blocking collectives  51.7 us (28%)
  Pallas kernels  47.2 us (26%)
  waiting for transfers between devices  14.3 us (8%)
  local copies, waits for them, and re-layouts  3.48 us (2%)
    all_to_all x2, blocking collectives, exchange(): lax.all_to_all(value, axis, 0, 0, tiled=True, axis_index_groups=groups)  51.7 us
    all_to_all x4, starting transfers between devices, exchange(): lax.all_to_all(value, axis, 0, 0, tiled=True, axis_index_groups=groups)  23.3 us
    pallas_call x1, Pallas kernels, body(): call(chain_second, (sds(4, 8, 128), sds(8, 128)), work)  13.2 us
    pallas_call x1, Pallas kernels, body(): part = call(chain_first, sds(4, 8, 128), work)(own, other, fac, facm, facp)  13.2 us
    ppermute x3, starting transfers between devices, halo(): lax.ppermute(zu, 'slab', up)  11 us
    all_to_all x4, waiting for transfers between devices, exchange(): lax.all_to_all(value, axis, 0, 0, tiled=True, axis_index_groups=groups)  10.9 us
    ppermute x3, starting transfers between devices, halo(): lax.ppermute(yu, 'quad', forth)  9.7 us
    ppermute x1, starting transfers between devices, body(): other = lax.ppermute(own, 'slab', [(i, i ^ 1) for i in range(slabs)])  7.1 us
  transfers between devices with their start and end apart: 19, of which 4 were waited for; matrix products, arithmetic and copies ran while one was open for 0% of the time, Pallas kernels for 14%

profile of v1, /device:TPU:1, one launch (start us, length us, event | category | flops | bytes accessed | tf_op | source)
XLA Modules:
  0.0 184.3 jit_solution(15647438749819880103)
XLA Ops:
  0.6 4.8 %begin.1 = (f32[4,16,1024]{2,1,0:T(8,128)}, f32[2,16,1024]{2,1,0:T(8,128)}, f32[2,16,1024]{2,1,0:T(8,128)}, f32[8,1024]{1,0:T(8,128)}, f32[8,1024]{1,0:T(8,128)}, /*index=5*/f32[4,64,128]{2,1,0:T(8,128)}) custom-call(f32[4,16,1024]{2,1,0:T(8,128)} %rs.7, s32[4,16,1024]{2,1,0:T(8,128)} %ph.1, f32[4,16,1024]{2,1,0:T(8,128)} %gain.1, s32[4,16,1024]{2,1,0:T(8,128)} %sub.5, ...), custom_call_target="tpu_custom_call" | custom-call | tf_op jit(solution)/shard_map/begin/pallas_call | solution.py:389
  5.4 4.9 %collective-permute-start = (f32[2,16,1024]{2,1,0:T(8,128)}, f32[2,16,1024]{2,1,0:T(8,128)S(1)}, u32[]{:S(2)}, u32[]{:S(2)}) collective-permute-start(f32[2,16,1024]{2,1,0:T(8,128)} %get-tuple-element.37), channel_id=1, source_target_pairs={{0,4},{4,8},{8,12},{12,16},{16,20},{20,24},{24,28},{28,32},{32,36}... | collective-permute-start | bytes 393224 | tf_op jit(solution)/shard_map/ppermute | solution.py:381
  10.4 1.9 %collective-permute-start.1 = (f32[2,16,1024]{2,1,0:T(8,128)}, f32[2,16,1024]{2,1,0:T(8,128)S(1)}, u32[]{:S(2)}, u32[]{:S(2)}) collective-permute-start(f32[2,16,1024]{2,1,0:T(8,128)} %get-tuple-element.38), channel_id=1, source_target_pairs={{4,0},{8,4},{12,8},{16,12},{20,16},{24,20},{28,24},{32,28},{36,32}... | collective-permute-start | bytes 393224 | tf_op jit(solution)/shard_map/ppermute | solution.py:382
  12.3 4.3 %all-to-all-start = ((f32[4,64,128]{2,1,0:T(8,128)}), f32[4,64,128]{2,1,0:T(8,128)S(1)}, u32[]{:S(2)}, u32[]{:S(2)}) async-start(f32[4,64,128]{2,1,0:T(8,128)} %get-tuple-element.41), calls=%async_computation | async-start | bytes 262144 | tf_op jit(solution)/shard_map/all_to_all | solution.py:377
  16.6 3.4 %collective-permute-start.2 = (f32[8,1024]{1,0:T(8,128)S(1)}, f32[8,1024]{1,0:T(8,128)S(1)}, u32[]{:S(2)}, u32[]{:S(2)}) collective-permute-start(f32[8,1024]{1,0:T(8,128)S(1)} %copy-done.26), channel_id=1, source_target_pairs={{0,1},{1,2},{2,3},{4,5},{5,6},{6,7},{8,9},{9,10},{10,11},{12,13},{... | collective-permute-start | bytes 98312 | tf_op jit(solution)/shard_map/ppermute | solution.py:383
  20.0 1.3 collective-permute-start.3
  21.3 3.3 %collective-permute-done.3.yhi = f32[8,1024]{1,0:T(8,128)S(1)} collective-permute-done((f32[8,1024]{1,0:T(8,128)S(1)}, f32[8,1024]{1,0:T(8,128)S(1)}, u32[]{:S(2)}, u32[]{:S(2)}) %collective-permute-start.3) | collective-permute-done | bytes 32800 | tf_op jit(solution)/shard_map/ppermute | solution.py:384
  25.5 3.4 %setup.1 = (f32[5,16,1024]{2,1,0:T(8,128)}, f32[4,16,1024]{2,1,0:T(8,128)}, f32[4,16,1024]{2,1,0:T(8,128)}, f32[4,16,1024]{2,1,0:T(8,128)}, f32[4,16,1024]{2,1,0...) custom-call(f32[4,16,1024]{2,1,0:T(8,128)} %rs.7, ...), custom_call_target="tpu_custom_call" | custom-call | tf_op jit(solution)/shard_map/setup/pallas_call | solution.py:396
  28.9 24.3 %all_to_all.30.own = f32[32,40,128]{2,1,0:T(8,128)S(1)} all-to-all(f32[32,40,128]{2,1,0:T(8,128)} %get-tuple-element.42), channel_id=1, replica_groups={{0,8,16,24,32,40,48,56,64,72,80,88,96,104,112,120,128,136,144,152,160,1..., dimensions={0} | all-to-all | bytes 1310720 | tf_op jit(solution)/shard_map/all_to_all | solution.py:377
  53.2 7.1 %collective-permute-start.4 = (f32[32,40,128]{2,1,0:T(8,128)S(1)}, f32[32,40,128]{2,1,0:T(8,128)S(1)}, u32[]{:S(2)}, u32[]{:S(2)}) collective-permute-start(f32[32,40,128]{2,1,0:T(8,128)S(1)} %all_to_all.30.own), channel_id=1, source_target_pairs={{0,4},{4,0},{8,12},{12,8},{16,20},{20,16},{24,28},{28,24},{32,36},... | collective-permute-start | bytes 1966088 | tf_op jit(solution)/shard_map/ppermute | solution.py:403
  60.3 1.9 %collective-permute-start.6 = (f32[64,256]{1,0:T(8,128)S(1)}, f32[64,256]{1,0:T(8,128)S(1)}, u32[]{:S(2)}, u32[]{:S(2)}) collective-permute-start(f32[64,256]{1,0:T(8,128)S(1)} %bitcast.14), channel_id=1, source_target_pairs={{4,0},{8,4},{12,8},{16,12},{20,16},{24,20},{28,24},{32,28},{36,32}... | collective-permute-start | bytes 196616 | tf_op jit(solution)/shard_map/ppermute | solution.py:388
  62.2 3.8 %collective-permute-start.5 = (f32[64,256]{1,0:T(8,128)S(1)}, f32[64,256]{1,0:T(8,128)S(1)}, u32[]{:S(2)}, u32[]{:S(2)}) collective-permute-start(f32[64,256]{1,0:T(8,128)S(1)} %bitcast.15), channel_id=1, source_target_pairs={{0,4},{4,8},{8,12},{12,16},{16,20},{20,24},{24,28},{28,32},{32,36}... | collective-permute-start | bytes 196616 | tf_op jit(solution)/shard_map/ppermute | solution.py:387
  66.0 2.4 %collective-permute-start.7 = (f32[1,16,1024]{2,1,0:T(8,128)S(1)}, f32[1,16,1024]{2,1,0:T(8,128)S(1)}, u32[]{:S(2)}, u32[]{:S(2)}) collective-permute-start(f32[1,16,1024]{2,1,0:T(8,128)S(1)} %copy-done.22), channel_id=1, source_target_pairs={{0,4},{4,8},{8,12},{12,16},{16,20},{20,24},{24,28},{28,32},{32,36}... | collective-permute-start | bytes 196616 | tf_op jit(solution)/shard_map/ppermute | solution.py:381
  68.4 1.9 %collective-permute-start.8 = (f32[1,16,1024]{2,1,0:T(8,128)S(1)}, f32[1,16,1024]{2,1,0:T(8,128)S(1)}, u32[]{:S(2)}, u32[]{:S(2)}) collective-permute-start(f32[1,16,1024]{2,1,0:T(8,128)S(1)} %copy-done.21), channel_id=1, source_target_pairs={{4,0},{8,4},{12,8},{16,12},{20,16},{24,20},{28,24},{32,28},{36,32}... | collective-permute-start | bytes 196616 | tf_op jit(solution)/shard_map/ppermute | solution.py:382
  70.4 3.2 %collective-permute-start.9 = (f32[4,1024]{1,0:T(4,128)S(1)}, f32[4,1024]{1,0:T(4,128)S(1)}, u32[]{:S(2)}, u32[]{:S(2)}) collective-permute-start(f32[4,1024]{1,0:T(4,128)S(1)} %copy-done.28), channel_id=1, source_target_pairs={{0,1},{1,2},{2,3},{4,5},{5,6},{6,7},{8,9},{9,10},{10,11},{12,13},{... | collective-permute-start | bytes 49160 | tf_op jit(solution)/shard_map/ppermute | solution.py:383
  73.6 1.3 collective-permute-start.10
  75.8 13.2 %chain_first.1 = f32[4,8,128]{2,1,0:T(8,128)} custom-call(f32[32,40,128]{2,1,0:T(8,128)} %copy-done, f32[32,40,128]{2,1,0:T(8,128)} %copy-done.1, f32[64,256]{1,0:T(8,128)} %bitcast.12, f32[64,256]{1,0:T(8,128)} %copy-done.10, f32[64,256]{1,0:T(8,128)} %copy-done.9), custom_call_target="tpu_custom_call" | custom-call | tf_op jit(solution)/shard_map/chain_first/pallas_call | solution.py:412
  89.0 4.3 %all-to-all-start.2 = ((f32[4,8,128]{2,1,0:T(8,128)}), f32[4,8,128]{2,1,0:T(8,128)S(1)}, u32[]{:S(2)}, u32[]{:S(2)}) async-start(f32[4,8,128]{2,1,0:T(8,128)} %chain_first.1), calls=%async_computation.2 | async-start | bytes 32768 | tf_op jit(solution)/shard_map/all_to_all | solution.py:377
  93.4 4.2 %all-to-all-done.2.got = f32[4,8,128]{2,1,0:T(8,128)S(1)} async-done(((f32[4,8,128]{2,1,0:T(8,128)}), f32[4,8,128]{2,1,0:T(8,128)S(1)}, u32[]{:S(2)}, u32[]{:S(2)}) %all-to-all-start.2) | async-done | bytes 16416 | tf_op jit(solution)/shard_map/all_to_all | solution.py:377
  98.2 6.5 %first.1 = (f32[4,16,1024]{2,1,0:T(8,128)}, f32[4,16,1024]{2,1,0:T(8,128)}, f32[4,16,1024]{2,1,0:T(8,128)}, f32[1,16,1024]{2,1,0:T(8,128)}, f32[1,16,1024]{2,1,0...) custom-call(f32[4,8,128]{2,1,0:T(8,128)} %copy-done.11, ...), custom_call_target="tpu_custom_call" | custom-call | tf_op jit(solution)/shard_map/first/pallas_call | solution.py:415
  104.7 11.4 %all-to-all-start.3 = ((f32[256,1,128]{2,1,0:T(1,128)}), f32[256,1,128]{2,1,0:T(1,128)S(1)}, u32[]{:S(2)}, u32[]{:S(2)}) async-start(f32[256,1,128]{2,1,0:T(1,128)} %bitcast.18), calls=%async_computation.3 | async-start | bytes 262144 | tf_op jit(solution)/shard_map/all_to_all | solution.py:377
  116.2 3.7 %collective-permute-start.11 = (f32[1,16,1024]{2,1,0:T(8,128)S(1)}, f32[1,16,1024]{2,1,0:T(8,128)S(1)}, u32[]{:S(2)}, u32[]{:S(2)}) collective-permute-start(f32[1,16,1024]{2,1,0:T(8,128)S(1)} %copy-done.24), channel_id=1, source_target_pairs={{0,4},{4,8},{8,12},{12,16},{16,20},{20,24},{24,28},{28,32},{32,36}... | collective-permute-start | bytes 196616 | tf_op jit(solution)/shard_map/ppermute | solution.py:381
  119.9 1.9 %collective-permute-start.12 = (f32[1,16,1024]{2,1,0:T(8,128)S(1)}, f32[1,16,1024]{2,1,0:T(8,128)S(1)}, u32[]{:S(2)}, u32[]{:S(2)}) collective-permute-start(f32[1,16,1024]{2,1,0:T(8,128)S(1)} %copy-done.23), channel_id=1, source_target_pairs={{4,0},{8,4},{12,8},{16,12},{20,16},{24,20},{28,24},{32,28},{36,32}... | collective-permute-start | bytes 196616 | tf_op jit(solution)/shard_map/ppermute | solution.py:382
  121.8 3.2 %collective-permute-start.13 = (f32[4,1024]{1,0:T(4,128)S(1)}, f32[4,1024]{1,0:T(4,128)S(1)}, u32[]{:S(2)}, u32[]{:S(2)}) collective-permute-start(f32[4,1024]{1,0:T(4,128)S(1)} %copy-done.30), channel_id=1, source_target_pairs={{0,1},{1,2},{2,3},{4,5},{5,6},{6,7},{8,9},{9,10},{10,11},{12,13},{... | collective-permute-start | bytes 49160 | tf_op jit(solution)/shard_map/ppermute | solution.py:383
  125.0 1.3 collective-permute-start.14
  126.3 2.7 %all-to-all-done.3 = f32[256,1,128]{2,1,0:T(1,128)S(1)} async-done(((f32[256,1,128]{2,1,0:T(1,128)}), f32[256,1,128]{2,1,0:T(1,128)S(1)}, u32[]{:S(2)}, u32[]{:S(2)}) %all-to-all-start.3) | async-done | bytes 131104 | tf_op jit(solution)/shard_map/all_to_all | solution.py:377
  129.6 13.2 %chain_second.1 = (f32[4,8,128]{2,1,0:T(8,128)}, f32[8,128]{1,0:T(8,128)}) custom-call(f32[32,40,128]{2,1,0:T(8,128)} %copy-done, f32[32,40,128]{2,1,0:T(8,128)} %copy-done.1, f32[256,128]{1,0:T(8,128)} %bitcast.16, f32[64,256]{1,0:T(8,128)} %bitcast.13, f32[64,256]{1,0:T(8,128)} %copy-done.10, f32[64,256]{1,0:T(8,128)} %copy-done.9), custom_call_target="tpu_custom_call" | custom-call | tf_op jit(solution)/shard_map/chain_second/pallas_call | solution.py:422
  142.9 3.2 %all-to-all-start.4 = ((f32[4,8,128]{2,1,0:T(8,128)}), f32[4,8,128]{2,1,0:T(8,128)S(1)}, u32[]{:S(2)}, u32[]{:S(2)}) async-start(f32[4,8,128]{2,1,0:T(8,128)} %get-tuple-element.57), calls=%async_computation.4 | async-start | bytes 32768 | tf_op jit(solution)/shard_map/all_to_all | solution.py:377
  146.2 4.1 %all-to-all-done.4.got = f32[4,8,128]{2,1,0:T(8,128)S(1)} async-done(((f32[4,8,128]{2,1,0:T(8,128)}), f32[4,8,128]{2,1,0:T(8,128)S(1)}, u32[]{:S(2)}, u32[]{:S(2)}) %all-to-all-start.4) | async-done | bytes 16416 | tf_op jit(solution)/shard_map/all_to_all | solution.py:377
  150.9 3.6 %second.1 = (f32[4,16,1024]{2,1,0:T(8,128)}, f32[4,16,1024]{2,1,0:T(8,128)}, f32[4,16,1024]{2,1,0:T(8,128)}, f32[256,128]{1,0:T(8,128)}) custom-call(f32[4,8,128]{2,1,0:T(8,128)} %copy-done.14, f32[4,16,1024]{2,1,0:T(8,128)} %get-tuple-element.58.bj, f32[2,16,1024]{2,1,0:T(8,128)} %copy-done.3, f32[2,16,1024]{2,1,0:T(8,128)} %copy-done.4, ...), custom_call_target="tpu_custom_call" | custom-call | tf_op jit(solution)/shard_map/second/pallas_call | solution.py:424
  154.5 27.4 %all_to_all.31 = f32[256,1,128]{2,1,0:T(1,128)} all-to-all(f32[256,1,128]{2,1,0:T(1,128)} %bitcast.19), channel_id=1, replica_groups=mesh['slab'=64,'quad'=4] {'slab','quad'}, dimensions={0} | all-to-all | bytes 262144 | tf_op jit(solution)/shard_map/all_to_all | solution.py:377
  181.9 2.4 %last.1 = (f32[4,16,1024]{2,1,0:T(8,128)}, f32[4,16,1024]{2,1,0:T(8,128)}) custom-call(f32[256,128]{1,0:T(8,128)} %bitcast.17, f32[8,128]{1,0:T(8,128)} %get-tuple-element.65.dots, f32[4,16,1024]{2,1,0:T(8,128)} %get-tuple-element.63.z0, f32[4,16,1024]{2,1,0:T(8,128)} %get-tuple-element.64.q0, f32[4,16,1024]{2,1,0:T(8,128)} %get-tuple-element.67.z1, ...), custom_call_target="tpu_custom_call" | custom-call | tf_op jit(solution)/shard_map/last/pallas_call | solution.py:428
  (77 shorter events, 3.5 us)
Async XLA Ops:
  5.4 19.3 %collective-permute-start = (f32[2,16,1024]{2,1,0:T(8,128)}, f32[2,16,1024]{2,1,0:T(8,128)S(1)}, u32[]{:S(2)}, u32[]{:S(2)}) collective-permute-start(f32[2,16,1024]{2,1,0:T(8,128)} %get-tuple-element.37), channel_id=1, source_target_pairs={{0,4},{4,8},{8,12},{12,16},{16,20},{20,24},{24,28},{28,32},{32,36}... | collective-permute-start | bytes 393224 | tf_op jit(solution)/shard_map/ppermute | solution.py:381
  10.4 14.3 %collective-permute-start.1 = (f32[2,16,1024]{2,1,0:T(8,128)}, f32[2,16,1024]{2,1,0:T(8,128)S(1)}, u32[]{:S(2)}, u32[]{:S(2)}) collective-permute-start(f32[2,16,1024]{2,1,0:T(8,128)} %get-tuple-element.38), channel_id=1, source_target_pairs={{4,0},{8,4},{12,8},{16,12},{20,16},{24,20},{28,24},{32,28},{36,32}... | collective-permute-start | bytes 393224 | tf_op jit(solution)/shard_map/ppermute | solution.py:382
  12.3 4.3 %copy-start.26 = (f32[8,1024]{1,0:T(8,128)S(1)}, f32[8,1024]{1,0:T(8,128)}, u32[]{:S(2)}) copy-start(f32[8,1024]{1,0:T(8,128)} %get-tuple-element.39) | copy-start | bytes 98308
  12.3 7.7 %copy-start.25 = (f32[8,1024]{1,0:T(8,128)S(1)}, f32[8,1024]{1,0:T(8,128)}, u32[]{:S(2)}) copy-start(f32[8,1024]{1,0:T(8,128)} %get-tuple-element.40) | copy-start | bytes 98308
  12.3 12.4 %all-to-all-start = ((f32[4,64,128]{2,1,0:T(8,128)}), f32[4,64,128]{2,1,0:T(8,128)S(1)}, u32[]{:S(2)}, u32[]{:S(2)}) async-start(f32[4,64,128]{2,1,0:T(8,128)} %get-tuple-element.41), calls=%async_computation | async-start | bytes 262144 | tf_op jit(solution)/shard_map/all_to_all | solution.py:377
  16.6 4.7 %collective-permute-start.2 = (f32[8,1024]{1,0:T(8,128)S(1)}, f32[8,1024]{1,0:T(8,128)S(1)}, u32[]{:S(2)}, u32[]{:S(2)}) collective-permute-start(f32[8,1024]{1,0:T(8,128)S(1)} %copy-done.26), channel_id=1, source_target_pairs={{0,1},{1,2},{2,3},{4,5},{5,6},{6,7},{8,9},{9,10},{10,11},{12,13},{... | collective-permute-start | bytes 98312 | tf_op jit(solution)/shard_map/ppermute | solution.py:383
  20.0 4.7 %collective-permute-start.3 = (f32[8,1024]{1,0:T(8,128)S(1)}, f32[8,1024]{1,0:T(8,128)S(1)}, u32[]{:S(2)}, u32[]{:S(2)}) collective-permute-start(f32[8,1024]{1,0:T(8,128)S(1)} %copy-done.25), channel_id=1, source_target_pairs={{1,0},{2,1},{3,2},{5,4},{6,5},{7,6},{9,8},{10,9},{11,10},{13,12},{... | collective-permute-start | bytes 98312 | tf_op jit(solution)/shard_map/ppermute | solution.py:384
  28.8 31.5 %copy-start.5 = (f32[1,64,256]{2,1,0:T(8,128)S(1)}, f32[1,64,256]{2,1,0:T(8,128)}, u32[]{:S(2)}) copy-start(f32[1,64,256]{2,1,0:T(8,128)} %param.10) | copy-start | bytes 196612
  28.8 37.2 %copy-start.22 = (f32[1,16,1024]{2,1,0:T(8,128)S(1)}, f32[1,16,1024]{2,1,0:T(8,128)}, u32[]{:S(2)}) copy-start(f32[1,16,1024]{2,1,0:T(8,128)} %get-tuple-element.44) | copy-start | bytes 196612
  28.9 39.6 %copy-start.21 = (f32[1,16,1024]{2,1,0:T(8,128)S(1)}, f32[1,16,1024]{2,1,0:T(8,128)}, u32[]{:S(2)}) copy-start(f32[1,16,1024]{2,1,0:T(8,128)} %get-tuple-element.45) | copy-start | bytes 196612
  28.9 41.5 %copy-start.28 = (f32[4,1024]{1,0:T(4,128)S(1)}, f32[4,1024]{1,0:T(4,128)}, u32[]{:S(2)}) copy-start(f32[4,1024]{1,0:T(4,128)} %get-tuple-element.46) | copy-start | bytes 49156
  28.9 44.7 %copy-start.27 = (f32[4,1024]{1,0:T(4,128)S(1)}, f32[4,1024]{1,0:T(4,128)}, u32[]{:S(2)}) copy-start(f32[4,1024]{1,0:T(4,128)} %get-tuple-element.47) | copy-start | bytes 49156
  53.2 21.7 %copy-start = (f32[32,40,128]{2,1,0:T(8,128)}, f32[32,40,128]{2,1,0:T(8,128)S(1)}, u32[]{:S(2)}) copy-start(f32[32,40,128]{2,1,0:T(8,128)S(1)} %all_to_all.30.own) | copy-start | bytes 1966084
  53.2 21.7 %collective-permute-start.4 = (f32[32,40,128]{2,1,0:T(8,128)S(1)}, f32[32,40,128]{2,1,0:T(8,128)S(1)}, u32[]{:S(2)}, u32[]{:S(2)}) collective-permute-start(f32[32,40,128]{2,1,0:T(8,128)S(1)} %all_to_all.30.own), channel_id=1, source_target_pairs={{0,4},{4,0},{8,12},{12,8},{16,20},{20,16},{24,28},{28,24},{32,36},... | collective-permute-start | bytes 1966088 | tf_op jit(solution)/shard_map/ppermute | solution.py:403
  60.3 10.1 %collective-permute-start.6 = (f32[64,256]{1,0:T(8,128)S(1)}, f32[64,256]{1,0:T(8,128)S(1)}, u32[]{:S(2)}, u32[]{:S(2)}) collective-permute-start(f32[64,256]{1,0:T(8,128)S(1)} %bitcast.14), channel_id=1, source_target_pairs={{4,0},{8,4},{12,8},{16,12},{20,16},{24,20},{28,24},{32,28},{36,32}... | collective-permute-start | bytes 196616 | tf_op jit(solution)/shard_map/ppermute | solution.py:388
  62.2 11.4 %collective-permute-start.5 = (f32[64,256]{1,0:T(8,128)S(1)}, f32[64,256]{1,0:T(8,128)S(1)}, u32[]{:S(2)}, u32[]{:S(2)}) collective-permute-start(f32[64,256]{1,0:T(8,128)S(1)} %bitcast.15), channel_id=1, source_target_pairs={{0,4},{4,8},{8,12},{12,16},{16,20},{20,24},{24,28},{28,32},{32,36}... | collective-permute-start | bytes 196616 | tf_op jit(solution)/shard_map/ppermute | solution.py:387
  66.0 27.4 %collective-permute-start.7 = (f32[1,16,1024]{2,1,0:T(8,128)S(1)}, f32[1,16,1024]{2,1,0:T(8,128)S(1)}, u32[]{:S(2)}, u32[]{:S(2)}) collective-permute-start(f32[1,16,1024]{2,1,0:T(8,128)S(1)} %copy-done.22), channel_id=1, source_target_pairs={{0,4},{4,8},{8,12},{12,16},{16,20},{20,24},{24,28},{28,32},{32,36}... | collective-permute-start | bytes 196616 | tf_op jit(solution)/shard_map/ppermute | solution.py:381
  68.4 25.0 %collective-permute-start.8 = (f32[1,16,1024]{2,1,0:T(8,128)S(1)}, f32[1,16,1024]{2,1,0:T(8,128)S(1)}, u32[]{:S(2)}, u32[]{:S(2)}) collective-permute-start(f32[1,16,1024]{2,1,0:T(8,128)S(1)} %copy-done.21), channel_id=1, source_target_pairs={{4,0},{8,4},{12,8},{16,12},{20,16},{24,20},{28,24},{32,28},{36,32}... | collective-permute-start | bytes 196616 | tf_op jit(solution)/shard_map/ppermute | solution.py:382
  70.4 4.6 %copy-start.9 = (f32[64,256]{1,0:T(8,128)}, f32[64,256]{1,0:T(8,128)S(1)}, u32[]{:S(2)}) copy-start(f32[64,256]{1,0:T(8,128)S(1)} %collective-permute-done.6.facp) | copy-start | bytes 196612
  70.4 23.0 %collective-permute-start.9 = (f32[4,1024]{1,0:T(4,128)S(1)}, f32[4,1024]{1,0:T(4,128)S(1)}, u32[]{:S(2)}, u32[]{:S(2)}) collective-permute-start(f32[4,1024]{1,0:T(4,128)S(1)} %copy-done.28), channel_id=1, source_target_pairs={{0,1},{1,2},{2,3},{4,5},{5,6},{6,7},{8,9},{9,10},{10,11},{12,13},{... | collective-permute-start | bytes 49160 | tf_op jit(solution)/shard_map/ppermute | solution.py:383
  73.6 19.7 %collective-permute-start.10 = (f32[4,1024]{1,0:T(4,128)S(1)}, f32[4,1024]{1,0:T(4,128)S(1)}, u32[]{:S(2)}, u32[]{:S(2)}) collective-permute-start(f32[4,1024]{1,0:T(4,128)S(1)} %copy-done.27), channel_id=1, source_target_pairs={{1,0},{2,1},{3,2},{5,4},{6,5},{7,6},{9,8},{10,9},{11,10},{13,12},{... | collective-permute-start | bytes 49160 | tf_op jit(solution)/shard_map/ppermute | solution.py:384
  89.0 8.5 %all-to-all-start.2 = ((f32[4,8,128]{2,1,0:T(8,128)}), f32[4,8,128]{2,1,0:T(8,128)S(1)}, u32[]{:S(2)}, u32[]{:S(2)}) async-start(f32[4,8,128]{2,1,0:T(8,128)} %chain_first.1), calls=%async_computation.2 | async-start | bytes 32768 | tf_op jit(solution)/shard_map/all_to_all | solution.py:377
  104.7 11.5 %copy-start.24 = (f32[1,16,1024]{2,1,0:T(8,128)S(1)}, f32[1,16,1024]{2,1,0:T(8,128)}, u32[]{:S(2)}) copy-start(f32[1,16,1024]{2,1,0:T(8,128)} %get-tuple-element.59) | copy-start | bytes 196612
  104.7 15.2 %copy-start.23 = (f32[1,16,1024]{2,1,0:T(8,128)S(1)}, f32[1,16,1024]{2,1,0:T(8,128)}, u32[]{:S(2)}) copy-start(f32[1,16,1024]{2,1,0:T(8,128)} %get-tuple-element.60) | copy-start | bytes 196612
  104.7 17.1 %copy-start.30 = (f32[4,1024]{1,0:T(4,128)S(1)}, f32[4,1024]{1,0:T(4,128)}, u32[]{:S(2)}) copy-start(f32[4,1024]{1,0:T(4,128)} %get-tuple-element.61) | copy-start | bytes 49156
  104.7 20.2 %copy-start.29 = (f32[4,1024]{1,0:T(4,128)S(1)}, f32[4,1024]{1,0:T(4,128)}, u32[]{:S(2)}) copy-start(f32[4,1024]{1,0:T(4,128)} %get-tuple-element.62) | copy-start | bytes 49156
  104.7 24.2 %all-to-all-start.3 = ((f32[256,1,128]{2,1,0:T(1,128)}), f32[256,1,128]{2,1,0:T(1,128)S(1)}, u32[]{:S(2)}, u32[]{:S(2)}) async-start(f32[256,1,128]{2,1,0:T(1,128)} %bitcast.18), calls=%async_computation.3 | async-start | bytes 262144 | tf_op jit(solution)/shard_map/all_to_all | solution.py:377
  116.2 30.0 %collective-permute-start.11 = (f32[1,16,1024]{2,1,0:T(8,128)S(1)}, f32[1,16,1024]{2,1,0:T(8,128)S(1)}, u32[]{:S(2)}, u32[]{:S(2)}) collective-permute-start(f32[1,16,1024]{2,1,0:T(8,128)S(1)} %copy-done.24), channel_id=1, source_target_pairs={{0,4},{4,8},{8,12},{12,16},{16,20},{20,24},{24,28},{28,32},{32,36}... | collective-permute-start | bytes 196616 | tf_op jit(solution)/shard_map/ppermute | solution.py:381
  119.9 26.3 %collective-permute-start.12 = (f32[1,16,1024]{2,1,0:T(8,128)S(1)}, f32[1,16,1024]{2,1,0:T(8,128)S(1)}, u32[]{:S(2)}, u32[]{:S(2)}) collective-permute-start(f32[1,16,1024]{2,1,0:T(8,128)S(1)} %copy-done.23), channel_id=1, source_target_pairs={{4,0},{8,4},{12,8},{16,12},{20,16},{24,20},{28,24},{32,28},{36,32}... | collective-permute-start | bytes 196616 | tf_op jit(solution)/shard_map/ppermute | solution.py:382
  121.8 24.3 %collective-permute-start.13 = (f32[4,1024]{1,0:T(4,128)S(1)}, f32[4,1024]{1,0:T(4,128)S(1)}, u32[]{:S(2)}, u32[]{:S(2)}) collective-permute-start(f32[4,1024]{1,0:T(4,128)S(1)} %copy-done.30), channel_id=1, source_target_pairs={{0,1},{1,2},{2,3},{4,5},{5,6},{6,7},{8,9},{9,10},{10,11},{12,13},{... | collective-permute-start | bytes 49160 | tf_op jit(solution)/shard_map/ppermute | solution.py:383
  125.0 21.2 %collective-permute-start.14 = (f32[4,1024]{1,0:T(4,128)S(1)}, f32[4,1024]{1,0:T(4,128)S(1)}, u32[]{:S(2)}, u32[]{:S(2)}) collective-permute-start(f32[4,1024]{1,0:T(4,128)S(1)} %copy-done.29), channel_id=1, source_target_pairs={{1,0},{2,1},{3,2},{5,4},{6,5},{7,6},{9,8},{10,9},{11,10},{13,12},{... | collective-permute-start | bytes 49160 | tf_op jit(solution)/shard_map/ppermute | solution.py:384
  142.9 7.4 %all-to-all-start.4 = ((f32[4,8,128]{2,1,0:T(8,128)}), f32[4,8,128]{2,1,0:T(8,128)S(1)}, u32[]{:S(2)}, u32[]{:S(2)}) async-start(f32[4,8,128]{2,1,0:T(8,128)} %get-tuple-element.57), calls=%async_computation.4 | async-start | bytes 32768 | tf_op jit(solution)/shard_map/all_to_all | solution.py:377
  (18 other events, 43.6 us)

commit v2 on v1

--- a/solution.py
+++ b/solution.py
@@ -95,21 +95,45 @@
     return out
 
 
-def begin(rs, ph, gain, sub, fac, mob, zup, zdn, yup, ydn, pay, rows):
+def parity():
+    return lax.axis_index("slab") % 2
+
+
+def choose(flag, a, b):
+    return jnp.where(jnp.broadcast_to(flag, a.shape) == 1, a, b)
+
+
+def spread(out, at, plane):
+    h = plane.shape[0]
+    for c in range(8):
+        out[at + c * h : at + (c + 1) * h, :] = plane[:, c * 128 : (c + 1) * 128]
+
+
+def gather_rows(block, at, h):
+    return jnp.concatenate([block[at + c * h : at + (c + 1) * h, :] for c in range(8)], axis=1)
+
+
+def face_for(dest, upward, downward):
+    return choose((lax.axis_index("quad") + 1 == dest).astype(jnp.int32), upward, downward)
+
+
+def begin(rs, ph, gain, sub, fac, mob, core, near, pay, rows):
+    odd = parity()
+    ms, ss = [], []
     for z in range(4):
         m = 1.0 / (gain[z] * (0.001 + 0.999 * ph[z].astype(F32)))
-        s = (sub[z] + 1).astype(F32)
         mob[z] = m
-        yup[z : z + 1, :] = m[15:16, :]
-        yup[z + 4 : z + 5, :] = s[15:16, :]
-        ydn[z : z + 1, :] = m[0:1, :]
-        ydn[z + 4 : z + 5, :] = s[0:1, :]
-        if z == 0:
-            zdn[0] = m
-            zdn[1] = s
-        if z == 3:
-            zup[0] = m
-            zup[1] = s
+        ms.append(m)
+        ss.append((sub[z] + 1).astype(F32))
+    spread(core, 0, choose(odd, ms[0], ms[3]))
+    spread(core, 128, choose(odd, ss[0], ss[3]))
+    spread(near, 0, choose(odd, ms[3], ms[0]))
+    spread(near, 128, choose(odd, ss[3], ss[0]))
+    for part in (core, near):
+        part[256:320, :] = fac[:, :128]
+        part[320:384, :] = fac[:, 128:]
+    upward = jnp.concatenate([m[15:16, :] for m in ms] + [s[15:16, :] for s in ss], axis=0)
+    downward = jnp.concatenate([m[0:1, :] for m in ms] + [s[0:1, :] for s in ss], axis=0)
     cin = restrict(sub, rs, rows)
     both = jnp.concatenate([cin, cin], axis=1)
     lane = lane_of((64, 128))
@@ -119,14 +143,36 @@
         block = fac[:, (q // 2) * 128 : (q // 2 + 1) * 128]
         if q % 2:
             block = pltpu.roll(block, 64, 1)
-        pay[q] = jnp.where(lane < 64, block, tail)
-
-
-def setup(rs, mob, zlo, zhi, ylo, yhi, fac, cou, got, kz, kyl, kyh, kxl, kxh, diag, inv, gam, bj, bzu, bzd, byu, byd, pay):
-    odd = lax.axis_index("slab") % 2
+        pay[q, 0:64, :] = jnp.where(lane < 64, block, tail)
+        spread(pay.at[q], 64, face_for(q, upward, downward))
+
+
+def send_faces(out, to_core, to_near, ups, downs):
+    odd = parity()
+    to_core[...] = choose(odd, out[0], out[3])
+    to_near[...] = choose(odd, out[3], out[0])
+    for z in range(4):
+        ups[z : z + 1, :] = out[z][15:16, :]
+        downs[z : z + 1, :] = out[z][0:1, :]
+
+
+def setup(
+    rs, mob, core, near, fac, cou, got, kz, kyl, kyh, kxl, kxh, diag, inv, gam, bj, to_core, to_near, ups, downs, zsub, ysub, pay
+):
+    odd = parity()
+    quad = lax.axis_index("quad")
     planes = [mob[z] for z in range(4)]
-    below = [zlo[0]] + planes[:3]
-    above = planes[1:] + [zhi[0]]
+    c_mob, n_mob = gather_rows(core, 0, 16), gather_rows(near, 0, 16)
+    c_sub, n_sub = gather_rows(core, 128, 16), gather_rows(near, 128, 16)
+    below = [choose(odd, c_mob, n_mob)] + planes[:3]
+    above = planes[1:] + [choose(odd, n_mob, c_mob)]
+    zsub[0] = choose(odd, c_sub, n_sub).astype(jnp.int32)
+    zsub[1] = choose(odd, n_sub, c_sub).astype(jnp.int32)
+    before = gather_rows(got[jnp.maximum(quad - 1, 0)], 64, 8)
+    after = gather_rows(got[jnp.minimum(quad + 1, 3)], 64, 8)
+    ylo = jnp.where(jnp.broadcast_to(quad, before.shape) > 0, before, 0.0)
+    yhi = jnp.where(jnp.broadcast_to(quad, after.shape) < 3, after, 0.0)
+    ysub[...] = jnp.concatenate([ylo[4:8, :], yhi[4:8, :]], axis=0).astype(jnp.int32)
     faces = [harmonic(planes[z], below[z]) for z in range(4)]
     faces.append(harmonic(planes[3], above[3]))
     for z in range(5):
@@ -157,10 +203,7 @@
     out = solve_lines(faces, invs, gams, [rs[z] for z in range(4)])
     for z in range(4):
         bj[z] = out[z]
-        byu[z : z + 1, :] = out[z][15:16, :]
-        byd[z : z + 1, :] = out[z][0:1, :]
-    bzu[0] = out[3]
-    bzd[0] = out[0]
+    send_faces(out, to_core, to_near, ups, downs)
     cins = [pltpu.roll(got[q][0:8, :], 64, 1)[0:1, :64] for q in range(4)]
     cin = jnp.concatenate(cins, axis=1)
     rhs = lax.dot_general(
@@ -175,7 +218,7 @@
         pay[m, 32:40, :] = tail
 
 
-def chain(own, other, rhs_ref, fac, facm, facp, out, mats, us, uc, ws, wc, core):
+def chain(own, other, rhs_ref, fac, core, near, ups, downs, out, mats, us, uc, ws, wc):
     odd = lax.axis_index("slab") % 2
     lane = lane_of((32, 128))
     low = lane < 64
@@ -208,42 +251,46 @@
             col = jnp.sum(mats[k] * row, axis=1, keepdims=True) + uc[k - 1][:, 0:1]
             wc[k] = jnp.broadcast_to(col, (64, 128))
     slab = lax.axis_index("slab")
-    for j, (shift, table) in enumerate(((0, fac), (-1, facm), (1, facp))):
+    c_fac = jnp.concatenate([core[256:320, :], core[320:384, :]], axis=1)
+    n_fac = jnp.concatenate([near[256:320, :], near[320:384, :]], axis=1)
+    shares = ((0, fac[...]), (-1, choose(odd, c_fac, n_fac)), (1, choose(odd, n_fac, c_fac)))
+    for j, (shift, table) in enumerate(shares):
         at = slab + shift + 1
         from_row = ws[pl.ds(jnp.minimum(at, 63), 1), :]
         from_col = wc[at].T[0:1, :]
         is_row = jnp.broadcast_to(at % 2, (1, 64)) == 1
         w = jnp.where(is_row, from_row[:, :64], from_col)
-        part = jnp.dot(jnp.broadcast_to(w, (8, 64)), table[...], precision=HIGH, preferred_element_type=F32)
+        part = jnp.dot(jnp.broadcast_to(w, (8, 64)), table, precision=HIGH, preferred_element_type=F32)
         for q in range(4):
             out[q, 2 * j : 2 * j + 1, :] = part[0:1, :128]
             out[q, 2 * j + 1 : 2 * j + 2, :] = part[0:1, 128:]
     for q in range(4):
         out[q, 6:8, :] = jnp.zeros((2, 128), F32)
-
-
-def chain_first(own, other, fac, facm, facp, out, mats, us, uc, ws, wc, rhs):
+        spread(out.at[q], 8, face_for(q, ups[...], downs[...]))
+
+
+def chain_first(own, other, fac, core, near, ups, downs, out, mats, us, uc, ws, wc, rhs):
     odd = lax.axis_index("slab") % 2
     lane = lane_of((1, 128))
     for m in range(32):
         for j, src in ((0, own), (1, other)):
             at = 2 * m + (odd if j == 0 else 1 - odd)
             rhs[pl.ds(at, 1), :] = jnp.where(lane < 64, src[m, 32:33, :], 0.0)
-    chain(own, other, rhs, fac, facm, facp, out, mats, us, uc, ws, wc, None)
-
-
-def chain_second(own, other, got, fac, facm, facp, out, dots, mats, us, uc, ws, wc, rhs):
+    chain(own, other, rhs, fac, core, near, ups, downs, out, mats, us, uc, ws, wc)
+
+
+def chain_second(own, other, got, fac, core, near, ups, downs, out, dots, mats, us, uc, ws, wc, rhs):
     total = got[pl.ds(0, 64, 4), :]
     for q in range(1, 4):
         total = total + got[pl.ds(q, 64, 4), :]
     rhs[...] = jnp.where(lane_of((64, 128)) < 64, total, 0.0)
     dots[...] = jnp.broadcast_to(jnp.sum(total, axis=0, keepdims=True), (8, 128))
-    chain(own, other, rhs, fac, facm, facp, out, mats, us, uc, ws, wc, None)
+    chain(own, other, rhs, fac, core, near, ups, downs, out, mats, us, uc, ws, wc)
 
 
 def tables(got):
     quad = lax.axis_index("quad")
-    total = got[0] + got[1] + got[2] + got[3]
+    total = got[0, 0:8, :] + got[1, 0:8, :] + got[2, 0:8, :] + got[3, 0:8, :]
     near = pltpu.roll(total, 1, 1)
     far = pltpu.roll(total, 65, 1)
     lane = lane_of((1, 128))
@@ -266,13 +313,17 @@
     )
 
 
-def apply(got, bj, zlo, zhi, ylo, yhi, bzl, bzh, byl, byh, sub, kz, kyl, kyh, kxl, kxh, diag):
+def apply(got, bj, core, near, sub, zsub, ysub, kz, kyl, kyh, kxl, kxh, diag):
+    odd = parity()
+    quad = lax.axis_index("quad")
     own, t_yl, t_yh, t_zl, t_zh = tables(got)
     planes = [bj[z] + look_up(own, sub[z] + 1) for z in range(4)]
-    below = bzl[0] + look_up(t_zl, zlo[1].astype(jnp.int32))
-    above = bzh[0] + look_up(t_zh, zhi[1].astype(jnp.int32))
-    before = byl[...] + look_up(t_yl, jnp.minimum(ylo[...], 64.0).astype(jnp.int32))[4:8, :]
-    after = byh[...] + look_up(t_yh, jnp.minimum(yhi[...], 64.0).astype(jnp.int32))[4:8, :]
+    below = choose(odd, core[...], near[...]) + look_up(t_zl, zsub[0])
+    above = choose(odd, near[...], core[...]) + look_up(t_zh, zsub[1])
+    before = gather_rows(got[jnp.maximum(quad - 1, 0)], 8, 4)
+    after = gather_rows(got[jnp.minimum(quad + 1, 3)], 8, 4)
+    before = jnp.where(jnp.broadcast_to(quad, before.shape) > 0, before, 0.0) + look_up(t_yl, ysub[...])[0:4, :]
+    after = jnp.where(jnp.broadcast_to(quad, after.shape) < 3, after, 0.0) + look_up(t_yh, ysub[...])[4:8, :]
     lower = [below] + planes[:3]
     upper = planes[1:] + [above]
     images = []
@@ -298,10 +349,10 @@
 
 
 def first(
-    got, bj, zlo, zhi, ylo, yhi, bzl, bzh, byl, byh, sub, kz, kyl, kyh, kxl, kxh, diag, rs, inv, gam, cols,
-    z_out, q_out, bj_out, bzu, bzd, byu, byd, pay, rows,
+    got, bj, core, near, sub, zsub, ysub, kz, kyl, kyh, kxl, kxh, diag, rs, inv, gam, cols,
+    z_out, q_out, bj_out, to_core, to_near, ups, downs, pay, rows,
 ):
-    planes, images = apply(got, bj, zlo, zhi, ylo, yhi, bzl, bzh, byl, byh, sub, kz, kyl, kyh, kxl, kxh, diag)
+    planes, images = apply(got, bj, core, near, sub, zsub, ysub, kz, kyl, kyh, kxl, kxh, diag)
     for z in range(4):
         z_out[z] = planes[z]
         q_out[z] = images[z]
@@ -310,16 +361,13 @@
     out = solve_lines([kz[z] for z in range(4)], [inv[z] for z in range(4)], [gam[z] for z in range(3)], images)
     for z in range(4):
         bj_out[z] = out[z]
-        byu[z : z + 1, :] = out[z][15:16, :]
-        byd[z : z + 1, :] = out[z][0:1, :]
-    bzu[0] = out[3]
-    bzd[0] = out[0]
+    send_faces(out, to_core, to_near, ups, downs)
     cin = jnp.broadcast_to(restrict(sub, q_out, rows), (8, 64))
     lane = lane_of((1, 128))
     parts = []
     for q in range(4):
         part = lax.dot_general(
-            cin, cols[q][:, :64], (((1,), (1,)), ((), ())), precision=HIGH, preferred_element_type=F32
+            cin, cols[q, 0:64, :64], (((1,), (1,)), ((), ())), precision=HIGH, preferred_element_type=F32
         )[0:1, :]
         part = jnp.concatenate([part, part], axis=1)
         parts.append(jnp.where(lane < 64, part, jnp.where(lane == 64, rz, jnp.where(lane == 65, pq, 0.0))))
@@ -329,10 +377,10 @@
 
 
 def second(
-    got, bj, zlo, zhi, ylo, yhi, bzl, bzh, byl, byh, sub, kz, kyl, kyh, kxl, kxh, diag, rs, z0, q0, dots,
+    got, bj, core, near, sub, zsub, ysub, kz, kyl, kyh, kxl, kxh, diag, rs, z0, q0, dots,
     z_out, g_out, r_out, pay,
 ):
-    planes, images = apply(got, bj, zlo, zhi, ylo, yhi, bzl, bzh, byl, byh, sub, kz, kyl, kyh, kxl, kxh, diag)
+    planes, images = apply(got, bj, core, near, sub, zsub, ysub, kz, kyl, kyh, kxl, kxh, diag)
     alpha = dots[0:1, 64:65] / dots[0:1, 65:66]
     zs, gs, rr = [], [], []
     for z in range(4):
@@ -364,43 +412,32 @@
 
 
 def body(right_side, phase_label, density_gain, subdomain, block_factor, coupling):
-    slabs, quads = lax.axis_size("slab"), lax.axis_size("quad")
+    slabs = lax.axis_size("slab")
     fac, cou = block_factor[0], coupling[0]
-    grid = sds(4, 16, 1024)
-    up = [(i, i + 1) for i in range(slabs - 1)]
-    down = [(j, i) for i, j in up]
-    forth = [(i, i + 1) for i in range(quads - 1)]
-    back = [(j, i) for i, j in forth]
+    grid, plane, edge = sds(4, 16, 1024), sds(16, 1024), sds(4, 1024)
     cores = [[i for i in range(slabs) if i % 2 == c] for c in range(2)]
+    with_core = [(i, i ^ 1) for i in range(slabs)]
+    with_near = [(i, i + 1 if i % 2 else i - 1) for i in range(1, slabs - 1)]
 
     def exchange(value, axis, groups=None):
         return lax.all_to_all(value, axis, 0, 0, tiled=True, axis_index_groups=groups)
 
-    def halo(zu, zd, yu, yd):
-        return (
-            lax.ppermute(zu, "slab", up),
-            lax.ppermute(zd, "slab", down),
-            lax.ppermute(yu, "quad", forth),
-            lax.ppermute(yd, "quad", back),
-        )
-
-    facm = lax.ppermute(fac, "slab", up)
-    facp = lax.ppermute(fac, "slab", down)
-    mob, *faces, pay = call(
-        begin,
-        (grid, sds(2, 16, 1024), sds(2, 16, 1024), sds(8, 1024), sds(8, 1024), sds(4, 64, 128)),
-        [pltpu.VMEM((64, 128), F32)],
+    def swap(to_core, to_near):
+        return lax.ppermute(to_core, "slab", with_core), lax.ppermute(to_near, "slab", with_near)
+
+    mob, core, near, pay = call(
+        begin, (grid, sds(384, 128), sds(384, 128), sds(4, 128, 128)), [pltpu.VMEM((64, 128), F32)]
     )(right_side, phase_label, density_gain, subdomain, fac)
-    sides = halo(*faces)
+    core, near = swap(core, near)
     got = exchange(pay, "quad")
-    kz, kyl, kyh, kxl, kxh, diag, inv, gam, bj, *ends, pay = call(
+    kz, kyl, kyh, kxl, kxh, diag, inv, gam, bj, to_core, to_near, ups, downs, zsub, ysub, pay = call(
         setup,
-        (sds(5, 16, 1024), grid, grid, grid, grid, grid, grid, sds(3, 16, 1024), grid)
-        + (sds(1, 16, 1024), sds(1, 16, 1024), sds(4, 1024), sds(4, 1024), sds(32, 40, 128)),
-    )(right_side, mob, *sides, fac, cou, got)
-    bjs = halo(*ends)
+        (sds(5, 16, 1024), grid, grid, grid, grid, grid, grid, sds(3, 16, 1024), grid, plane, plane, edge, edge)
+        + (jax.ShapeDtypeStruct((2, 16, 1024), jnp.int32), jax.ShapeDtypeStruct((8, 1024), jnp.int32), sds(32, 40, 128)),
+    )(right_side, mob, core, near, fac, cou, got)
+    bj_core, bj_near = swap(to_core, to_near)
     own = exchange(pay, "slab", cores)
-    other = lax.ppermute(own, "slab", [(i, i ^ 1) for i in range(slabs)])
+    other = lax.ppermute(own, "slab", with_core)
     work = [
         pltpu.VMEM((64, 64, 128), F32),
         pltpu.VMEM((64, 128), F32),
@@ -409,20 +446,20 @@
         pltpu.VMEM((66, 64, 128), F32),
         pltpu.VMEM((64, 128), F32),
     ]
-    part = call(chain_first, sds(4, 8, 128), work)(own, other, fac, facm, facp)
+    part = call(chain_first, sds(4, 40, 128), work)(own, other, fac, core, near, ups, downs)
     coarse = exchange(part, "quad")
-    stencil = (kz, kyl, kyh, kxl, kxh, diag)
-    z0, q0, bj1, *ends, pay = call(
-        first,
-        (grid, grid, grid, sds(1, 16, 1024), sds(1, 16, 1024), sds(4, 1024), sds(4, 1024), sds(256, 128)),
-        [pltpu.VMEM((64, 128), F32)],
-    )(coarse, bj, *sides, *bjs, subdomain, *stencil, right_side, inv, gam, got)
-    bjs = halo(*ends)
+    stencil = (subdomain, zsub, ysub, kz, kyl, kyh, kxl, kxh, diag, right_side)
+    z0, q0, bj1, to_core, to_near, ups, downs, pay = call(
+        first, (grid, grid, grid, plane, plane, edge, edge, sds(256, 128)), [pltpu.VMEM((64, 128), F32)]
+    )(coarse, bj, bj_core, bj_near, *stencil, inv, gam, got)
+    bj_core, bj_near = swap(to_core, to_near)
     everyone = exchange(pay.reshape(256, 1, 128), BOTH).reshape(256, 128)
-    part, dots = call(chain_second, (sds(4, 8, 128), sds(8, 128)), work)(own, other, everyone, fac, facm, facp)
+    part, dots = call(chain_second, (sds(4, 40, 128), sds(8, 128)), work)(
+        own, other, everyone, fac, core, near, ups, downs
+    )
     coarse = exchange(part, "quad")
     z1, g1, r1, pay = call(second, (grid, grid, grid, sds(256, 128)))(
-        coarse, bj1, *sides, *bjs, subdomain, *stencil, right_side, z0, q0, dots
+        coarse, bj1, bj_core, bj_near, *stencil, z0, q0, dots
     )
     everyone = exchange(pay.reshape(256, 1, 128), BOTH).reshape(256, 128)
     return tuple(call(last, (grid, grid))(everyone, dots, z0, q0, z1, g1, r1))

time: 185 us -> 162 us (0.88)
  starting transfers between devices: 66.4 us -> 37.9 us
  waiting for transfers between devices: 14.3 us -> 22 us
  blocking collectives: 51.7 us -> 49.5 us
    ppermute x15 -> x7, starting transfers between devices: 43.1 us -> 16.7 us  [the longest x3 8.42 us: swap(): lax.ppermute(to_near, 'slab', with_near)]
    all_to_all x4, waiting for transfers between devices: 10.9 us -> 18.8 us  [exchange(): lax.all_to_all(value, axis, 0, 0, tiled=True, axis_index_groups=groups)]
    all_to_all x2, blocking collectives: 51.7 us -> 49.5 us  [exchange(): lax.all_to_all(value, axis, 0, 0, tiled=True, axis_index_groups=groups)]
    all_to_all x4, starting transfers between devices: 23.3 us -> 21.2 us  [exchange(): lax.all_to_all(value, axis, 0, 0, tiled=True, axis_index_groups=groups)]
  transfers between devices with their start and end apart: 19 -> 11, of which waited for: 4 -> 5; matrix products, arithmetic and copies ran while one was open for 0% -> 0% of each run, Pallas kernels for 14% -> 17%
where the time goes in v2:
time: 162 us; the launch traced here: 161 us
  blocking collectives  49.5 us (31%)
  Pallas kernels  47.6 us (29%)
  starting transfers between devices  37.9 us (23%)
  waiting for transfers between devices  22 us (14%)
  local copies, waits for them, and re-layouts  3.48 us (2%)
    all_to_all x2, blocking collectives, exchange(): lax.all_to_all(value, axis, 0, 0, tiled=True, axis_index_groups=groups)  49.5 us
    all_to_all x4, starting transfers between devices, exchange(): lax.all_to_all(value, axis, 0, 0, tiled=True, axis_index_groups=groups)  21.2 us
    all_to_all x4, waiting for transfers between devices, exchange(): lax.all_to_all(value, axis, 0, 0, tiled=True, axis_index_groups=groups)  18.8 us
    pallas_call x1, Pallas kernels, body(): call(chain_second, (sds(4, 40, 128), sds(8, 128)), work)  13.4 us
    pallas_call x1, Pallas kernels, body(): call(chain_first, sds(4, 40, 128), work)  13.4 us
    ppermute x3, starting transfers between devices, swap(): lax.ppermute(to_near, 'slab', with_near)  8.42 us
    pallas_call x1, Pallas kernels, body(): call(first, (grid, grid, grid, plane, plane, edge, edge, sds(256, 128)),...  6.52 us
    pallas_call x1, Pallas kernels, body(): call(begin, (grid, sds(384, 128), sds(384, 128), sds(4, 128, 128)), [pltp...  4.87 us
  transfers between devices with their start and end apart: 11, of which 5 were waited for; matrix products, arithmetic and copies ran while one was open for 0% of the time, Pallas kernels for 17%

profile of v2, /device:TPU:1, one launch (start us, length us, event | category | flops | bytes accessed | tf_op | source)
XLA Modules:
  0.0 161.2 jit_solution(5313098595454284731)
XLA Ops:
  0.6 4.9 %begin.1 = (f32[4,16,1024]{2,1,0:T(8,128)}, f32[384,128]{1,0:T(8,128)}, f32[384,128]{1,0:T(8,128)}, f32[4,128,128]{2,1,0:T(8,128)}) custom-call(f32[4,16,1024]{2,1,0:T(8,128)} %rs.7, s32[4,16,1024]{2,1,0:T(8,128)} %ph.1, f32[4,16,1024]{2,1,0:T(8,128)} %gain.1, s32[4,16,1024]{2,1,0:T(8,128)} %sub.5, f32[64,256]{1,0:T(8,128)} %bitcast.10), custom_call_target="tpu_custom_call" | custom-call | tf_op jit(solution)/shard_map/begin/pallas_call | solution.py:428
  5.5 5.1 %all-to-all-start = ((f32[4,128,128]{2,1,0:T(8,128)}), f32[4,128,128]{2,1,0:T(8,128)S(1)}, u32[]{:S(2)}, u32[]{:S(2)}) async-start(f32[4,128,128]{2,1,0:T(8,128)} %get-tuple-element.39), calls=%async_computation | async-start | bytes 524288 | tf_op jit(solution)/shard_map/all_to_all | solution.py:423
  10.7 1.7 %collective-permute-start = (f32[384,128]{1,0:T(8,128)S(1)}, f32[384,128]{1,0:T(8,128)S(1)}, u32[]{:S(2)}, u32[]{:S(2)}) collective-permute-start(f32[384,128]{1,0:T(8,128)S(1)} %copy-done.13), channel_id=1, source_target_pairs={{0,4},{4,0},{8,12},{12,8},{16,20},{20,16},{24,28},{28,24},{32,36},... | collective-permute-start | bytes 589832 | tf_op jit(solution)/shard_map/ppermute | solution.py:426
  12.4 2.7 %collective-permute-start.1 = (f32[384,128]{1,0:T(8,128)S(1)}, f32[384,128]{1,0:T(8,128)S(1)}, u32[]{:S(2)}, u32[]{:S(2)}) collective-permute-start(f32[384,128]{1,0:T(8,128)S(1)} %copy-done.12), channel_id=1, source_target_pairs={{4,8},{8,4},{12,16},{16,12},{20,24},{24,20},{28,32},{32,28},{36,40... | collective-permute-start | bytes 589832 | tf_op jit(solution)/shard_map/ppermute | solution.py:426
  15.1 1.1 all-to-all-done.got.cols
  16.2 0.0 collective-permute-done.core
  16.2 3.2 %collective-permute-done.1.near = f32[384,128]{1,0:T(8,128)S(1)} collective-permute-done((f32[384,128]{1,0:T(8,128)S(1)}, f32[384,128]{1,0:T(8,128)S(1)}, u32[]{:S(2)}, u32[]{:S(2)}) %collective-permute-start.1) | collective-permute-done | bytes 196640 | tf_op jit(solution)/shard_map/ppermute | solution.py:426
  19.4 0.7 copy-done.4
  20.0 3.5 %setup.1 = (f32[5,16,1024]{2,1,0:T(8,128)}, f32[4,16,1024]{2,1,0:T(8,128)}, f32[4,16,1024]{2,1,0:T(8,128)}, f32[4,16,1024]{2,1,0:T(8,128)}, f32[4,16,1024]{2,1,0...) custom-call(f32[4,16,1024]{2,1,0:T(8,128)} %rs.7, ...), custom_call_target="tpu_custom_call" | custom-call | tf_op jit(solution)/shard_map/setup/pallas_call | solution.py:433
  23.5 28.1 %all_to_all.30.own = f32[32,40,128]{2,1,0:T(8,128)S(1)} all-to-all(f32[32,40,128]{2,1,0:T(8,128)} %get-tuple-element.40), channel_id=1, replica_groups={{0,8,16,24,32,40,48,56,64,72,80,88,96,104,112,120,128,136,144,152,160,1..., dimensions={0} | all-to-all | bytes 1310720 | tf_op jit(solution)/shard_map/all_to_all | solution.py:423
  51.6 4.2 %collective-permute-start.2 = (f32[32,40,128]{2,1,0:T(8,128)S(1)}, f32[32,40,128]{2,1,0:T(8,128)S(1)}, u32[]{:S(2)}, u32[]{:S(2)}) collective-permute-start(f32[32,40,128]{2,1,0:T(8,128)S(1)} %all_to_all.30.own), channel_id=1, source_target_pairs={{0,4},{4,0},{8,12},{12,8},{16,20},{20,16},{24,28},{28,24},{32,36},... | collective-permute-start | bytes 1966088 | tf_op jit(solution)/shard_map/ppermute | solution.py:440
  55.8 0.1 collective-permute-start.3
  55.9 3.9 %collective-permute-start.4 = (f32[16,1024]{1,0:T(8,128)S(1)}, f32[16,1024]{1,0:T(8,128)S(1)}, u32[]{:S(2)}, u32[]{:S(2)}) collective-permute-start(f32[16,1024]{1,0:T(8,128)S(1)} %copy-done.16), channel_id=1, source_target_pairs={{4,8},{8,4},{12,16},{16,12},{20,24},{24,20},{28,32},{32,28},{36,40... | collective-permute-start | bytes 196616 | tf_op jit(solution)/shard_map/ppermute | solution.py:426
  59.8 0.8 copy-done.1
  60.6 13.4 %chain_first.1 = f32[4,40,128]{2,1,0:T(8,128)} custom-call(f32[32,40,128]{2,1,0:T(8,128)} %copy-done, f32[32,40,128]{2,1,0:T(8,128)} %copy-done.1, f32[64,256]{1,0:T(8,128)} %bitcast.12, f32[384,128]{1,0:T(8,128)} %copy-done.3, f32[384,128]{1,0:T(8,128)} %copy-done.4, f32[4,1024]{1,0:T(4,128)} %get-tuple-element.41.ups, f32[4,1024]{1,0:T(4,128)} %get-tuple-element.42.downs), custom_call_target="tpu_custom_call" | custom-call | tf_op jit(solution)/shard_map/chain_first/pallas_call | solution.py:449
  74.0 4.5 %all-to-all-start.2 = ((f32[4,40,128]{2,1,0:T(8,128)}), f32[4,40,128]{2,1,0:T(8,128)S(1)}, u32[]{:S(2)}, u32[]{:S(2)}) async-start(f32[4,40,128]{2,1,0:T(8,128)} %chain_first.1), calls=%async_computation.2 | async-start | bytes 163840 | tf_op jit(solution)/shard_map/all_to_all | solution.py:423
  78.5 0.0 collective-permute-done.3.core
  78.5 4.5 %all-to-all-done.2.got = f32[4,40,128]{2,1,0:T(8,128)S(1)} async-done(((f32[4,40,128]{2,1,0:T(8,128)}), f32[4,40,128]{2,1,0:T(8,128)S(1)}, u32[]{:S(2)}, u32[]{:S(2)}) %all-to-all-start.2) | async-done | bytes 81952 | tf_op jit(solution)/shard_map/all_to_all | solution.py:423
  83.1 0.6 copy-done.6
  83.7 6.5 %first.1 = (f32[4,16,1024]{2,1,0:T(8,128)}, f32[4,16,1024]{2,1,0:T(8,128)}, f32[4,16,1024]{2,1,0:T(8,128)}, f32[16,1024]{1,0:T(8,128)}, f32[16,1024]{1,0:T(8,128...) custom-call(f32[4,40,128]{2,1,0:T(8,128)} %copy-done.6, f32[4,16,1024]{2,1,0:T(8,128)} %get-tuple-element.43.bj, ...), custom_call_target="tpu_custom_call" | custom-call | tf_op jit(solution)/shard_map/first/pallas_call | solution.py:452
  90.2 8.2 %all-to-all-start.3 = ((f32[256,1,128]{2,1,0:T(1,128)}), f32[256,1,128]{2,1,0:T(1,128)S(1)}, u32[]{:S(2)}, u32[]{:S(2)}) async-start(f32[256,1,128]{2,1,0:T(1,128)} %bitcast.16), calls=%async_computation.3 | async-start | bytes 262144 | tf_op jit(solution)/shard_map/all_to_all | solution.py:423
  98.5 2.2 %collective-permute-start.5 = (f32[16,1024]{1,0:T(8,128)S(1)}, f32[16,1024]{1,0:T(8,128)S(1)}, u32[]{:S(2)}, u32[]{:S(2)}) collective-permute-start(f32[16,1024]{1,0:T(8,128)S(1)} %copy-done.15), channel_id=1, source_target_pairs={{0,4},{4,0},{8,12},{12,8},{16,20},{20,16},{24,28},{28,24},{32,36},... | collective-permute-start | bytes 196616 | tf_op jit(solution)/shard_map/ppermute | solution.py:426
  100.7 1.9 %collective-permute-start.6 = (f32[16,1024]{1,0:T(8,128)S(1)}, f32[16,1024]{1,0:T(8,128)S(1)}, u32[]{:S(2)}, u32[]{:S(2)}) collective-permute-start(f32[16,1024]{1,0:T(8,128)S(1)} %copy-done.14), channel_id=1, source_target_pairs={{4,8},{8,4},{12,16},{16,12},{20,24},{24,20},{28,32},{32,28},{36,40... | collective-permute-start | bytes 196616 | tf_op jit(solution)/shard_map/ppermute | solution.py:426
  102.6 8.6 %all-to-all-done.3 = f32[256,1,128]{2,1,0:T(1,128)S(1)} async-done(((f32[256,1,128]{2,1,0:T(1,128)}), f32[256,1,128]{2,1,0:T(1,128)S(1)}, u32[]{:S(2)}, u32[]{:S(2)}) %all-to-all-start.3) | async-done | bytes 131104 | tf_op jit(solution)/shard_map/all_to_all | solution.py:423
  111.3 0.7 copy-done.5
  111.9 13.4 %chain_second.1 = (f32[4,40,128]{2,1,0:T(8,128)}, f32[8,128]{1,0:T(8,128)}) custom-call(f32[32,40,128]{2,1,0:T(8,128)} %copy-done, f32[32,40,128]{2,1,0:T(8,128)} %copy-done.1, f32[256,128]{1,0:T(8,128)} %bitcast.15, f32[64,256]{1,0:T(8,128)} %bitcast.13, f32[384,128]{1,0:T(8,128)} %copy-done.3, f32[384,128]{1,0:T(8,128)} %copy-done.4, ...), custom_call_target="tpu_custom_call" | custom-call | tf_op jit(solution)/shard_map/chain_second/pallas_call | solution.py:457
  125.3 3.3 %all-to-all-start.4 = ((f32[4,40,128]{2,1,0:T(8,128)}), f32[4,40,128]{2,1,0:T(8,128)S(1)}, u32[]{:S(2)}, u32[]{:S(2)}) async-start(f32[4,40,128]{2,1,0:T(8,128)} %get-tuple-element.59), calls=%async_computation.4 | async-start | bytes 163840 | tf_op jit(solution)/shard_map/all_to_all | solution.py:423
  128.7 4.5 %all-to-all-done.4.got = f32[4,40,128]{2,1,0:T(8,128)S(1)} async-done(((f32[4,40,128]{2,1,0:T(8,128)}), f32[4,40,128]{2,1,0:T(8,128)S(1)}, u32[]{:S(2)}, u32[]{:S(2)}) %all-to-all-start.4) | async-done | bytes 81952 | tf_op jit(solution)/shard_map/all_to_all | solution.py:423
  133.2 0.6 copy-done.7
  133.8 3.6 %second.1 = (f32[4,16,1024]{2,1,0:T(8,128)}, f32[4,16,1024]{2,1,0:T(8,128)}, f32[4,16,1024]{2,1,0:T(8,128)}, f32[256,128]{1,0:T(8,128)}) custom-call(f32[4,40,128]{2,1,0:T(8,128)} %copy-done.7, f32[4,16,1024]{2,1,0:T(8,128)} %get-tuple-element.60.bj, f32[16,1024]{1,0:T(8,128)} %copy-done.10, f32[16,1024]{1,0:T(8,128)} %copy-done.11, s32[4,16,1024]{2,1,0:T(8,128)} %sub.5, ...), custom_call_target="tpu_custom_call" | custom-call | tf_op jit(solution)/shard_map/second/pallas_call | solution.py:461
  137.4 21.4 %all_to_all.31 = f32[256,1,128]{2,1,0:T(1,128)} all-to-all(f32[256,1,128]{2,1,0:T(1,128)} %bitcast.17), channel_id=1, replica_groups=mesh['slab'=64,'quad'=4] {'slab','quad'}, dimensions={0} | all-to-all | bytes 262144 | tf_op jit(solution)/shard_map/all_to_all | solution.py:423
  158.8 2.4 %last.1 = (f32[4,16,1024]{2,1,0:T(8,128)}, f32[4,16,1024]{2,1,0:T(8,128)}) custom-call(f32[256,128]{1,0:T(8,128)} %bitcast.14, f32[8,128]{1,0:T(8,128)} %get-tuple-element.65.dots, f32[4,16,1024]{2,1,0:T(8,128)} %get-tuple-element.63.z0, f32[4,16,1024]{2,1,0:T(8,128)} %get-tuple-element.64.q0, f32[4,16,1024]{2,1,0:T(8,128)} %get-tuple-element.67.z1, ...), custom_call_target="tpu_custom_call" | custom-call | tf_op jit(solution)/shard_map/last/pallas_call | solution.py:465
  (35 shorter events, 0.1 us)
Async XLA Ops:
  5.5 5.2 %copy-start.13 = (f32[384,128]{1,0:T(8,128)S(1)}, f32[384,128]{1,0:T(8,128)}, u32[]{:S(2)}) copy-start(f32[384,128]{1,0:T(8,128)} %get-tuple-element.37) | copy-start | bytes 589828
  5.5 6.9 %copy-start.12 = (f32[384,128]{1,0:T(8,128)S(1)}, f32[384,128]{1,0:T(8,128)}, u32[]{:S(2)}) copy-start(f32[384,128]{1,0:T(8,128)} %get-tuple-element.38) | copy-start | bytes 589828
  5.5 10.7 %all-to-all-start = ((f32[4,128,128]{2,1,0:T(8,128)}), f32[4,128,128]{2,1,0:T(8,128)S(1)}, u32[]{:S(2)}, u32[]{:S(2)}) async-start(f32[4,128,128]{2,1,0:T(8,128)} %get-tuple-element.39), calls=%async_computation | async-start | bytes 524288 | tf_op jit(solution)/shard_map/all_to_all | solution.py:423
  10.7 5.5 %collective-permute-start = (f32[384,128]{1,0:T(8,128)S(1)}, f32[384,128]{1,0:T(8,128)S(1)}, u32[]{:S(2)}, u32[]{:S(2)}) collective-permute-start(f32[384,128]{1,0:T(8,128)S(1)} %copy-done.13), channel_id=1, source_target_pairs={{0,4},{4,0},{8,12},{12,8},{16,20},{20,16},{24,28},{28,24},{32,36},... | collective-permute-start | bytes 589832 | tf_op jit(solution)/shard_map/ppermute | solution.py:426
  12.4 7.0 %collective-permute-start.1 = (f32[384,128]{1,0:T(8,128)S(1)}, f32[384,128]{1,0:T(8,128)S(1)}, u32[]{:S(2)}, u32[]{:S(2)}) collective-permute-start(f32[384,128]{1,0:T(8,128)S(1)} %copy-done.12), channel_id=1, source_target_pairs={{4,8},{8,4},{12,16},{16,12},{20,24},{24,20},{28,32},{32,28},{36,40... | collective-permute-start | bytes 589832 | tf_op jit(solution)/shard_map/ppermute | solution.py:426
  16.2 3.2 %copy-start.2 = (f32[4,128,128]{2,1,0:T(8,128)}, f32[4,128,128]{2,1,0:T(8,128)S(1)}, u32[]{:S(2)}) copy-start(f32[4,128,128]{2,1,0:T(8,128)S(1)} %all-to-all-done.got.cols) | copy-start | bytes 786436
  16.2 3.2 %copy-start.3 = (f32[384,128]{1,0:T(8,128)}, f32[384,128]{1,0:T(8,128)S(1)}, u32[]{:S(2)}) copy-start(f32[384,128]{1,0:T(8,128)S(1)} %collective-permute-done.core) | copy-start | bytes 589828
  19.4 0.7 copy-start.4
  23.5 32.3 %copy-start.17 = (f32[16,1024]{1,0:T(8,128)S(1)}, f32[16,1024]{1,0:T(8,128)}, u32[]{:S(2)}) copy-start(f32[16,1024]{1,0:T(8,128)} %get-tuple-element.44) | copy-start | bytes 196612
  23.5 32.4 %copy-start.16 = (f32[16,1024]{1,0:T(8,128)S(1)}, f32[16,1024]{1,0:T(8,128)}, u32[]{:S(2)}) copy-start(f32[16,1024]{1,0:T(8,128)} %get-tuple-element.45) | copy-start | bytes 196612
  51.6 8.2 %copy-start = (f32[32,40,128]{2,1,0:T(8,128)}, f32[32,40,128]{2,1,0:T(8,128)S(1)}, u32[]{:S(2)}) copy-start(f32[32,40,128]{2,1,0:T(8,128)S(1)} %all_to_all.30.own) | copy-start | bytes 1966084
  51.6 8.2 %collective-permute-start.2 = (f32[32,40,128]{2,1,0:T(8,128)S(1)}, f32[32,40,128]{2,1,0:T(8,128)S(1)}, u32[]{:S(2)}, u32[]{:S(2)}) collective-permute-start(f32[32,40,128]{2,1,0:T(8,128)S(1)} %all_to_all.30.own), channel_id=1, source_target_pairs={{0,4},{4,0},{8,12},{12,8},{16,20},{20,16},{24,28},{28,24},{32,36},... | collective-permute-start | bytes 1966088 | tf_op jit(solution)/shard_map/ppermute | solution.py:440
  55.8 22.7 %collective-permute-start.3 = (f32[16,1024]{1,0:T(8,128)S(1)}, f32[16,1024]{1,0:T(8,128)S(1)}, u32[]{:S(2)}, u32[]{:S(2)}) collective-permute-start(f32[16,1024]{1,0:T(8,128)S(1)} %copy-done.17), channel_id=1, source_target_pairs={{0,4},{4,0},{8,12},{12,8},{16,20},{20,16},{24,28},{28,24},{32,36},... | collective-permute-start | bytes 196616 | tf_op jit(solution)/shard_map/ppermute | solution.py:426
  55.9 22.6 %collective-permute-start.4 = (f32[16,1024]{1,0:T(8,128)S(1)}, f32[16,1024]{1,0:T(8,128)S(1)}, u32[]{:S(2)}, u32[]{:S(2)}) collective-permute-start(f32[16,1024]{1,0:T(8,128)S(1)} %copy-done.16), channel_id=1, source_target_pairs={{4,8},{8,4},{12,16},{16,12},{20,24},{24,20},{28,32},{32,28},{36,40... | collective-permute-start | bytes 196616 | tf_op jit(solution)/shard_map/ppermute | solution.py:426
  59.7 0.9 copy-start.1
  74.0 9.1 %all-to-all-start.2 = ((f32[4,40,128]{2,1,0:T(8,128)}), f32[4,40,128]{2,1,0:T(8,128)S(1)}, u32[]{:S(2)}, u32[]{:S(2)}) async-start(f32[4,40,128]{2,1,0:T(8,128)} %chain_first.1), calls=%async_computation.2 | async-start | bytes 163840 | tf_op jit(solution)/shard_map/all_to_all | solution.py:423
  78.5 4.6 %copy-start.8 = (f32[16,1024]{1,0:T(8,128)}, f32[16,1024]{1,0:T(8,128)S(1)}, u32[]{:S(2)}) copy-start(f32[16,1024]{1,0:T(8,128)S(1)} %collective-permute-done.3.core) | copy-start | bytes 196612
  78.5 4.6 %copy-start.9 = (f32[16,1024]{1,0:T(8,128)}, f32[16,1024]{1,0:T(8,128)S(1)}, u32[]{:S(2)}) copy-start(f32[16,1024]{1,0:T(8,128)S(1)} %collective-permute-done.4.near) | copy-start | bytes 196612
  83.1 0.6 copy-start.6
  90.2 8.3 %copy-start.15 = (f32[16,1024]{1,0:T(8,128)S(1)}, f32[16,1024]{1,0:T(8,128)}, u32[]{:S(2)}) copy-start(f32[16,1024]{1,0:T(8,128)} %get-tuple-element.61) | copy-start | bytes 196612
  90.2 10.5 %copy-start.14 = (f32[16,1024]{1,0:T(8,128)S(1)}, f32[16,1024]{1,0:T(8,128)}, u32[]{:S(2)}) copy-start(f32[16,1024]{1,0:T(8,128)} %get-tuple-element.62) | copy-start | bytes 196612
  90.2 21.0 %all-to-all-start.3 = ((f32[256,1,128]{2,1,0:T(1,128)}), f32[256,1,128]{2,1,0:T(1,128)S(1)}, u32[]{:S(2)}, u32[]{:S(2)}) async-start(f32[256,1,128]{2,1,0:T(1,128)} %bitcast.16), calls=%async_computation.3 | async-start | bytes 262144 | tf_op jit(solution)/shard_map/all_to_all | solution.py:423
  98.5 30.1 %collective-permute-start.5 = (f32[16,1024]{1,0:T(8,128)S(1)}, f32[16,1024]{1,0:T(8,128)S(1)}, u32[]{:S(2)}, u32[]{:S(2)}) collective-permute-start(f32[16,1024]{1,0:T(8,128)S(1)} %copy-done.15), channel_id=1, source_target_pairs={{0,4},{4,0},{8,12},{12,8},{16,20},{20,16},{24,28},{28,24},{32,36},... | collective-permute-start | bytes 196616 | tf_op jit(solution)/shard_map/ppermute | solution.py:426
  100.7 27.9 %collective-permute-start.6 = (f32[16,1024]{1,0:T(8,128)S(1)}, f32[16,1024]{1,0:T(8,128)S(1)}, u32[]{:S(2)}, u32[]{:S(2)}) collective-permute-start(f32[16,1024]{1,0:T(8,128)S(1)} %copy-done.14), channel_id=1, source_target_pairs={{4,8},{8,4},{12,16},{16,12},{20,24},{24,20},{28,32},{32,28},{36,40... | collective-permute-start | bytes 196616 | tf_op jit(solution)/shard_map/ppermute | solution.py:426
  111.3 0.7 copy-start.5
  125.3 7.8 %all-to-all-start.4 = ((f32[4,40,128]{2,1,0:T(8,128)}), f32[4,40,128]{2,1,0:T(8,128)S(1)}, u32[]{:S(2)}, u32[]{:S(2)}) async-start(f32[4,40,128]{2,1,0:T(8,128)} %get-tuple-element.59), calls=%async_computation.4 | async-start | bytes 163840 | tf_op jit(solution)/shard_map/all_to_all | solution.py:423
  128.6 4.5 %copy-start.10 = (f32[16,1024]{1,0:T(8,128)}, f32[16,1024]{1,0:T(8,128)S(1)}, u32[]{:S(2)}) copy-start(f32[16,1024]{1,0:T(8,128)S(1)} %collective-permute-done.5.core) | copy-start | bytes 196612
  128.7 4.5 %copy-start.11 = (f32[16,1024]{1,0:T(8,128)}, f32[16,1024]{1,0:T(8,128)S(1)}, u32[]{:S(2)}) copy-start(f32[16,1024]{1,0:T(8,128)S(1)} %collective-permute-done.6.near) | copy-start | bytes 196612
  133.2 0.6 copy-start.7

commit v3 on v2

--- a/solution.py
+++ b/solution.py
@@ -14,8 +14,72 @@
     return jax.ShapeDtypeStruct(shape, F32)
 
 
-def call(kernel, outs, scratch=()):
-    return pl.pallas_call(kernel, out_shape=outs, scratch_shapes=list(scratch), name=kernel.__name__)
+def call(kernel, outs, scratch=(), far=(), spread_out=()):
+    single = not isinstance(outs, tuple)
+    shapes = (outs,) if single else outs
+    whole = [-1 - i for i in spread_out if i < 0]
+    copied = [i for i in spread_out if i >= 0]
+    vmem, hbm = pl.BlockSpec(memory_space=pltpu.VMEM), pl.BlockSpec(memory_space=pltpu.HBM)
+
+    def run(*args):
+        count = len(args)
+        extra = [pltpu.VMEM(args[i].shape, args[i].dtype) for i in far]
+        extra += [pltpu.VMEM(shapes[i].shape, F32) for i in whole]
+        extra += [pltpu.VMEM(shapes[i].shape[1:], F32) for i in copied]
+        copies = len(far) + len(whole) + sum(shapes[i].shape[0] for i in copied)
+        if copies:
+            extra.append(pltpu.SemaphoreType.DMA((copies,)))
+
+        def wrapped(*refs):
+            ins, made = list(refs[:count]), list(refs[count : count + len(shapes)])
+            rest = list(refs[count + len(shapes) : count + len(shapes) + len(scratch)])
+            more = list(refs[count + len(shapes) + len(scratch) :])
+            sems = more.pop() if copies else None
+            coming = {}
+            for n, i in enumerate(far):
+                coming[i] = pltpu.make_async_copy(ins[i], more[n], sems.at[n])
+                coming[i].start()
+                ins[i] = more[n]
+            targets = {}
+            for n, i in enumerate(whole + copied):
+                targets[i] = made[i]
+                made[i] = more[len(far) + n]
+            waited = set()
+
+            def ready(*which):
+                for i in which:
+                    if i in coming and i not in waited:
+                        waited.add(i)
+                        coming[i].wait()
+
+            kernel(ready, *ins, *made, *rest)
+            ready(*far)
+            at = len(far)
+            going = []
+            for i in whole:
+                going.append(pltpu.make_async_copy(made[i], targets[i], sems.at[at]))
+                at += 1
+            for i in copied:
+                for m in range(shapes[i].shape[0]):
+                    going.append(pltpu.make_async_copy(made[i], targets[i].at[m], sems.at[at]))
+                    at += 1
+            for copy in going:
+                copy.start()
+            for copy in going:
+                copy.wait()
+
+        out = pl.pallas_call(
+            wrapped,
+            in_specs=[hbm if i in far else vmem for i in range(count)],
+            out_specs=tuple(hbm if i in whole + copied else vmem for i in range(len(shapes))),
+            out_shape=tuple(pltpu.HBM(s.shape, s.dtype) if i in whole + copied else s for i, s in enumerate(shapes)),
+            scratch_shapes=list(scratch) + extra,
+            compiler_params=pltpu.CompilerParams(vmem_limit_bytes=16 << 20),
+            name=kernel.__name__,
+        )(*[pltpu.with_memory_space_constraint(a, pltpu.HBM) if i in far else a for i, a in enumerate(args)])
+        return out[0] if single else out
+
+    return run
 
 
 def harmonic(here, there):
@@ -84,14 +148,14 @@
     return jnp.concatenate(rows, axis=0)
 
 
-def solve_lines(kz, inv, gam, rhs):
+def solve_lines(kz, inv, rhs):
     rho = [rhs[0] * inv[0]]
     for j in range(1, 4):
         rho.append((rhs[j] + kz[j] * rho[j - 1]) * inv[j])
     out = [None] * 4
     out[3] = rho[3]
     for j in (2, 1, 0):
-        out[j] = rho[j] - gam[j] * out[j + 1]
+        out[j] = rho[j] + kz[j + 1] * inv[j] * out[j + 1]
     return out
 
 
@@ -117,8 +181,11 @@
     return choose((lax.axis_index("quad") + 1 == dest).astype(jnp.int32), upward, downward)
 
 
-def begin(rs, ph, gain, sub, fac, mob, core, near, pay, rows):
+def begin(ready, rs, ph, gain, sub, fac, mob, core, near, pay, rows):
     odd = parity()
+    ready(0, 3)
+    cin = restrict(sub, rs, rows)
+    ready(1, 2, 4)
     ms, ss = [], []
     for z in range(4):
         m = 1.0 / (gain[z] * (0.001 + 0.999 * ph[z].astype(F32)))
@@ -134,7 +201,6 @@
         part[320:384, :] = fac[:, 128:]
     upward = jnp.concatenate([m[15:16, :] for m in ms] + [s[15:16, :] for s in ss], axis=0)
     downward = jnp.concatenate([m[0:1, :] for m in ms] + [s[0:1, :] for s in ss], axis=0)
-    cin = restrict(sub, rs, rows)
     both = jnp.concatenate([cin, cin], axis=1)
     lane = lane_of((64, 128))
     row = lax.broadcasted_iota(jnp.int32, (64, 128), 0)
@@ -157,7 +223,7 @@
 
 
 def setup(
-    rs, mob, core, near, fac, cou, got, kz, kyl, kyh, kxl, kxh, diag, inv, gam, bj, to_core, to_near, ups, downs, zsub, ysub, pay
+    ready, rs, mob, core, near, fac, cou, got, kz, ky, kyt, kx, kxe, inv, bj, to_core, to_near, ups, downs, zsub, ysub, cols, beside, pay
 ):
     odd = parity()
     quad = lax.axis_index("quad")
@@ -184,13 +250,11 @@
         b = harmonic(m, y_after(m, yhi[z : z + 1, :]))
         c = harmonic(m, x_before(m))
         d = harmonic(m, x_after(m))
-        kyl[z] = a
-        kyh[z] = b
-        kxl[z] = c
-        kxh[z] = d
-        total = faces[z] + faces[z + 1] + a + b + c + d
-        diag[z] = total
-        diags.append(total)
+        ky[z] = a
+        kyt[z : z + 1, :] = b[15:16, :]
+        kx[z] = c
+        kxe[z] = jnp.where(lane_of((16, 128)) == 127, d[:, 896:], 0.0)
+        diags.append(faces[z] + faces[z + 1] + a + b + c + d)
     invs = [1.0 / diags[0]]
     gams = [-faces[1] * invs[0]]
     for j in range(1, 4):
@@ -198,12 +262,18 @@
         gams.append(-faces[j + 1] * invs[j])
     for j in range(4):
         inv[j] = invs[j]
-    for j in range(3):
-        gam[j] = gams[j]
-    out = solve_lines(faces, invs, gams, [rs[z] for z in range(4)])
+    ready(0)
+    out = solve_lines(faces, invs, [rs[z] for z in range(4)])
     for z in range(4):
         bj[z] = out[z]
     send_faces(out, to_core, to_near, ups, downs)
+    for q in range(4):
+        cols[q] = got[q, 0:64, :]
+    c_fac = jnp.concatenate([core[256:320, :], core[320:384, :]], axis=1)
+    n_fac = jnp.concatenate([near[256:320, :], near[320:384, :]], axis=1)
+    beside[0] = choose(odd, c_fac, n_fac)
+    beside[1] = choose(odd, n_fac, c_fac)
+    ready(4, 5)
     cins = [pltpu.roll(got[q][0:8, :], 64, 1)[0:1, :64] for q in range(4)]
     cin = jnp.concatenate(cins, axis=1)
     rhs = lax.dot_general(
@@ -213,15 +283,15 @@
     mat = jnp.where(flag, cou[...], cou[...].T)
     packed = jnp.concatenate([mat[:32, :], mat[32:, :]], axis=1)
     tail = jnp.concatenate([rhs, rhs], axis=1)
-    for m in range(32):
-        pay[m, 0:32, :] = packed
-        pay[m, 32:40, :] = tail
-
-
-def chain(own, other, rhs_ref, fac, core, near, ups, downs, out, mats, us, uc, ws, wc):
+    pay[0:32, :] = packed
+    pay[32:40, :] = tail
+
+
+def chain(ready, own, other, rhs_ref, fac, beside, ups, downs, out, mats, us, uc, ws, wc):
     odd = lax.axis_index("slab") % 2
     lane = lane_of((32, 128))
     low = lane < 64
+    ready(0, 1)
     for m in range(32):
         for j, src in ((0, own), (1, other)):
             packed = src[m, 0:32, :]
@@ -229,31 +299,32 @@
             mats[at, 0:32, :] = jnp.where(low, packed, 0.0)
             mats[at, 32:64, :] = jnp.where(low, pltpu.roll(packed, 64, 1), 0.0)
     cols = rhs_ref[...].T
+    for k in range(1, 64, 2):
+        uc[k] = jnp.broadcast_to(cols[:64, k : k + 1], (64, 128))
     row = rhs_ref[0:1, :]
     us[0:1, :] = row
     col = None
     for k in range(1, 64):
         if k % 2:
-            col = jnp.sum(mats[k] * row, axis=1, keepdims=True) + cols[:64, k : k + 1]
-            uc[k] = jnp.broadcast_to(col, (64, 128))
+            col = jnp.broadcast_to(jnp.sum(mats[k] * row, axis=1, keepdims=True), (64, 128)) + uc[k]
+            uc[k] = col
         else:
             row = jnp.sum(mats[k] * col, axis=0, keepdims=True) + rhs_ref[k : k + 1, :]
             us[k : k + 1, :] = row
     ws[0:8, :] = jnp.zeros((8, 128), F32)
     wc[0] = jnp.zeros((64, 128), F32)
     wc[65] = jnp.zeros((64, 128), F32)
-    wc[64] = jnp.broadcast_to(col, (64, 128))
+    wc[64] = col
     for k in range(63, 0, -1):
         if k % 2:
             row = jnp.sum(mats[k] * col, axis=0, keepdims=True) + us[k - 1 : k, :]
             ws[k : k + 1, :] = row
         else:
-            col = jnp.sum(mats[k] * row, axis=1, keepdims=True) + uc[k - 1][:, 0:1]
-            wc[k] = jnp.broadcast_to(col, (64, 128))
+            col = jnp.broadcast_to(jnp.sum(mats[k] * row, axis=1, keepdims=True), (64, 128)) + uc[k - 1]
+            wc[k] = col
     slab = lax.axis_index("slab")
-    c_fac = jnp.concatenate([core[256:320, :], core[320:384, :]], axis=1)
-    n_fac = jnp.concatenate([near[256:320, :], near[320:384, :]], axis=1)
-    shares = ((0, fac[...]), (-1, choose(odd, c_fac, n_fac)), (1, choose(odd, n_fac, c_fac)))
+    ready(2, 3)
+    shares = ((0, fac[...]), (-1, beside[0]), (1, beside[1]))
     for j, (shift, table) in enumerate(shares):
         at = slab + shift + 1
         from_row = ws[pl.ds(jnp.minimum(at, 63), 1), :]
@@ -269,23 +340,23 @@
         spread(out.at[q], 8, face_for(q, ups[...], downs[...]))
 
 
-def chain_first(own, other, fac, core, near, ups, downs, out, mats, us, uc, ws, wc, rhs):
+def chain_first(ready, own, other, fac, beside, ups, downs, out, mats, us, uc, ws, wc, rhs):
     odd = lax.axis_index("slab") % 2
     lane = lane_of((1, 128))
     for m in range(32):
         for j, src in ((0, own), (1, other)):
             at = 2 * m + (odd if j == 0 else 1 - odd)
             rhs[pl.ds(at, 1), :] = jnp.where(lane < 64, src[m, 32:33, :], 0.0)
-    chain(own, other, rhs, fac, core, near, ups, downs, out, mats, us, uc, ws, wc)
-
-
-def chain_second(own, other, got, fac, core, near, ups, downs, out, dots, mats, us, uc, ws, wc, rhs):
+    chain(ready, own, other, rhs, fac, beside, ups, downs, out, mats, us, uc, ws, wc)
+
+
+def chain_second(ready, own, other, got, fac, beside, ups, downs, out, dots, mats, us, uc, ws, wc, rhs):
     total = got[pl.ds(0, 64, 4), :]
     for q in range(1, 4):
         total = total + got[pl.ds(q, 64, 4), :]
     rhs[...] = jnp.where(lane_of((64, 128)) < 64, total, 0.0)
     dots[...] = jnp.broadcast_to(jnp.sum(total, axis=0, keepdims=True), (8, 128))
-    chain(own, other, rhs, fac, core, near, ups, downs, out, mats, us, uc, ws, wc)
+    chain(ready, own, other, rhs, fac, beside, ups, downs, out, mats, us, uc, ws, wc)
 
 
 def tables(got):
@@ -313,7 +384,7 @@
     )
 
 
-def apply(got, bj, core, near, sub, zsub, ysub, kz, kyl, kyh, kxl, kxh, diag):
+def apply(got, bj, core, near, sub, zsub, ysub, kz, ky, kyt, kx, kxe):
     odd = parity()
     quad = lax.axis_index("quad")
     own, t_yl, t_yh, t_zl, t_zh = tables(got)
@@ -324,20 +395,17 @@
     after = gather_rows(got[jnp.minimum(quad + 1, 3)], 8, 4)
     before = jnp.where(jnp.broadcast_to(quad, before.shape) > 0, before, 0.0) + look_up(t_yl, ysub[...])[0:4, :]
     after = jnp.where(jnp.broadcast_to(quad, after.shape) < 3, after, 0.0) + look_up(t_yh, ysub[...])[4:8, :]
-    lower = [below] + planes[:3]
-    upper = planes[1:] + [above]
+    line = [below] + planes + [above]
+    rise = [kz[j] * (line[j + 1] - line[j]) for j in range(5)]
     images = []
     for z in range(4):
         v = planes[z]
-        images.append(
-            diag[z] * v
-            - kz[z] * lower[z]
-            - kz[z + 1] * upper[z]
-            - kyl[z] * y_before(v, before[z : z + 1, :])
-            - kyh[z] * y_after(v, after[z : z + 1, :])
-            - kxl[z] * x_before(v)
-            - kxh[z] * x_after(v)
-        )
+        y_low = ky[z] * (v - y_before(v, before[z : z + 1, :]))
+        y_high = y_after(y_low, kyt[z : z + 1, :] * (after[z : z + 1, :] - v[15:16, :]))
+        x_low = kx[z] * (v - x_before(v))
+        x_high = x_after(x_low)
+        x_high = jnp.concatenate([x_high[:, :896], x_high[:, 896:] - kxe[z] * v[:, 896:]], axis=1)
+        images.append((rise[z] - rise[z + 1]) + (y_low - y_high) + (x_low - x_high))
     return planes, images
 
 
@@ -349,16 +417,17 @@
 
 
 def first(
-    got, bj, core, near, sub, zsub, ysub, kz, kyl, kyh, kxl, kxh, diag, rs, inv, gam, cols,
+    ready, got, bj, core, near, sub, zsub, ysub, kz, ky, kyt, kx, kxe, rs, inv, cols,
     z_out, q_out, bj_out, to_core, to_near, ups, downs, pay, rows,
 ):
-    planes, images = apply(got, bj, core, near, sub, zsub, ysub, kz, kyl, kyh, kxl, kxh, diag)
+    ready(4, 12)
+    planes, images = apply(got, bj, core, near, sub, zsub, ysub, kz, ky, kyt, kx, kxe)
     for z in range(4):
         z_out[z] = planes[z]
         q_out[z] = images[z]
     rz = total_of([rs[z] for z in range(4)], planes)
     pq = total_of(planes, images)
-    out = solve_lines([kz[z] for z in range(4)], [inv[z] for z in range(4)], [gam[z] for z in range(3)], images)
+    out = solve_lines([kz[z] for z in range(5)], [inv[z] for z in range(4)], images)
     for z in range(4):
         bj_out[z] = out[z]
     send_faces(out, to_core, to_near, ups, downs)
@@ -371,16 +440,15 @@
         )[0:1, :]
         part = jnp.concatenate([part, part], axis=1)
         parts.append(jnp.where(lane < 64, part, jnp.where(lane == 64, rz, jnp.where(lane == 65, pq, 0.0))))
-    tile = jnp.concatenate(parts + parts, axis=0)
-    for j in range(32):
-        pay[j * 8 : (j + 1) * 8, :] = tile
+    pay[...] = jnp.concatenate(parts + parts, axis=0)
 
 
 def second(
-    got, bj, core, near, sub, zsub, ysub, kz, kyl, kyh, kxl, kxh, diag, rs, z0, q0, dots,
+    ready, got, bj, core, near, sub, zsub, ysub, kz, ky, kyt, kx, kxe, rs, z0, q0, dots,
     z_out, g_out, r_out, pay,
 ):
-    planes, images = apply(got, bj, core, near, sub, zsub, ysub, kz, kyl, kyh, kxl, kxh, diag)
+    ready(4, 12)
+    planes, images = apply(got, bj, core, near, sub, zsub, ysub, kz, ky, kyt, kx, kxe)
     alpha = dots[0:1, 64:65] / dots[0:1, 65:66]
     zs, gs, rr = [], [], []
     for z in range(4):
@@ -394,12 +462,10 @@
     own = total_of(zs, gs)
     cross = total_of([z0[z] for z in range(4)], gs)
     lane = lane_of((8, 128))
-    tile = jnp.where(lane == 0, new, jnp.where(lane == 1, own, jnp.where(lane == 2, cross, 0.0)))
-    for j in range(32):
-        pay[j * 8 : (j + 1) * 8, :] = tile
-
-
-def last(got, dots, z0, q0, z1, g1, r1, x_out, r_out):
+    pay[...] = jnp.where(lane == 0, new, jnp.where(lane == 1, own, jnp.where(lane == 2, cross, 0.0)))
+
+
+def last(ready, got, dots, z0, q0, z1, g1, r1, x_out, r_out):
     total = jnp.sum(got[...], axis=0, keepdims=True)
     new, own, cross = total[:, 0:1], total[:, 1:2], total[:, 2:3]
     rz, pq = dots[0:1, 64:65], dots[0:1, 65:66]
@@ -426,14 +492,22 @@
         return lax.ppermute(to_core, "slab", with_core), lax.ppermute(to_near, "slab", with_near)
 
     mob, core, near, pay = call(
-        begin, (grid, sds(384, 128), sds(384, 128), sds(4, 128, 128)), [pltpu.VMEM((64, 128), F32)]
+        begin,
+        (grid, sds(384, 128), sds(384, 128), sds(4, 128, 128)),
+        [pltpu.VMEM((64, 128), F32)],
+        (0, 1, 2, 3, 4),
+        (-4,),
     )(right_side, phase_label, density_gain, subdomain, fac)
     core, near = swap(core, near)
     got = exchange(pay, "quad")
-    kz, kyl, kyh, kxl, kxh, diag, inv, gam, bj, to_core, to_near, ups, downs, zsub, ysub, pay = call(
+    kz, ky, kyt, kx, kxe, inv, bj, to_core, to_near, ups, downs, zsub, ysub, cols, beside, pay = call(
         setup,
-        (sds(5, 16, 1024), grid, grid, grid, grid, grid, grid, sds(3, 16, 1024), grid, plane, plane, edge, edge)
-        + (jax.ShapeDtypeStruct((2, 16, 1024), jnp.int32), jax.ShapeDtypeStruct((8, 1024), jnp.int32), sds(32, 40, 128)),
+        (sds(5, 16, 1024), grid, edge, grid, sds(4, 16, 128), grid, grid, plane, plane, edge, edge)
+        + (jax.ShapeDtypeStruct((2, 16, 1024), jnp.int32), jax.ShapeDtypeStruct((8, 1024), jnp.int32))
+        + (sds(4, 64, 128), sds(2, 64, 256), sds(32, 40, 128)),
+        (),
+        (0, 4, 5),
+        (15,),
     )(right_side, mob, core, near, fac, cou, got)
     bj_core, bj_near = swap(to_core, to_near)
     own = exchange(pay, "slab", cores)
@@ -446,19 +520,23 @@
         pltpu.VMEM((66, 64, 128), F32),
         pltpu.VMEM((64, 128), F32),
     ]
-    part = call(chain_first, sds(4, 40, 128), work)(own, other, fac, core, near, ups, downs)
+    part = call(chain_first, sds(4, 40, 128), work, (2,), (-1,))(own, other, fac, beside, ups, downs)
     coarse = exchange(part, "quad")
-    stencil = (subdomain, zsub, ysub, kz, kyl, kyh, kxl, kxh, diag, right_side)
+    stencil = (subdomain, zsub, ysub, kz, ky, kyt, kx, kxe, right_side)
     z0, q0, bj1, to_core, to_near, ups, downs, pay = call(
-        first, (grid, grid, grid, plane, plane, edge, edge, sds(256, 128)), [pltpu.VMEM((64, 128), F32)]
-    )(coarse, bj, bj_core, bj_near, *stencil, inv, gam, got)
+        first,
+        (grid, grid, grid, plane, plane, edge, edge, sds(32, 8, 128)),
+        [pltpu.VMEM((64, 128), F32)],
+        (4, 12),
+        (7,),
+    )(coarse, bj, bj_core, bj_near, *stencil, inv, cols)
     bj_core, bj_near = swap(to_core, to_near)
     everyone = exchange(pay.reshape(256, 1, 128), BOTH).reshape(256, 128)
-    part, dots = call(chain_second, (sds(4, 40, 128), sds(8, 128)), work)(
-        own, other, everyone, fac, core, near, ups, downs
+    part, dots = call(chain_second, (sds(4, 40, 128), sds(8, 128)), work, (0, 1, 3), (-1,))(
+        own, other, everyone, fac, beside, ups, downs
     )
     coarse = exchange(part, "quad")
-    z1, g1, r1, pay = call(second, (grid, grid, grid, sds(256, 128)))(
+    z1, g1, r1, pay = call(second, (grid, grid, grid, sds(32, 8, 128)), (), (4, 12), (3,))(
         coarse, bj1, bj_core, bj_near, *stencil, z0, q0, dots
     )
     everyone = exchange(pay.reshape(256, 1, 128), BOTH).reshape(256, 128)

time: 162 us -> 144 us (0.89)
  Pallas kernels: 47.6 us -> 34.7 us
  local copies, waits for them, and re-layouts: 3.48 us -> 0.01 us
    pallas_call x7, Pallas kernels: 47.6 us -> 34.7 us  [run(): pl.pallas_call(wrapped, in_specs=[hbm if i in far else vmem for i in rang...]
    unnamed x36 -> x4, local copies, waits for them, and re-layouts: 3.48 us -> 0.01 us
  transfers between devices with their start and end apart: 11 -> 11, of which waited for: 5 -> 5; matrix products, arithmetic and copies ran while one was open for 0% -> 0% of each run, Pallas kernels for 17% -> 12%
where the time goes in v3:
time: 144 us
  blocking collectives  48.5 us (34%)
  starting transfers between devices  37.6 us (26%)
  Pallas kernels  34.7 us (24%)
  waiting for transfers between devices  22 us (15%)
    all_to_all x2, blocking collectives, exchange(): lax.all_to_all(value, axis, 0, 0, tiled=True, axis_index_groups=groups)  48.5 us
    pallas_call x7, Pallas kernels, run(): pl.pallas_call(wrapped, in_specs=[hbm if i in far else vmem for i in rang...  34.7 us
    all_to_all x4, starting transfers between devices, exchange(): lax.all_to_all(value, axis, 0, 0, tiled=True, axis_index_groups=groups)  21 us
    all_to_all x4, waiting for transfers between devices, exchange(): lax.all_to_all(value, axis, 0, 0, tiled=True, axis_index_groups=groups)  18.8 us
    ppermute x3, starting transfers between devices, swap(): lax.ppermute(to_near, 'slab', with_near)  8.54 us
    ppermute x1, starting transfers between devices, body(): other = lax.ppermute(own, 'slab', with_core)  4.12 us
    ppermute x3, starting transfers between devices, swap(): lax.ppermute(to_core, 'slab', with_core)  3.96 us
    ppermute x3, waiting for transfers between devices, swap(): lax.ppermute(to_near, 'slab', with_near)  3.18 us
  transfers between devices with their start and end apart: 11, of which 5 were waited for; matrix products, arithmetic and copies ran while one was open for 0% of the time, Pallas kernels for 12%

profile of v3, /device:TPU:1, one launch (start us, length us, event | category | flops | bytes accessed | tf_op | source)
XLA Modules:
  0.0 143.6 jit_solution(2374248671317919246)
XLA Ops:
  0.6 4.9 %begin.1 = (f32[4,16,1024]{2,1,0:T(8,128)S(1)}, f32[384,128]{1,0:T(8,128)S(1)}, f32[384,128]{1,0:T(8,128)S(1)}, f32[4,128,128]{2,1,0:T(8,128)}) custom-call(f32[4,16,1024]{2,1,0:T(8,128)} %refs_12_.3, s32[4,16,1024]{2,1,0:T(8,128)} %refs_1_.1, f32[4,16,1024]{2,1,0:T(8,128)} %refs_2_.1, s32[4,16,1024]{2,1,0:T(8,128)} %refs_4_.3, f32[64,256]{1,0:T(8,128)} %bitcast.12), custom_call_target="tpu_custom_call" | custom-call | tf_op jit(solution)/shard_map/begin/pallas_call | solution.py:71
  5.5 5.0 %all-to-all-start = ((f32[4,128,128]{2,1,0:T(8,128)}), f32[4,128,128]{2,1,0:T(8,128)S(1)}, u32[]{:S(2)}, u32[]{:S(2)}) async-start(f32[4,128,128]{2,1,0:T(8,128)} %get-tuple-element.39), calls=%async_computation | async-start | bytes 524288 | tf_op jit(solution)/shard_map/all_to_all | solution.py:489
  10.5 1.7 %collective-permute-start = (f32[384,128]{1,0:T(8,128)S(1)}, f32[384,128]{1,0:T(8,128)S(1)}, u32[]{:S(2)}, u32[]{:S(2)}) collective-permute-start(f32[384,128]{1,0:T(8,128)S(1)} %get-tuple-element.37), channel_id=1, source_target_pairs={{0,4},{4,0},{8,12},{12,8},{16,20},{20,16},{24,28},{28,24},{32,36},... | collective-permute-start | bytes 589832 | tf_op jit(solution)/shard_map/ppermute | solution.py:492
  12.3 2.6 %collective-permute-start.1 = (f32[384,128]{1,0:T(8,128)S(1)}, f32[384,128]{1,0:T(8,128)S(1)}, u32[]{:S(2)}, u32[]{:S(2)}) collective-permute-start(f32[384,128]{1,0:T(8,128)S(1)} %get-tuple-element.38), channel_id=1, source_target_pairs={{4,8},{8,4},{12,16},{16,12},{20,24},{24,20},{28,32},{32,28},{36,40... | collective-permute-start | bytes 589832 | tf_op jit(solution)/shard_map/ppermute | solution.py:492
  14.9 1.1 all-to-all-done.refs_6_
  16.1 0.0 collective-permute-done.refs_2_
  16.1 3.2 %collective-permute-done.1.refs_3_ = f32[384,128]{1,0:T(8,128)S(1)} collective-permute-done((f32[384,128]{1,0:T(8,128)S(1)}, f32[384,128]{1,0:T(8,128)S(1)}, u32[]{:S(2)}, u32[]{:S(2)}) %collective-permute-start.1) | collective-permute-done | bytes 196640 | tf_op jit(solution)/shard_map/ppermute | solution.py:492
  19.3 2.7 %setup.1 = (f32[5,16,1024]{2,1,0:T(8,128)S(1)}, f32[4,16,1024]{2,1,0:T(8,128)S(1)}, f32[4,1024]{1,0:T(4,128)S(1)}, f32[4,16,1024]{2,1,0:T(8,128)S(1)}, f32[4,16,...) custom-call(f32[4,16,1024]{2,1,0:T(8,128)} %refs_12_.3, ...), custom_call_target="tpu_custom_call" | custom-call | tf_op jit(solution)/shard_map/setup/pallas_call | solution.py:71
  22.0 28.0 %all_to_all.30.refs_0_ = f32[32,40,128]{2,1,0:T(8,128)S(1)} all-to-all(f32[32,40,128]{2,1,0:T(8,128)} %get-tuple-element.40), channel_id=1, replica_groups={{0,8,16,24,32,40,48,56,64,72,80,88,96,104,112,120,128,136,144,152,160,1..., dimensions={0} | all-to-all | bytes 1310720 | tf_op jit(solution)/shard_map/all_to_all | solution.py:489
  50.0 4.1 %collective-permute-start.2 = (f32[32,40,128]{2,1,0:T(8,128)S(1)}, f32[32,40,128]{2,1,0:T(8,128)S(1)}, u32[]{:S(2)}, u32[]{:S(2)}) collective-permute-start(f32[32,40,128]{2,1,0:T(8,128)S(1)} %all_to_all.30.refs_0_), channel_id=1, source_target_pairs={{0,4},{4,0},{8,12},{12,8},{16,20},{20,16},{24,28},{28,24},{32,36},... | collective-permute-start | bytes 1966088 | tf_op jit(solution)/shard_map/ppermute | solution.py:514
  54.1 0.0 collective-permute-start.3
  54.1 4.0 %collective-permute-start.4 = (f32[16,1024]{1,0:T(8,128)S(1)}, f32[16,1024]{1,0:T(8,128)S(1)}, u32[]{:S(2)}, u32[]{:S(2)}) collective-permute-start(f32[16,1024]{1,0:T(8,128)S(1)} %get-tuple-element.46), channel_id=1, source_target_pairs={{4,8},{8,4},{12,16},{16,12},{20,24},{24,20},{28,32},{32,28},{36,40... | collective-permute-start | bytes 196616 | tf_op jit(solution)/shard_map/ppermute | solution.py:492
  58.1 0.0 collective-permute-done.2.refs_1_
  58.1 8.0 %chain_first.1 = f32[4,40,128]{2,1,0:T(8,128)} custom-call(f32[32,40,128]{2,1,0:T(8,128)S(1)} %all_to_all.30.refs_0_, f32[32,40,128]{2,1,0:T(8,128)S(1)} %collective-permute-done.2.refs_1_, f32[64,256]{1,0:T(8,128)} %bitcast.14, f32[2,64,256]{2,1,0:T(8,128)S(1)} %get-tuple-element.41.refs_3_.refs_4_, f32[4,1024]{1,0:T(4,128)S(1)} %get-tuple-element.42.refs_4_, ...), custom_call_target="tpu_custom_call" | custom-call | tf_op jit(solution)/shard_map/chain_first/pallas_call | solution.py:71
  66.1 0.0 copy-done
  66.1 4.5 %all-to-all-start.2 = ((f32[4,40,128]{2,1,0:T(8,128)}), f32[4,40,128]{2,1,0:T(8,128)S(1)}, u32[]{:S(2)}, u32[]{:S(2)}) async-start(f32[4,40,128]{2,1,0:T(8,128)} %chain_first.1), calls=%async_computation.2 | async-start | bytes 163840 | tf_op jit(solution)/shard_map/all_to_all | solution.py:489
  70.6 0.0 collective-permute-done.3.refs_2_
  70.6 0.0 collective-permute-done.4.refs_3_
  70.6 4.6 %all-to-all-done.2.refs_0_ = f32[4,40,128]{2,1,0:T(8,128)S(1)} async-done(((f32[4,40,128]{2,1,0:T(8,128)}), f32[4,40,128]{2,1,0:T(8,128)S(1)}, u32[]{:S(2)}, u32[]{:S(2)}) %all-to-all-start.2) | async-done | bytes 81952 | tf_op jit(solution)/shard_map/all_to_all | solution.py:489
  75.2 6.0 %first.1 = (f32[4,16,1024]{2,1,0:T(8,128)S(1)}, f32[4,16,1024]{2,1,0:T(8,128)S(1)}, f32[4,16,1024]{2,1,0:T(8,128)S(1)}, f32[16,1024]{1,0:T(8,128)S(1)}, f32[16,1...) custom-call(f32[4,40,128]{2,1,0:T(8,128)S(1)} %all-to-all-done.2.refs_0_, ...), custom_call_target="tpu_custom_call" | custom-call | tf_op jit(solution)/shard_map/first/pallas_call | solution.py:71
  81.2 8.2 %all-to-all-start.3 = ((f32[256,1,128]{2,1,0:T(1,128)}), f32[256,1,128]{2,1,0:T(1,128)S(1)}, u32[]{:S(2)}, u32[]{:S(2)}) async-start(f32[256,1,128]{2,1,0:T(1,128)} %bitcast.16), calls=%async_computation.3 | async-start | bytes 262144 | tf_op jit(solution)/shard_map/all_to_all | solution.py:489
  89.3 2.2 %collective-permute-start.5 = (f32[16,1024]{1,0:T(8,128)S(1)}, f32[16,1024]{1,0:T(8,128)S(1)}, u32[]{:S(2)}, u32[]{:S(2)}) collective-permute-start(f32[16,1024]{1,0:T(8,128)S(1)} %get-tuple-element.61), channel_id=1, source_target_pairs={{0,4},{4,0},{8,12},{12,8},{16,20},{20,16},{24,28},{28,24},{32,36},... | collective-permute-start | bytes 196616 | tf_op jit(solution)/shard_map/ppermute | solution.py:492
  91.5 1.9 %collective-permute-start.6 = (f32[16,1024]{1,0:T(8,128)S(1)}, f32[16,1024]{1,0:T(8,128)S(1)}, u32[]{:S(2)}, u32[]{:S(2)}) collective-permute-start(f32[16,1024]{1,0:T(8,128)S(1)} %get-tuple-element.62), channel_id=1, source_target_pairs={{4,8},{8,4},{12,16},{16,12},{20,24},{24,20},{28,32},{32,28},{36,40... | collective-permute-start | bytes 196616 | tf_op jit(solution)/shard_map/ppermute | solution.py:492
  93.5 8.6 %all-to-all-done.3 = f32[256,1,128]{2,1,0:T(1,128)S(1)} async-done(((f32[256,1,128]{2,1,0:T(1,128)}), f32[256,1,128]{2,1,0:T(1,128)S(1)}, u32[]{:S(2)}, u32[]{:S(2)}) %all-to-all-start.3) | async-done | bytes 131104 | tf_op jit(solution)/shard_map/all_to_all | solution.py:489
  102.0 9.2 %chain_second.1 = (f32[4,40,128]{2,1,0:T(8,128)}, f32[8,128]{1,0:T(8,128)S(1)}) custom-call(f32[32,40,128]{2,1,0:T(8,128)} %copy-done, f32[32,40,128]{2,1,0:T(8,128)} %copy-done.1, f32[256,128]{1,0:T(8,128)S(1)} %bitcast.10, f32[64,256]{1,0:T(8,128)} %bitcast.15, f32[2,64,256]{2,1,0:T(8,128)S(1)} %get-tuple-element.41.refs_3_.refs_4_, ...), custom_call_target="tpu_custom_call" | custom-call | tf_op jit(solution)/shard_map/chain_second/pallas_call | solution.py:71
  111.3 3.3 %all-to-all-start.4 = ((f32[4,40,128]{2,1,0:T(8,128)}), f32[4,40,128]{2,1,0:T(8,128)S(1)}, u32[]{:S(2)}, u32[]{:S(2)}) async-start(f32[4,40,128]{2,1,0:T(8,128)} %get-tuple-element.59), calls=%async_computation.4 | async-start | bytes 163840 | tf_op jit(solution)/shard_map/all_to_all | solution.py:489
  114.6 0.0 collective-permute-done.5.refs_2_
  114.6 0.0 collective-permute-done.6.refs_3_
  114.6 4.5 %all-to-all-done.4.refs_0_ = f32[4,40,128]{2,1,0:T(8,128)S(1)} async-done(((f32[4,40,128]{2,1,0:T(8,128)}), f32[4,40,128]{2,1,0:T(8,128)S(1)}, u32[]{:S(2)}, u32[]{:S(2)}) %all-to-all-start.4) | async-done | bytes 81952 | tf_op jit(solution)/shard_map/all_to_all | solution.py:489
  119.1 2.9 %second.1 = (f32[4,16,1024]{2,1,0:T(8,128)S(1)}, f32[4,16,1024]{2,1,0:T(8,128)S(1)}, f32[4,16,1024]{2,1,0:T(8,128)S(1)}, f32[32,8,128]{2,1,0:T(8,128)}) custom-call(f32[4,40,128]{2,1,0:T(8,128)S(1)} %all-to-all-done.4.refs_0_, f32[4,16,1024]{2,1,0:T(8,128)S(1)} %get-tuple-element.60.refs_1_, f32[16,1024]{1,0:T(8,128)S(1)} %collective-permute-done.5.refs_2_, ...), custom_call_target="tpu_custom_call" | custom-call | tf_op jit(solution)/shard_map/second/pallas_call | solution.py:71
  122.0 20.5 %all_to_all.31 = f32[256,1,128]{2,1,0:T(1,128)S(1)} all-to-all(f32[256,1,128]{2,1,0:T(1,128)} %bitcast.17), channel_id=1, replica_groups=mesh['slab'=64,'quad'=4] {'slab','quad'}, dimensions={0} | all-to-all | bytes 262144 | tf_op jit(solution)/shard_map/all_to_all | solution.py:489
  142.5 1.1 last.1
  (3 shorter events, 0.0 us)
Async XLA Ops:
  5.5 10.6 %all-to-all-start = ((f32[4,128,128]{2,1,0:T(8,128)}), f32[4,128,128]{2,1,0:T(8,128)S(1)}, u32[]{:S(2)}, u32[]{:S(2)}) async-start(f32[4,128,128]{2,1,0:T(8,128)} %get-tuple-element.39), calls=%async_computation | async-start | bytes 524288 | tf_op jit(solution)/shard_map/all_to_all | solution.py:489
  10.5 5.5 %collective-permute-start = (f32[384,128]{1,0:T(8,128)S(1)}, f32[384,128]{1,0:T(8,128)S(1)}, u32[]{:S(2)}, u32[]{:S(2)}) collective-permute-start(f32[384,128]{1,0:T(8,128)S(1)} %get-tuple-element.37), channel_id=1, source_target_pairs={{0,4},{4,0},{8,12},{12,8},{16,20},{20,16},{24,28},{28,24},{32,36},... | collective-permute-start | bytes 589832 | tf_op jit(solution)/shard_map/ppermute | solution.py:492
  12.3 7.0 %collective-permute-start.1 = (f32[384,128]{1,0:T(8,128)S(1)}, f32[384,128]{1,0:T(8,128)S(1)}, u32[]{:S(2)}, u32[]{:S(2)}) collective-permute-start(f32[384,128]{1,0:T(8,128)S(1)} %get-tuple-element.38), channel_id=1, source_target_pairs={{4,8},{8,4},{12,16},{16,12},{20,24},{24,20},{28,32},{32,28},{36,40... | collective-permute-start | bytes 589832 | tf_op jit(solution)/shard_map/ppermute | solution.py:492
  50.0 16.1 %copy-start = (f32[32,40,128]{2,1,0:T(8,128)}, f32[32,40,128]{2,1,0:T(8,128)S(1)}, u32[]{:S(2)}) copy-start(f32[32,40,128]{2,1,0:T(8,128)S(1)} %all_to_all.30.refs_0_) | copy-start | bytes 1966084
  50.0 8.1 %collective-permute-start.2 = (f32[32,40,128]{2,1,0:T(8,128)S(1)}, f32[32,40,128]{2,1,0:T(8,128)S(1)}, u32[]{:S(2)}, u32[]{:S(2)}) collective-permute-start(f32[32,40,128]{2,1,0:T(8,128)S(1)} %all_to_all.30.refs_0_), channel_id=1, source_target_pairs={{0,4},{4,0},{8,12},{12,8},{16,20},{20,16},{24,28},{28,24},{32,36},... | collective-permute-start | bytes 1966088 | tf_op jit(solution)/shard_map/ppermute | solution.py:514
  54.1 16.5 %collective-permute-start.3 = (f32[16,1024]{1,0:T(8,128)S(1)}, f32[16,1024]{1,0:T(8,128)S(1)}, u32[]{:S(2)}, u32[]{:S(2)}) collective-permute-start(f32[16,1024]{1,0:T(8,128)S(1)} %get-tuple-element.45), channel_id=1, source_target_pairs={{0,4},{4,0},{8,12},{12,8},{16,20},{20,16},{24,28},{28,24},{32,36},... | collective-permute-start | bytes 196616 | tf_op jit(solution)/shard_map/ppermute | solution.py:492
  54.1 16.5 %collective-permute-start.4 = (f32[16,1024]{1,0:T(8,128)S(1)}, f32[16,1024]{1,0:T(8,128)S(1)}, u32[]{:S(2)}, u32[]{:S(2)}) collective-permute-start(f32[16,1024]{1,0:T(8,128)S(1)} %get-tuple-element.46), channel_id=1, source_target_pairs={{4,8},{8,4},{12,16},{16,12},{20,24},{24,20},{28,32},{32,28},{36,40... | collective-permute-start | bytes 196616 | tf_op jit(solution)/shard_map/ppermute | solution.py:492
  58.1 8.0 %copy-start.1 = (f32[32,40,128]{2,1,0:T(8,128)}, f32[32,40,128]{2,1,0:T(8,128)S(1)}, u32[]{:S(2)}) copy-start(f32[32,40,128]{2,1,0:T(8,128)S(1)} %collective-permute-done.2.refs_1_) | copy-start | bytes 1966084
  66.1 9.1 %all-to-all-start.2 = ((f32[4,40,128]{2,1,0:T(8,128)}), f32[4,40,128]{2,1,0:T(8,128)S(1)}, u32[]{:S(2)}, u32[]{:S(2)}) async-start(f32[4,40,128]{2,1,0:T(8,128)} %chain_first.1), calls=%async_computation.2 | async-start | bytes 163840 | tf_op jit(solution)/shard_map/all_to_all | solution.py:489
  81.2 20.9 %all-to-all-start.3 = ((f32[256,1,128]{2,1,0:T(1,128)}), f32[256,1,128]{2,1,0:T(1,128)S(1)}, u32[]{:S(2)}, u32[]{:S(2)}) async-start(f32[256,1,128]{2,1,0:T(1,128)} %bitcast.16), calls=%async_computation.3 | async-start | bytes 262144 | tf_op jit(solution)/shard_map/all_to_all | solution.py:489
  89.3 25.3 %collective-permute-start.5 = (f32[16,1024]{1,0:T(8,128)S(1)}, f32[16,1024]{1,0:T(8,128)S(1)}, u32[]{:S(2)}, u32[]{:S(2)}) collective-permute-start(f32[16,1024]{1,0:T(8,128)S(1)} %get-tuple-element.61), channel_id=1, source_target_pairs={{0,4},{4,0},{8,12},{12,8},{16,20},{20,16},{24,28},{28,24},{32,36},... | collective-permute-start | bytes 196616 | tf_op jit(solution)/shard_map/ppermute | solution.py:492
  91.5 23.1 %collective-permute-start.6 = (f32[16,1024]{1,0:T(8,128)S(1)}, f32[16,1024]{1,0:T(8,128)S(1)}, u32[]{:S(2)}, u32[]{:S(2)}) collective-permute-start(f32[16,1024]{1,0:T(8,128)S(1)} %get-tuple-element.62), channel_id=1, source_target_pairs={{4,8},{8,4},{12,16},{16,12},{20,24},{24,20},{28,32},{32,28},{36,40... | collective-permute-start | bytes 196616 | tf_op jit(solution)/shard_map/ppermute | solution.py:492
  111.3 7.8 %all-to-all-start.4 = ((f32[4,40,128]{2,1,0:T(8,128)}), f32[4,40,128]{2,1,0:T(8,128)S(1)}, u32[]{:S(2)}, u32[]{:S(2)}) async-start(f32[4,40,128]{2,1,0:T(8,128)} %get-tuple-element.59), calls=%async_computation.4 | async-start | bytes 163840 | tf_op jit(solution)/shard_map/all_to_all | solution.py:489

commit v4 on v3

--- a/solution.py
+++ b/solution.py
@@ -8,6 +8,7 @@
 F32 = jnp.float32
 HIGH = lax.Precision.HIGHEST
 BOTH = ("slab", "quad")
+PIECES = 4
 
 
 def sds(*shape):
@@ -26,7 +27,8 @@
         extra = [pltpu.VMEM(args[i].shape, args[i].dtype) for i in far]
         extra += [pltpu.VMEM(shapes[i].shape, F32) for i in whole]
         extra += [pltpu.VMEM(shapes[i].shape[1:], F32) for i in copied]
-        copies = len(far) + len(whole) + sum(shapes[i].shape[0] for i in copied)
+        pieces_of = {i: PIECES if len(args[i].shape) == 3 and args[i].shape[0] % 8 == 0 else 1 for i in far}
+        copies = sum(pieces_of.values()) + len(whole) + sum(shapes[i].shape[0] for i in copied)
         if copies:
             extra.append(pltpu.SemaphoreType.DMA((copies,)))
 
@@ -35,10 +37,17 @@
             rest = list(refs[count + len(shapes) : count + len(shapes) + len(scratch)])
             more = list(refs[count + len(shapes) + len(scratch) :])
             sems = more.pop() if copies else None
-            coming = {}
+            coming, at = {}, 0
             for n, i in enumerate(far):
-                coming[i] = pltpu.make_async_copy(ins[i], more[n], sems.at[n])
-                coming[i].start()
+                size = ins[i].shape[0] // pieces_of[i]
+                coming[i] = []
+                for p in range(pieces_of[i]):
+                    src, dst = ins[i], more[n]
+                    if pieces_of[i] > 1:
+                        src, dst = src.at[pl.ds(p * size, size)], dst.at[pl.ds(p * size, size)]
+                    coming[i].append(pltpu.make_async_copy(src, dst, sems.at[at]))
+                    coming[i][p].start()
+                    at += 1
                 ins[i] = more[n]
             targets = {}
             for n, i in enumerate(whole + copied):
@@ -46,15 +55,16 @@
                 made[i] = more[len(far) + n]
             waited = set()
 
-            def ready(*which):
+            def ready(*which, pieces=range(PIECES)):
                 for i in which:
-                    if i in coming and i not in waited:
-                        waited.add(i)
-                        coming[i].wait()
+                    for p in pieces:
+                        if i in coming and p < pieces_of[i] and (i, p) not in waited:
+                            waited.add((i, p))
+                            coming[i][p].wait()
 
             kernel(ready, *ins, *made, *rest)
             ready(*far)
-            at = len(far)
+            at = sum(pieces_of.values())
             going = []
             for i in whole:
                 going.append(pltpu.make_async_copy(made[i], targets[i], sems.at[at]))
@@ -222,8 +232,23 @@
         downs[z : z + 1, :] = out[z][0:1, :]
 
 
+def share(ready, got, fac, cou, cols, pay):
+    for q in range(4):
+        cols[q] = got[q, 0:64, :]
+    cins = [pltpu.roll(got[q, 0:8, :], 64, 1)[0:1, :64] for q in range(4)]
+    cin = jnp.concatenate(cins, axis=1)
+    ready(1)
+    rhs = lax.dot_general(
+        jnp.broadcast_to(cin, (8, 256)), fac[...], (((1,), (1,)), ((), ())), precision=HIGH, preferred_element_type=F32
+    )
+    ready(2)
+    mat = choose(parity(), cou[...], cou[...].T)
+    pay[0:32, :] = jnp.concatenate([mat[:32, :], mat[32:, :]], axis=1)
+    pay[32:40, :] = jnp.concatenate([rhs, rhs], axis=1)
+
+
 def setup(
-    ready, rs, mob, core, near, fac, cou, got, kz, ky, kyt, kx, kxe, inv, bj, to_core, to_near, ups, downs, zsub, ysub, cols, beside, pay
+    ready, rs, mob, core, near, got, kz, ky, kyt, kx, kxe, inv, bj, to_core, to_near, ups, downs, zsub, ysub, beside
 ):
     odd = parity()
     quad = lax.axis_index("quad")
@@ -234,6 +259,10 @@
     above = planes[1:] + [choose(odd, n_mob, c_mob)]
     zsub[0] = choose(odd, c_sub, n_sub).astype(jnp.int32)
     zsub[1] = choose(odd, n_sub, c_sub).astype(jnp.int32)
+    c_fac = jnp.concatenate([core[256:320, :], core[320:384, :]], axis=1)
+    n_fac = jnp.concatenate([near[256:320, :], near[320:384, :]], axis=1)
+    beside[0] = choose(odd, c_fac, n_fac)
+    beside[1] = choose(odd, n_fac, c_fac)
     before = gather_rows(got[jnp.maximum(quad - 1, 0)], 64, 8)
     after = gather_rows(got[jnp.minimum(quad + 1, 3)], 64, 8)
     ylo = jnp.where(jnp.broadcast_to(quad, before.shape) > 0, before, 0.0)
@@ -256,10 +285,8 @@
         kxe[z] = jnp.where(lane_of((16, 128)) == 127, d[:, 896:], 0.0)
         diags.append(faces[z] + faces[z + 1] + a + b + c + d)
     invs = [1.0 / diags[0]]
-    gams = [-faces[1] * invs[0]]
     for j in range(1, 4):
-        invs.append(1.0 / (diags[j] + faces[j] * gams[j - 1]))
-        gams.append(-faces[j + 1] * invs[j])
+        invs.append(1.0 / (diags[j] - faces[j] * faces[j] * invs[j - 1]))
     for j in range(4):
         inv[j] = invs[j]
     ready(0)
@@ -267,37 +294,18 @@
     for z in range(4):
         bj[z] = out[z]
     send_faces(out, to_core, to_near, ups, downs)
-    for q in range(4):
-        cols[q] = got[q, 0:64, :]
-    c_fac = jnp.concatenate([core[256:320, :], core[320:384, :]], axis=1)
-    n_fac = jnp.concatenate([near[256:320, :], near[320:384, :]], axis=1)
-    beside[0] = choose(odd, c_fac, n_fac)
-    beside[1] = choose(odd, n_fac, c_fac)
-    ready(4, 5)
-    cins = [pltpu.roll(got[q][0:8, :], 64, 1)[0:1, :64] for q in range(4)]
-    cin = jnp.concatenate(cins, axis=1)
-    rhs = lax.dot_general(
-        jnp.broadcast_to(cin, (8, 256)), fac[...], (((1,), (1,)), ((), ())), precision=HIGH, preferred_element_type=F32
-    )
-    flag = jnp.broadcast_to(odd, (64, 64)) == 1
-    mat = jnp.where(flag, cou[...], cou[...].T)
-    packed = jnp.concatenate([mat[:32, :], mat[32:, :]], axis=1)
-    tail = jnp.concatenate([rhs, rhs], axis=1)
-    pay[0:32, :] = packed
-    pay[32:40, :] = tail
+
+
+def smooth(ready, field, kz, inv, bj, to_core, to_near, ups, downs):
+    out = solve_lines([kz[z] for z in range(5)], [inv[z] for z in range(4)], [field[z] for z in range(4)])
+    for z in range(4):
+        bj[z] = out[z]
+    send_faces(out, to_core, to_near, ups, downs)
 
 
 def chain(ready, own, other, rhs_ref, fac, beside, ups, downs, out, mats, us, uc, ws, wc):
     odd = lax.axis_index("slab") % 2
-    lane = lane_of((32, 128))
-    low = lane < 64
-    ready(0, 1)
-    for m in range(32):
-        for j, src in ((0, own), (1, other)):
-            packed = src[m, 0:32, :]
-            at = 2 * m + (odd if j == 0 else 1 - odd)
-            mats[at, 0:32, :] = jnp.where(low, packed, 0.0)
-            mats[at, 32:64, :] = jnp.where(low, pltpu.roll(packed, 64, 1), 0.0)
+    low = lane_of((32, 128)) < 64
     cols = rhs_ref[...].T
     for k in range(1, 64, 2):
         uc[k] = jnp.broadcast_to(cols[:64, k : k + 1], (64, 128))
@@ -305,11 +313,19 @@
     us[0:1, :] = row
     col = None
     for k in range(1, 64):
+        m = k // 2
+        if m % 8 == 0:
+            ready(0, 1, pieces=(m // 8,))
+        packed = choose(odd, own[m, 0:32, :], other[m, 0:32, :])
+        if k % 2 == 0:
+            packed = choose(odd, other[m, 0:32, :], own[m, 0:32, :])
+        mat = jnp.concatenate([jnp.where(low, packed, 0.0), jnp.where(low, pltpu.roll(packed, 64, 1), 0.0)], axis=0)
+        mats[k] = mat
         if k % 2:
-            col = jnp.broadcast_to(jnp.sum(mats[k] * row, axis=1, keepdims=True), (64, 128)) + uc[k]
+            col = jnp.broadcast_to(jnp.sum(mat * row, axis=1, keepdims=True), (64, 128)) + uc[k]
             uc[k] = col
         else:
-            row = jnp.sum(mats[k] * col, axis=0, keepdims=True) + rhs_ref[k : k + 1, :]
+            row = jnp.sum(mat * col, axis=0, keepdims=True) + rhs_ref[k : k + 1, :]
             us[k : k + 1, :] = row
     ws[0:8, :] = jnp.zeros((8, 128), F32)
     wc[0] = jnp.zeros((64, 128), F32)
@@ -323,7 +339,7 @@
             col = jnp.broadcast_to(jnp.sum(mats[k] * row, axis=1, keepdims=True), (64, 128)) + uc[k - 1]
             wc[k] = col
     slab = lax.axis_index("slab")
-    ready(2, 3)
+    ready(2, 3, 4, 5, 6)
     shares = ((0, fac[...]), (-1, beside[0]), (1, beside[1]))
     for j, (shift, table) in enumerate(shares):
         at = slab + shift + 1
@@ -417,21 +433,18 @@
 
 
 def first(
-    ready, got, bj, core, near, sub, zsub, ysub, kz, ky, kyt, kx, kxe, rs, inv, cols,
-    z_out, q_out, bj_out, to_core, to_near, ups, downs, pay, rows,
+    ready, got, bj, core, near, sub, zsub, ysub, kz, ky, kyt, kx, kxe, rs, cols,
+    z_out, q_out, pay, rows,
 ):
-    ready(4, 12)
+    ready(4)
     planes, images = apply(got, bj, core, near, sub, zsub, ysub, kz, ky, kyt, kx, kxe)
     for z in range(4):
         z_out[z] = planes[z]
         q_out[z] = images[z]
+    cin = jnp.broadcast_to(restrict(sub, q_out, rows), (8, 64))
+    ready(12)
     rz = total_of([rs[z] for z in range(4)], planes)
     pq = total_of(planes, images)
-    out = solve_lines([kz[z] for z in range(5)], [inv[z] for z in range(4)], images)
-    for z in range(4):
-        bj_out[z] = out[z]
-    send_faces(out, to_core, to_near, ups, downs)
-    cin = jnp.broadcast_to(restrict(sub, q_out, rows), (8, 64))
     lane = lane_of((1, 128))
     parts = []
     for q in range(4):
@@ -447,9 +460,10 @@
     ready, got, bj, core, near, sub, zsub, ysub, kz, ky, kyt, kx, kxe, rs, z0, q0, dots,
     z_out, g_out, r_out, pay,
 ):
-    ready(4, 12)
+    ready(4)
     planes, images = apply(got, bj, core, near, sub, zsub, ysub, kz, ky, kyt, kx, kxe)
     alpha = dots[0:1, 64:65] / dots[0:1, 65:66]
+    ready(12)
     zs, gs, rr = [], [], []
     for z in range(4):
         rr.append(rs[z] - alpha * q0[z])
@@ -500,17 +514,18 @@
     )(right_side, phase_label, density_gain, subdomain, fac)
     core, near = swap(core, near)
     got = exchange(pay, "quad")
-    kz, ky, kyt, kx, kxe, inv, bj, to_core, to_near, ups, downs, zsub, ysub, cols, beside, pay = call(
+    cols, pay = call(share, (sds(4, 64, 128), sds(32, 40, 128)), (), (1, 2), (1,))(got, fac, cou)
+    pay, core, near = lax.optimization_barrier((pay, core, near))
+    own = exchange(pay, "slab", cores)
+    kz, ky, kyt, kx, kxe, inv, bj, to_core, to_near, ups, downs, zsub, ysub, beside = call(
         setup,
         (sds(5, 16, 1024), grid, edge, grid, sds(4, 16, 128), grid, grid, plane, plane, edge, edge)
-        + (jax.ShapeDtypeStruct((2, 16, 1024), jnp.int32), jax.ShapeDtypeStruct((8, 1024), jnp.int32))
-        + (sds(4, 64, 128), sds(2, 64, 256), sds(32, 40, 128)),
+        + (jax.ShapeDtypeStruct((2, 16, 1024), jnp.int32), jax.ShapeDtypeStruct((8, 1024), jnp.int32), sds(2, 64, 256)),
         (),
-        (0, 4, 5),
-        (15,),
-    )(right_side, mob, core, near, fac, cou, got)
-    bj_core, bj_near = swap(to_core, to_near)
-    own = exchange(pay, "slab", cores)
+        (0,),
+        (-10, -11),
+    )(right_side, mob, core, near, got)
+    own, bj_core, bj_near = lax.optimization_barrier((own, *swap(to_core, to_near)))
     other = lax.ppermute(own, "slab", with_core)
     work = [
         pltpu.VMEM((64, 64, 128), F32),
@@ -520,19 +535,16 @@
         pltpu.VMEM((66, 64, 128), F32),
         pltpu.VMEM((64, 128), F32),
     ]
-    part = call(chain_first, sds(4, 40, 128), work, (2,), (-1,))(own, other, fac, beside, ups, downs)
+    part = call(chain_first, sds(4, 40, 128), work, (2, 4, 5), (-1,))(own, other, fac, beside, ups, downs)
     coarse = exchange(part, "quad")
     stencil = (subdomain, zsub, ysub, kz, ky, kyt, kx, kxe, right_side)
-    z0, q0, bj1, to_core, to_near, ups, downs, pay = call(
-        first,
-        (grid, grid, grid, plane, plane, edge, edge, sds(32, 8, 128)),
-        [pltpu.VMEM((64, 128), F32)],
-        (4, 12),
-        (7,),
-    )(coarse, bj, bj_core, bj_near, *stencil, inv, cols)
+    z0, q0, pay = call(
+        first, (grid, grid, sds(32, 8, 128)), [pltpu.VMEM((64, 128), F32)], (4, 12), (2,)
+    )(coarse, bj, bj_core, bj_near, *stencil, cols)
+    everyone = exchange(pay.reshape(256, 1, 128), BOTH).reshape(256, 128)
+    bj1, to_core, to_near, ups, downs = call(smooth, (grid, plane, plane, edge, edge), (), (), (-4, -5))(q0, kz, inv)
     bj_core, bj_near = swap(to_core, to_near)
-    everyone = exchange(pay.reshape(256, 1, 128), BOTH).reshape(256, 128)
-    part, dots = call(chain_second, (sds(4, 40, 128), sds(8, 128)), work, (0, 1, 3), (-1,))(
+    part, dots = call(chain_second, (sds(4, 40, 128), sds(8, 128)), work, (0, 1, 3, 5, 6), (-1,))(
         own, other, everyone, fac, beside, ups, downs
     )
     coarse = exchange(part, "quad")

time: 144 us -> 138 us (0.958)
  blocking collectives: 48.5 us -> 30.2 us
  starting transfers between devices: 37.6 us -> 44.3 us
  waiting for transfers between devices: 22 us -> 26.8 us
    all_to_all x2, blocking collectives: 48.5 us -> 30.2 us  [exchange(): lax.all_to_all(value, axis, 0, 0, tiled=True, axis_index_groups=groups)]
    ppermute x3, waiting for transfers between devices: 3.18 us -> 11.5 us  [swap(): lax.ppermute(to_near, 'slab', with_near)]
    all_to_all x4, waiting for transfers between devices: 18.8 us -> 13.5 us  [exchange(): lax.all_to_all(value, axis, 0, 0, tiled=True, axis_index_groups=groups)]
    all_to_all x4, starting transfers between devices: 21 us -> 26.2 us  [exchange(): lax.all_to_all(value, axis, 0, 0, tiled=True, axis_index_groups=groups)]
    ppermute x3, starting transfers between devices: 3.96 us -> 5.77 us  [swap(): lax.ppermute(to_core, 'slab', with_core)]
    ppermute x1, waiting for transfers between devices: 0.01 us -> 1.72 us  [body(): other = lax.ppermute(own, 'slab', with_core)]
    pallas_call x7 -> x9, Pallas kernels: 34.7 us -> 35.4 us  [run(): pl.pallas_call(wrapped, in_specs=[hbm if i in far else vmem for i in rang...]
  transfers between devices with their start and end apart: 11 -> 11, of which waited for: 5 -> 6; matrix products, arithmetic and copies ran while one was open for 0% -> 0% of each run, Pallas kernels for 12% -> 10%
where the time goes in v4:
time: 138 us; the launch traced here: 137 us
  starting transfers between devices  44.3 us (32%)
  Pallas kernels  35.4 us (26%)
  blocking collectives  30.2 us (22%)
  waiting for transfers between devices  26.8 us (19%)
    pallas_call x9, Pallas kernels, run(): pl.pallas_call(wrapped, in_specs=[hbm if i in far else vmem for i in rang...  35.4 us
    all_to_all x2, blocking collectives, exchange(): lax.all_to_all(value, axis, 0, 0, tiled=True, axis_index_groups=groups)  30.2 us
    all_to_all x4, starting transfers between devices, exchange(): lax.all_to_all(value, axis, 0, 0, tiled=True, axis_index_groups=groups)  26.2 us
    all_to_all x4, waiting for transfers between devices, exchange(): lax.all_to_all(value, axis, 0, 0, tiled=True, axis_index_groups=groups)  13.5 us
    ppermute x3, waiting for transfers between devices, swap(): lax.ppermute(to_near, 'slab', with_near)  11.5 us
    ppermute x3, starting transfers between devices, swap(): lax.ppermute(to_near, 'slab', with_near)  7.87 us
    ppermute x3, starting transfers between devices, swap(): lax.ppermute(to_core, 'slab', with_core)  5.77 us
    ppermute x1, starting transfers between devices, body(): other = lax.ppermute(own, 'slab', with_core)  4.47 us
  transfers between devices with their start and end apart: 11, of which 6 were waited for; matrix products, arithmetic and copies ran while one was open for 0% of the time, Pallas kernels for 10%

profile of v4, /device:TPU:1, one launch (start us, length us, event | category | flops | bytes accessed | tf_op | source)
XLA Modules:
  0.0 137.5 jit_solution(3211038769288838583)
XLA Ops:
  0.6 4.9 %begin.1 = (f32[4,16,1024]{2,1,0:T(8,128)S(1)}, f32[384,128]{1,0:T(8,128)S(1)}, f32[384,128]{1,0:T(8,128)S(1)}, f32[4,128,128]{2,1,0:T(8,128)}) custom-call(f32[4,16,1024]{2,1,0:T(8,128)} %refs_12_.3, s32[4,16,1024]{2,1,0:T(8,128)} %refs_1_.1, f32[4,16,1024]{2,1,0:T(8,128)} %refs_2_.1, s32[4,16,1024]{2,1,0:T(8,128)} %refs_4_.3, f32[64,256]{1,0:T(8,128)} %bitcast.12), custom_call_target="tpu_custom_call" | custom-call | tf_op jit(solution)/shard_map/begin/pallas_call | solution.py:81
  5.5 5.0 %all-to-all-start = ((f32[4,128,128]{2,1,0:T(8,128)}), f32[4,128,128]{2,1,0:T(8,128)S(1)}, u32[]{:S(2)}, u32[]{:S(2)}) async-start(f32[4,128,128]{2,1,0:T(8,128)} %get-tuple-element.42), calls=%async_computation | async-start | bytes 524288 | tf_op jit(solution)/shard_map/all_to_all | solution.py:503
  10.5 1.7 %collective-permute-start = (f32[384,128]{1,0:T(8,128)S(1)}, f32[384,128]{1,0:T(8,128)S(1)}, u32[]{:S(2)}, u32[]{:S(2)}) collective-permute-start(f32[384,128]{1,0:T(8,128)S(1)} %get-tuple-element.44), channel_id=1, source_target_pairs={{0,4},{4,0},{8,12},{12,8},{16,20},{20,16},{24,28},{28,24},{32,36},... | collective-permute-start | bytes 589832 | tf_op jit(solution)/shard_map/ppermute | solution.py:506
  12.3 2.6 %collective-permute-start.1 = (f32[384,128]{1,0:T(8,128)S(1)}, f32[384,128]{1,0:T(8,128)S(1)}, u32[]{:S(2)}, u32[]{:S(2)}) collective-permute-start(f32[384,128]{1,0:T(8,128)S(1)} %get-tuple-element.45), channel_id=1, source_target_pairs={{4,8},{8,4},{12,16},{16,12},{20,24},{24,20},{28,32},{32,28},{36,40... | collective-permute-start | bytes 589832 | tf_op jit(solution)/shard_map/ppermute | solution.py:506
  14.9 1.1 all-to-all-done.refs_0_.refs_4_
  16.1 2.3 %share.1 = (f32[4,64,128]{2,1,0:T(8,128)S(1)}, f32[32,40,128]{2,1,0:T(8,128)}) custom-call(f32[4,128,128]{2,1,0:T(8,128)S(1)} %all-to-all-done.refs_0_.refs_4_, f32[64,256]{1,0:T(8,128)} %bitcast.13, f32[64,64]{1,0:T(8,128)} %bitcast.18), custom_call_target="tpu_custom_call" | custom-call | tf_op jit(solution)/shard_map/share/pallas_call | solution.py:81
  18.4 0.0 collective-permute-done.refs_2_
  18.4 0.8 collective-permute-done.1.refs_3_
  19.3 11.0 %all-to-all-start.1 = ((f32[32,40,128]{2,1,0:T(8,128)}), f32[32,40,128]{2,1,0:T(8,128)S(1)}, u32[]{:S(2)}, u32[]{:S(2)}) async-start(f32[32,40,128]{2,1,0:T(8,128)} %get-tuple-element.46), calls=%async_computation.1 | async-start | bytes 1310720 | tf_op jit(solution)/shard_map/all_to_all | solution.py:503
  30.3 1.7 %setup.1 = (f32[5,16,1024]{2,1,0:T(8,128)S(1)}, f32[4,16,1024]{2,1,0:T(8,128)S(1)}, f32[4,1024]{1,0:T(4,128)S(1)}, f32[4,16,1024]{2,1,0:T(8,128)S(1)}, f32[4,16,...) custom-call(f32[4,16,1024]{2,1,0:T(8,128)} %refs_12_.3, ...), custom_call_target="tpu_custom_call" | custom-call | tf_op jit(solution)/shard_map/setup/pallas_call | solution.py:81
  32.0 1.7 %collective-permute-start.2 = (f32[16,1024]{1,0:T(8,128)S(1)}, f32[16,1024]{1,0:T(8,128)S(1)}, u32[]{:S(2)}, u32[]{:S(2)}) collective-permute-start(f32[16,1024]{1,0:T(8,128)S(1)} %get-tuple-element.50), channel_id=1, source_target_pairs={{0,4},{4,0},{8,12},{12,8},{16,20},{20,16},{24,28},{28,24},{32,36},... | collective-permute-start | bytes 196616 | tf_op jit(solution)/shard_map/ppermute | solution.py:506
  33.6 3.3 %collective-permute-start.3 = (f32[16,1024]{1,0:T(8,128)S(1)}, f32[16,1024]{1,0:T(8,128)S(1)}, u32[]{:S(2)}, u32[]{:S(2)}) collective-permute-start(f32[16,1024]{1,0:T(8,128)S(1)} %get-tuple-element.51), channel_id=1, source_target_pairs={{4,8},{8,4},{12,16},{16,12},{20,24},{24,20},{28,32},{32,28},{36,40... | collective-permute-start | bytes 196616 | tf_op jit(solution)/shard_map/ppermute | solution.py:506
  37.0 0.0 collective-permute-done.2.refs_2_
  37.0 10.7 %collective-permute-done.3.refs_3_ = f32[16,1024]{1,0:T(8,128)S(1)} collective-permute-done((f32[16,1024]{1,0:T(8,128)S(1)}, f32[16,1024]{1,0:T(8,128)S(1)}, u32[]{:S(2)}, u32[]{:S(2)}) %collective-permute-start.3) | collective-permute-done | bytes 65568 | tf_op jit(solution)/shard_map/ppermute | solution.py:506
  47.7 0.0 all-to-all-done.1.refs_0_
  47.7 4.5 %collective-permute-start.4 = (f32[32,40,128]{2,1,0:T(8,128)S(1)}, f32[32,40,128]{2,1,0:T(8,128)S(1)}, u32[]{:S(2)}, u32[]{:S(2)}) collective-permute-start(f32[32,40,128]{2,1,0:T(8,128)S(1)} %all-to-all-done.1.refs_0_), channel_id=1, source_target_pairs={{0,4},{4,0},{8,12},{12,8},{16,20},{20,16},{24,28},{28,24},{32,36},... | collective-permute-start | bytes 1966088 | tf_op jit(solution)/shard_map/ppermute | solution.py:529
  52.1 1.7 %collective-permute-done.4.refs_1_ = f32[32,40,128]{2,1,0:T(8,128)S(1)} collective-permute-done((f32[32,40,128]{2,1,0:T(8,128)S(1)}, f32[32,40,128]{2,1,0:T(8,128)S(1)}, u32[]{:S(2)}, u32[]{:S(2)}) %collective-permute-start.4) | collective-permute-done | bytes 655392 | tf_op jit(solution)/shard_map/ppermute | solution.py:529
  53.9 7.2 %chain_first.1 = f32[4,40,128]{2,1,0:T(8,128)} custom-call(f32[32,40,128]{2,1,0:T(8,128)S(1)} %all-to-all-done.1.refs_0_, f32[32,40,128]{2,1,0:T(8,128)S(1)} %collective-permute-done.4.refs_1_, f32[64,256]{1,0:T(8,128)} %bitcast.14, f32[2,64,256]{2,1,0:T(8,128)S(1)} %get-tuple-element.53.refs_3_.refs_4_, f32[4,1024]{1,0:T(4,128)} %get-tuple-element.54.refs_4_, ...), custom_call_target="tpu_custom_call" | custom-call | tf_op jit(solution)/shard_map/chain_first/pallas_call | solution.py:81
  61.1 9.7 %all_to_all.30.refs_0_ = f32[4,40,128]{2,1,0:T(8,128)S(1)} all-to-all(f32[4,40,128]{2,1,0:T(8,128)} %chain_first.1), channel_id=1, replica_groups=mesh['slab'=64,'quad'=4] {'quad'}, dimensions={0} | all-to-all | bytes 163840 | tf_op jit(solution)/shard_map/all_to_all | solution.py:503
  70.7 5.8 %first.1 = (f32[4,16,1024]{2,1,0:T(8,128)S(1)}, f32[4,16,1024]{2,1,0:T(8,128)S(1)}, f32[32,8,128]{2,1,0:T(8,128)}) custom-call(f32[4,40,128]{2,1,0:T(8,128)S(1)} %all_to_all.30.refs_0_, f32[4,16,1024]{2,1,0:T(8,128)S(1)} %get-tuple-element.56.refs_1_, f32[16,1024]{1,0:T(8,128)S(1)} %collective-permute-done.2.refs_2_, ...), custom_call_target="tpu_custom_call" | custom-call | tf_op jit(solution)/shard_map/first/pallas_call | solution.py:81
  76.6 6.8 %all-to-all-start.3 = ((f32[256,1,128]{2,1,0:T(1,128)}), f32[256,1,128]{2,1,0:T(1,128)S(1)}, u32[]{:S(2)}, u32[]{:S(2)}) async-start(f32[256,1,128]{2,1,0:T(1,128)} %bitcast.16), calls=%async_computation.3 | async-start | bytes 262144 | tf_op jit(solution)/shard_map/all_to_all | solution.py:503
  83.4 0.7 smooth.1
  84.1 2.4 %collective-permute-start.5 = (f32[16,1024]{1,0:T(8,128)S(1)}, f32[16,1024]{1,0:T(8,128)S(1)}, u32[]{:S(2)}, u32[]{:S(2)}) collective-permute-start(f32[16,1024]{1,0:T(8,128)S(1)} %get-tuple-element.74), channel_id=1, source_target_pairs={{0,4},{4,0},{8,12},{12,8},{16,20},{20,16},{24,28},{28,24},{32,36},... | collective-permute-start | bytes 196616 | tf_op jit(solution)/shard_map/ppermute | solution.py:506
  86.5 1.9 %collective-permute-start.6 = (f32[16,1024]{1,0:T(8,128)S(1)}, f32[16,1024]{1,0:T(8,128)S(1)}, u32[]{:S(2)}, u32[]{:S(2)}) collective-permute-start(f32[16,1024]{1,0:T(8,128)S(1)} %get-tuple-element.75), channel_id=1, source_target_pairs={{4,8},{8,4},{12,16},{16,12},{20,24},{24,20},{28,32},{32,28},{36,40... | collective-permute-start | bytes 196616 | tf_op jit(solution)/shard_map/ppermute | solution.py:506
  88.4 7.9 %all-to-all-done.3 = f32[256,1,128]{2,1,0:T(1,128)S(1)} async-done(((f32[256,1,128]{2,1,0:T(1,128)}), f32[256,1,128]{2,1,0:T(1,128)S(1)}, u32[]{:S(2)}, u32[]{:S(2)}) %all-to-all-start.3) | async-done | bytes 131104 | tf_op jit(solution)/shard_map/all_to_all | solution.py:503
  96.3 8.7 %chain_second.1 = (f32[4,40,128]{2,1,0:T(8,128)}, f32[8,128]{1,0:T(8,128)S(1)}) custom-call(f32[32,40,128]{2,1,0:T(8,128)} %copy-done, f32[32,40,128]{2,1,0:T(8,128)} %copy-done.1, f32[256,128]{1,0:T(8,128)S(1)} %bitcast.10, f32[64,256]{1,0:T(8,128)} %bitcast.15, f32[2,64,256]{2,1,0:T(8,128)S(1)} %get-tuple-element.53.refs_3_.refs_4_, ...), custom_call_target="tpu_custom_call" | custom-call | tf_op jit(solution)/shard_map/chain_second/pallas_call | solution.py:81
  104.9 3.3 %all-to-all-start.4 = ((f32[4,40,128]{2,1,0:T(8,128)}), f32[4,40,128]{2,1,0:T(8,128)S(1)}, u32[]{:S(2)}, u32[]{:S(2)}) async-start(f32[4,40,128]{2,1,0:T(8,128)} %get-tuple-element.72), calls=%async_computation.4 | async-start | bytes 163840 | tf_op jit(solution)/shard_map/all_to_all | solution.py:503
  108.3 0.0 collective-permute-done.5.refs_2_
  108.3 4.5 %all-to-all-done.4.refs_0_ = f32[4,40,128]{2,1,0:T(8,128)S(1)} async-done(((f32[4,40,128]{2,1,0:T(8,128)}), f32[4,40,128]{2,1,0:T(8,128)S(1)}, u32[]{:S(2)}, u32[]{:S(2)}) %all-to-all-start.4) | async-done | bytes 81952 | tf_op jit(solution)/shard_map/all_to_all | solution.py:503
  112.8 3.0 %second.1 = (f32[4,16,1024]{2,1,0:T(8,128)S(1)}, f32[4,16,1024]{2,1,0:T(8,128)S(1)}, f32[4,16,1024]{2,1,0:T(8,128)S(1)}, f32[32,8,128]{2,1,0:T(8,128)}) custom-call(f32[4,40,128]{2,1,0:T(8,128)S(1)} %all-to-all-done.4.refs_0_, f32[4,16,1024]{2,1,0:T(8,128)S(1)} %get-tuple-element.73.refs_1_, f32[16,1024]{1,0:T(8,128)S(1)} %collective-permute-done.5.refs_2_, ...), custom_call_target="tpu_custom_call" | custom-call | tf_op jit(solution)/shard_map/second/pallas_call | solution.py:81
  115.8 20.5 %all_to_all.31 = f32[256,1,128]{2,1,0:T(1,128)S(1)} all-to-all(f32[256,1,128]{2,1,0:T(1,128)} %bitcast.17), channel_id=1, replica_groups=mesh['slab'=64,'quad'=4] {'slab','quad'}, dimensions={0} | all-to-all | bytes 262144 | tf_op jit(solution)/shard_map/all_to_all | solution.py:503
  136.3 1.1 last.1
  (5 shorter events, 0.0 us)
Async XLA Ops:
  5.5 10.6 %all-to-all-start = ((f32[4,128,128]{2,1,0:T(8,128)}), f32[4,128,128]{2,1,0:T(8,128)S(1)}, u32[]{:S(2)}, u32[]{:S(2)}) async-start(f32[4,128,128]{2,1,0:T(8,128)} %get-tuple-element.42), calls=%async_computation | async-start | bytes 524288 | tf_op jit(solution)/shard_map/all_to_all | solution.py:503
  10.5 7.9 %collective-permute-start = (f32[384,128]{1,0:T(8,128)S(1)}, f32[384,128]{1,0:T(8,128)S(1)}, u32[]{:S(2)}, u32[]{:S(2)}) collective-permute-start(f32[384,128]{1,0:T(8,128)S(1)} %get-tuple-element.44), channel_id=1, source_target_pairs={{0,4},{4,0},{8,12},{12,8},{16,20},{20,16},{24,28},{28,24},{32,36},... | collective-permute-start | bytes 589832 | tf_op jit(solution)/shard_map/ppermute | solution.py:506
  12.3 7.0 %collective-permute-start.1 = (f32[384,128]{1,0:T(8,128)S(1)}, f32[384,128]{1,0:T(8,128)S(1)}, u32[]{:S(2)}, u32[]{:S(2)}) collective-permute-start(f32[384,128]{1,0:T(8,128)S(1)} %get-tuple-element.45), channel_id=1, source_target_pairs={{4,8},{8,4},{12,16},{16,12},{20,24},{24,20},{28,32},{32,28},{36,40... | collective-permute-start | bytes 589832 | tf_op jit(solution)/shard_map/ppermute | solution.py:506
  19.3 28.4 %all-to-all-start.1 = ((f32[32,40,128]{2,1,0:T(8,128)}), f32[32,40,128]{2,1,0:T(8,128)S(1)}, u32[]{:S(2)}, u32[]{:S(2)}) async-start(f32[32,40,128]{2,1,0:T(8,128)} %get-tuple-element.46), calls=%async_computation.1 | async-start | bytes 1310720 | tf_op jit(solution)/shard_map/all_to_all | solution.py:503
  32.0 5.0 %collective-permute-start.2 = (f32[16,1024]{1,0:T(8,128)S(1)}, f32[16,1024]{1,0:T(8,128)S(1)}, u32[]{:S(2)}, u32[]{:S(2)}) collective-permute-start(f32[16,1024]{1,0:T(8,128)S(1)} %get-tuple-element.50), channel_id=1, source_target_pairs={{0,4},{4,0},{8,12},{12,8},{16,20},{20,16},{24,28},{28,24},{32,36},... | collective-permute-start | bytes 196616 | tf_op jit(solution)/shard_map/ppermute | solution.py:506
  33.6 14.0 %collective-permute-start.3 = (f32[16,1024]{1,0:T(8,128)S(1)}, f32[16,1024]{1,0:T(8,128)S(1)}, u32[]{:S(2)}, u32[]{:S(2)}) collective-permute-start(f32[16,1024]{1,0:T(8,128)S(1)} %get-tuple-element.51), channel_id=1, source_target_pairs={{4,8},{8,4},{12,16},{16,12},{20,24},{24,20},{28,32},{32,28},{36,40... | collective-permute-start | bytes 196616 | tf_op jit(solution)/shard_map/ppermute | solution.py:506
  47.7 13.4 %copy-start = (f32[32,40,128]{2,1,0:T(8,128)}, f32[32,40,128]{2,1,0:T(8,128)S(1)}, u32[]{:S(2)}) copy-start(f32[32,40,128]{2,1,0:T(8,128)S(1)} %all-to-all-done.1.refs_0_) | copy-start | bytes 1966084
  47.7 6.2 %collective-permute-start.4 = (f32[32,40,128]{2,1,0:T(8,128)S(1)}, f32[32,40,128]{2,1,0:T(8,128)S(1)}, u32[]{:S(2)}, u32[]{:S(2)}) collective-permute-start(f32[32,40,128]{2,1,0:T(8,128)S(1)} %all-to-all-done.1.refs_0_), channel_id=1, source_target_pairs={{0,4},{4,0},{8,12},{12,8},{16,20},{20,16},{24,28},{28,24},{32,36},... | collective-permute-start | bytes 1966088 | tf_op jit(solution)/shard_map/ppermute | solution.py:529
  53.9 7.2 %copy-start.1 = (f32[32,40,128]{2,1,0:T(8,128)}, f32[32,40,128]{2,1,0:T(8,128)S(1)}, u32[]{:S(2)}) copy-start(f32[32,40,128]{2,1,0:T(8,128)S(1)} %collective-permute-done.4.refs_1_) | copy-start | bytes 1966084
  76.6 19.7 %all-to-all-start.3 = ((f32[256,1,128]{2,1,0:T(1,128)}), f32[256,1,128]{2,1,0:T(1,128)S(1)}, u32[]{:S(2)}, u32[]{:S(2)}) async-start(f32[256,1,128]{2,1,0:T(1,128)} %bitcast.16), calls=%async_computation.3 | async-start | bytes 262144 | tf_op jit(solution)/shard_map/all_to_all | solution.py:503
  84.1 24.2 %collective-permute-start.5 = (f32[16,1024]{1,0:T(8,128)S(1)}, f32[16,1024]{1,0:T(8,128)S(1)}, u32[]{:S(2)}, u32[]{:S(2)}) collective-permute-start(f32[16,1024]{1,0:T(8,128)S(1)} %get-tuple-element.74), channel_id=1, source_target_pairs={{0,4},{4,0},{8,12},{12,8},{16,20},{20,16},{24,28},{28,24},{32,36},... | collective-permute-start | bytes 196616 | tf_op jit(solution)/shard_map/ppermute | solution.py:506
  86.5 21.8 %collective-permute-start.6 = (f32[16,1024]{1,0:T(8,128)S(1)}, f32[16,1024]{1,0:T(8,128)S(1)}, u32[]{:S(2)}, u32[]{:S(2)}) collective-permute-start(f32[16,1024]{1,0:T(8,128)S(1)} %get-tuple-element.75), channel_id=1, source_target_pairs={{4,8},{8,4},{12,16},{16,12},{20,24},{24,20},{28,32},{32,28},{36,40... | collective-permute-start | bytes 196616 | tf_op jit(solution)/shard_map/ppermute | solution.py:506
  104.9 7.8 %all-to-all-start.4 = ((f32[4,40,128]{2,1,0:T(8,128)}), f32[4,40,128]{2,1,0:T(8,128)S(1)}, u32[]{:S(2)}, u32[]{:S(2)}) async-start(f32[4,40,128]{2,1,0:T(8,128)} %get-tuple-element.72), calls=%async_computation.4 | async-start | bytes 163840 | tf_op jit(solution)/shard_map/all_to_all | solution.py:503

commit v5 on v4

--- a/solution.py
+++ b/solution.py
@@ -9,6 +9,8 @@
 HIGH = lax.Precision.HIGHEST
 BOTH = ("slab", "quad")
 PIECES = 4
+GROUP = 16
+SCALE = 2.0**-30
 
 
 def sds(*shape):
@@ -122,7 +124,7 @@
     return lax.broadcasted_iota(jnp.int32, shape, len(shape) - 1)
 
 
-def restrict(sub_ref, field_ref, rows_ref):
+def restrict(sub_ref, field_ref, rows_ref, least=0):
     def group(g, unused):
         def tile(t, totals):
             rows = pl.ds(pl.multiple_of((t % 2) * 8, 8), 8)
@@ -130,7 +132,7 @@
             field = field_ref[t // 2, rows, :]
             out = []
             for label in range(8):
-                picked = jnp.where(sub == g * 8 + label, field, 0.0)
+                picked = jnp.where(sub == g * 8 + (label + least), field, 0.0)
                 total = totals[label]
                 for j in range(8):
                     total = total + picked[:, j * 128 : (j + 1) * 128]
@@ -191,11 +193,15 @@
     return choose((lax.axis_index("quad") + 1 == dest).astype(jnp.int32), upward, downward)
 
 
-def begin(ready, rs, ph, gain, sub, fac, mob, core, near, pay, rows):
+def begin(ready, rs, ph, gain, sub, fac, cou, mob, core, near, rs_out, sub_out, fac_out, cou_out, pay, rows):
     odd = parity()
     ready(0, 3)
     cin = restrict(sub, rs, rows)
-    ready(1, 2, 4)
+    rs_out[...] = rs[...]
+    sub_out[...] = sub[...] + 1
+    ready(1, 2, 4, 5)
+    fac_out[...] = fac[...]
+    cou_out[...] = pack(choose(odd, cou[...], cou[...].T))
     ms, ss = [], []
     for z in range(4):
         m = 1.0 / (gain[z] * (0.001 + 0.999 * ph[z].astype(F32)))
@@ -233,22 +239,20 @@
 
 
 def share(ready, got, fac, cou, cols, pay):
-    for q in range(4):
-        cols[q] = got[q, 0:64, :]
+    low = lane_of((64, 128)) < 64
+    for h in range(2):
+        cols[h] = jnp.where(low, got[2 * h, 0:64, :], pltpu.roll(got[2 * h + 1, 0:64, :], 64, 1))
     cins = [pltpu.roll(got[q, 0:8, :], 64, 1)[0:1, :64] for q in range(4)]
     cin = jnp.concatenate(cins, axis=1)
-    ready(1)
     rhs = lax.dot_general(
         jnp.broadcast_to(cin, (8, 256)), fac[...], (((1,), (1,)), ((), ())), precision=HIGH, preferred_element_type=F32
     )
-    ready(2)
-    mat = choose(parity(), cou[...], cou[...].T)
-    pay[0:32, :] = jnp.concatenate([mat[:32, :], mat[32:, :]], axis=1)
+    pay[0:32, :] = cou[...]
     pay[32:40, :] = jnp.concatenate([rhs, rhs], axis=1)
 
 
 def setup(
-    ready, rs, mob, core, near, got, kz, ky, kyt, kx, kxe, inv, bj, to_core, to_near, ups, downs, zsub, ysub, beside
+    ready, rs, mob, core, near, got, kz, ky, kyt, kx, kxe, inv, to_core, to_near, ups, downs, zsub, ysub, beside
 ):
     odd = parity()
     quad = lax.axis_index("quad")
@@ -291,62 +295,176 @@
         inv[j] = invs[j]
     ready(0)
     out = solve_lines(faces, invs, [rs[z] for z in range(4)])
-    for z in range(4):
-        bj[z] = out[z]
     send_faces(out, to_core, to_near, ups, downs)
 
 
-def smooth(ready, field, kz, inv, bj, to_core, to_near, ups, downs):
+def smooth(ready, field, kz, inv, to_core, to_near, ups, downs):
     out = solve_lines([kz[z] for z in range(5)], [inv[z] for z in range(4)], [field[z] for z in range(4)])
-    for z in range(4):
-        bj[z] = out[z]
     send_faces(out, to_core, to_near, ups, downs)
 
 
-def chain(ready, own, other, rhs_ref, fac, beside, ups, downs, out, mats, us, uc, ws, wc):
-    odd = lax.axis_index("slab") % 2
+def unpack(packed):
     low = lane_of((32, 128)) < 64
-    cols = rhs_ref[...].T
-    for k in range(1, 64, 2):
-        uc[k] = jnp.broadcast_to(cols[:64, k : k + 1], (64, 128))
-    row = rhs_ref[0:1, :]
-    us[0:1, :] = row
+    return jnp.concatenate([jnp.where(low, packed, 0.0), jnp.where(low, pltpu.roll(packed, 64, 1), 0.0)], axis=0)
+
+
+def pack(mat):
+    return jnp.concatenate([mat[:32, :64], mat[32:, :64]], axis=1)
+
+
+def across(mat, row):
+    return jnp.broadcast_to(jnp.sum(mat * row, axis=1, keepdims=True), (64, 128))
+
+
+def down(mat, col):
+    return jnp.sum(mat * col, axis=0, keepdims=True)
+
+
+def as_col(rows_t, k):
+    return jnp.broadcast_to(rows_t[:64, k : k + 1], (64, 128))
+
+
+def condense(mats, rhs):
+    rows_t = rhs.T
+    held = {}
+    col = as_col(rows_t, 1)
+    held[1] = col
+    row = None
+    for k in range(2, GROUP):
+        if k % 2:
+            col = across(mats[k], row) + as_col(rows_t, k)
+            held[k] = col
+        else:
+            row = down(mats[k], col) + rhs[k : k + 1, :]
+            held[k] = row
+    end = col
+    for k in range(GROUP - 1, 0, -1):
+        if k % 2:
+            row = down(mats[k], col)
+            if k > 1:
+                row = row + held[k - 1]
+        else:
+            col = across(mats[k], row) + held[k - 1]
+    return jnp.concatenate([end.T[0:1, :], jnp.zeros((1, 64), F32)], axis=1), row
+
+
+def of_slab(own, other, k, rows):
+    at_even, at_odd = (other, own) if k % 2 else (own, other)
+    return choose(parity(), at_odd[k // 2, rows, :], at_even[k // 2, rows, :])
+
+
+def local_mats(own, other, mats):
+    for k in range(GROUP):
+        mats[k] = unpack(of_slab(own, other, k, slice(0, 32)))
+
+
+def condense_first(ready, own, other, out, rhs_out, mats, tall):
+    rows = [of_slab(own, other, k, slice(32, 33)) for k in range(GROUP)]
+    rhs = jnp.where(lane_of((GROUP, 128)) < 64, jnp.concatenate(rows, axis=0), 0.0)
+    rhs_out[...] = rhs
+    local_mats(own, other, mats)
+    eye = lax.broadcasted_iota(jnp.int32, (64, 64), 0) == lax.broadcasted_iota(jnp.int32, (64, 64), 1)
+    one = jnp.where(eye, 1.0, 0.0)
+    runs = [[mats[b][:, :64] if b else one] for b in range(0, GROUP, 4)]
+    for k in range(1, 4):
+        for b, run in enumerate(runs):
+            mat = mats[4 * b + k][:, :64]
+            dims = (((1,), (1 if k % 2 else 0,)), ((), ()))
+            run.append(lax.dot_general(run[-1], mat, dims, precision=HIGH, preferred_element_type=F32))
+    psi = one * SCALE
+    for b, run in enumerate(runs):
+        wide = jnp.concatenate(run, axis=1)
+        wide = wide * SCALE if b == 0 else jnp.dot(psi, wide, precision=HIGH, preferred_element_type=F32)
+        tall[:, b * 256 : (b + 1) * 256] = wide
+        psi = wide[:, 192:]
+    gram = lax.dot_general(
+        tall[...], tall[...], (((1,), (1,)), ((), ())), precision=HIGH, preferred_element_type=F32
+    )
+    end, start = condense(mats, rhs)
+    out[0:32, :] = pack(psi.T * (1.0 / SCALE))
+    out[32:64, :] = of_slab(own, other, 0, slice(0, 32))
+    out[64:96, :] = pack(gram)
+    out[96:104, :] = jnp.concatenate([end, start, rhs[0:1, :], jnp.zeros((5, 128), F32)], axis=0)
+
+
+def condense_second(ready, got, own, other, out, rhs_out, mats):
+    local_mats(own, other, mats)
+    total = got[pl.ds(0, GROUP, 4), :]
+    for q in range(1, 4):
+        total = total + got[pl.ds(q, GROUP, 4), :]
+    rhs = jnp.where(lane_of((GROUP, 128)) < 64, total, 0.0)
+    rhs_out[...] = rhs
+    end, start = condense(mats, rhs)
+    dots = jnp.sum(total, axis=0, keepdims=True)
+    out[...] = jnp.concatenate([end, start, rhs[0:1, :], dots, jnp.zeros((4, 128), F32)], axis=0)
+
+
+def chain(ready, bounds, vecs, mats, rhs, fac, beside, ups, downs, out, ys, vs, wb, ws, wc):
+    slab = lax.axis_index("slab")
+    group, place = slab // GROUP, slab % GROUP
+    groups = 4
+    psi = [unpack(bounds[g, 0:32, :]) for g in range(groups)]
+    lead = [unpack(bounds[g, 32:64, :]) for g in range(groups)]
+    ends_t = jnp.concatenate([v[0:1, :] for v in vecs] + [jnp.zeros((4, 128), F32)], axis=0).T
+    ends = [as_col(ends_t, g) for g in range(groups)]
+    starts = []
+    lasts = []
+    for g in range(groups):
+        begins = jnp.where(lane_of((1, 128)) < 64, vecs[g][2:3, :], 0.0)
+        if g:
+            begins = begins + down(lead[g], lasts[g - 1])
+        starts.append(begins)
+        ys[g : g + 1, :] = begins
+        lasts.append(across(psi[g], begins) + ends[g])
+    grown = []
+    for g in range(groups):
+        packed = bounds[g, 64:96, :]
+        gram = jnp.concatenate([packed[:, :64], packed[:, 64:]], axis=0)
+        part = jnp.dot(
+            jnp.broadcast_to(starts[g][:, :64], (8, 64)), gram, precision=HIGH, preferred_element_type=F32
+        )[0:1, :]
+        part = part * (1.0 / SCALE) * (1.0 / SCALE)
+        grown.append(jnp.concatenate([part, jnp.zeros((1, 64), F32)], axis=1) + vecs[g][1:2, :])
+    vs[...] = jnp.zeros((8, 128), F32)
+    wb[0] = jnp.zeros((64, 128), F32)
+    wb[groups] = lasts[groups - 1]
+    head = grown[groups - 1]
+    vs[groups - 1 : groups, :] = head
+    for g in range(groups - 2, -1, -1):
+        back = across(lead[g + 1], head)
+        wb[g + 1] = lasts[g] + back
+        head = grown[g] + down(psi[g], back)
+        vs[g : g + 1, :] = head
+    rows_t = rhs[...].T
+    row = ys[pl.ds(group, 1), :]
+    held = {0: row}
     col = None
-    for k in range(1, 64):
-        m = k // 2
-        if m % 8 == 0:
-            ready(0, 1, pieces=(m // 8,))
-        packed = choose(odd, own[m, 0:32, :], other[m, 0:32, :])
-        if k % 2 == 0:
-            packed = choose(odd, other[m, 0:32, :], own[m, 0:32, :])
-        mat = jnp.concatenate([jnp.where(low, packed, 0.0), jnp.where(low, pltpu.roll(packed, 64, 1), 0.0)], axis=0)
-        mats[k] = mat
+    for k in range(1, GROUP):
         if k % 2:
-            col = jnp.broadcast_to(jnp.sum(mat * row, axis=1, keepdims=True), (64, 128)) + uc[k]
-            uc[k] = col
+            col = across(mats[k], row) + as_col(rows_t, k)
+            held[k] = col
         else:
-            row = jnp.sum(mat * col, axis=0, keepdims=True) + rhs_ref[k : k + 1, :]
-            us[k : k + 1, :] = row
-    ws[0:8, :] = jnp.zeros((8, 128), F32)
-    wc[0] = jnp.zeros((64, 128), F32)
-    wc[65] = jnp.zeros((64, 128), F32)
-    wc[64] = col
-    for k in range(63, 0, -1):
+            row = down(mats[k], col) + rhs[k : k + 1, :]
+            held[k] = row
+    wc[0] = wb[group]
+    col = wb[group + 1]
+    wc[GROUP] = col
+    ws[GROUP + 1 : GROUP + 2, :] = vs[pl.ds(group + 1, 1), :]
+    for k in range(GROUP - 1, 0, -1):
         if k % 2:
-            row = jnp.sum(mats[k] * col, axis=0, keepdims=True) + us[k - 1 : k, :]
+            row = down(mats[k], col) + held[k - 1]
             ws[k : k + 1, :] = row
         else:
-            col = jnp.broadcast_to(jnp.sum(mats[k] * row, axis=1, keepdims=True), (64, 128)) + uc[k - 1]
+            col = across(mats[k], row) + held[k - 1]
             wc[k] = col
-    slab = lax.axis_index("slab")
-    ready(2, 3, 4, 5, 6)
+    ready(*range(len(vecs) + 10))
     shares = ((0, fac[...]), (-1, beside[0]), (1, beside[1]))
     for j, (shift, table) in enumerate(shares):
-        at = slab + shift + 1
-        from_row = ws[pl.ds(jnp.minimum(at, 63), 1), :]
+        at = place + shift + 1
+        from_row = ws[pl.ds(at, 1), :]
         from_col = wc[at].T[0:1, :]
         is_row = jnp.broadcast_to(at % 2, (1, 64)) == 1
-        w = jnp.where(is_row, from_row[:, :64], from_col)
+        w = jnp.where(is_row, from_row[:, :64], from_col[:, :64])
         part = jnp.dot(jnp.broadcast_to(w, (8, 64)), table, precision=HIGH, preferred_element_type=F32)
         for q in range(4):
             out[q, 2 * j : 2 * j + 1, :] = part[0:1, :128]
@@ -356,23 +474,18 @@
         spread(out.at[q], 8, face_for(q, ups[...], downs[...]))
 
 
-def chain_first(ready, own, other, fac, beside, ups, downs, out, mats, us, uc, ws, wc, rhs):
-    odd = lax.axis_index("slab") % 2
-    lane = lane_of((1, 128))
-    for m in range(32):
-        for j, src in ((0, own), (1, other)):
-            at = 2 * m + (odd if j == 0 else 1 - odd)
-            rhs[pl.ds(at, 1), :] = jnp.where(lane < 64, src[m, 32:33, :], 0.0)
-    chain(ready, own, other, rhs, fac, beside, ups, downs, out, mats, us, uc, ws, wc)
-
-
-def chain_second(ready, own, other, got, fac, beside, ups, downs, out, dots, mats, us, uc, ws, wc, rhs):
-    total = got[pl.ds(0, 64, 4), :]
-    for q in range(1, 4):
-        total = total + got[pl.ds(q, 64, 4), :]
-    rhs[...] = jnp.where(lane_of((64, 128)) < 64, total, 0.0)
-    dots[...] = jnp.broadcast_to(jnp.sum(total, axis=0, keepdims=True), (8, 128))
-    chain(ready, own, other, rhs, fac, beside, ups, downs, out, mats, us, uc, ws, wc)
+def chain_first(ready, bounds, own, other, rhs, fac, beside, ups, downs, out, mats, *work):
+    local_mats(own, other, mats)
+    vecs = [bounds[g, 96:104, :] for g in range(4)]
+    chain(ready, bounds, vecs, mats, rhs, fac, beside, ups, downs, out, *work)
+
+
+def chain_second(ready, bounds, got, own, other, rhs, fac, beside, ups, downs, out, dots, mats, *work):
+    local_mats(own, other, mats)
+    vecs = [got[g] for g in range(4)]
+    total = vecs[0][3:4, :] + vecs[1][3:4, :] + vecs[2][3:4, :] + vecs[3][3:4, :]
+    dots[...] = jnp.broadcast_to(total, (8, 128))
+    chain(ready, bounds, vecs, mats, rhs, fac, beside, ups, downs, out, *work)
 
 
 def tables(got):
@@ -400,11 +513,12 @@
     )
 
 
-def apply(got, bj, core, near, sub, zsub, ysub, kz, ky, kyt, kx, kxe):
+def apply(got, field, core, near, sub, zsub, ysub, kz, ky, kyt, kx, kxe, inv):
     odd = parity()
     quad = lax.axis_index("quad")
     own, t_yl, t_yh, t_zl, t_zh = tables(got)
-    planes = [bj[z] + look_up(own, sub[z] + 1) for z in range(4)]
+    bj = solve_lines([kz[z] for z in range(5)], [inv[z] for z in range(4)], [field[z] for z in range(4)])
+    planes = [bj[z] + look_up(own, sub[z]) for z in range(4)]
     below = choose(odd, core[...], near[...]) + look_up(t_zl, zsub[0])
     above = choose(odd, near[...], core[...]) + look_up(t_zh, zsub[1])
     before = gather_rows(got[jnp.maximum(quad - 1, 0)], 8, 4)
@@ -433,15 +547,15 @@
 
 
 def first(
-    ready, got, bj, core, near, sub, zsub, ysub, kz, ky, kyt, kx, kxe, rs, cols,
+    ready, got, core, near, sub, zsub, ysub, kz, ky, kyt, kx, kxe, inv, rs, cols,
     z_out, q_out, pay, rows,
 ):
     ready(4)
-    planes, images = apply(got, bj, core, near, sub, zsub, ysub, kz, ky, kyt, kx, kxe)
+    planes, images = apply(got, rs, core, near, sub, zsub, ysub, kz, ky, kyt, kx, kxe, inv)
     for z in range(4):
         z_out[z] = planes[z]
         q_out[z] = images[z]
-    cin = jnp.broadcast_to(restrict(sub, q_out, rows), (8, 64))
+    cin = jnp.broadcast_to(restrict(sub, q_out, rows, 1), (8, 64))
     ready(12)
     rz = total_of([rs[z] for z in range(4)], planes)
     pq = total_of(planes, images)
@@ -449,7 +563,7 @@
     parts = []
     for q in range(4):
         part = lax.dot_general(
-            cin, cols[q, 0:64, :64], (((1,), (1,)), ((), ())), precision=HIGH, preferred_element_type=F32
+            cin, cols[q // 2][:, q % 2 * 64 : q % 2 * 64 + 64], (((1,), (1,)), ((), ())), precision=HIGH, preferred_element_type=F32
         )[0:1, :]
         part = jnp.concatenate([part, part], axis=1)
         parts.append(jnp.where(lane < 64, part, jnp.where(lane == 64, rz, jnp.where(lane == 65, pq, 0.0))))
@@ -457,11 +571,11 @@
 
 
 def second(
-    ready, got, bj, core, near, sub, zsub, ysub, kz, ky, kyt, kx, kxe, rs, z0, q0, dots,
+    ready, got, core, near, sub, zsub, ysub, kz, ky, kyt, kx, kxe, inv, rs, z0, q0, dots,
     z_out, g_out, r_out, pay,
 ):
     ready(4)
-    planes, images = apply(got, bj, core, near, sub, zsub, ysub, kz, ky, kyt, kx, kxe)
+    planes, images = apply(got, q0, core, near, sub, zsub, ysub, kz, ky, kyt, kx, kxe, inv)
     alpha = dots[0:1, 64:65] / dots[0:1, 65:66]
     ready(12)
     zs, gs, rr = [], [], []
@@ -495,7 +609,10 @@
     slabs = lax.axis_size("slab")
     fac, cou = block_factor[0], coupling[0]
     grid, plane, edge = sds(4, 16, 1024), sds(16, 1024), sds(4, 1024)
-    cores = [[i for i in range(slabs) if i % 2 == c] for c in range(2)]
+    quads = lax.axis_size("quad")
+    within = [list(range(g + c, g + GROUP, 2)) for g in range(0, slabs, GROUP) for c in range(2)]
+    planes = [list(range(g, g + GROUP * quads)) for g in range(0, slabs * quads, GROUP * quads)]
+    between = [list(range(i, slabs, GROUP)) for i in range(GROUP)]
     with_core = [(i, i ^ 1) for i in range(slabs)]
     with_near = [(i, i + 1 if i % 2 else i - 1) for i in range(1, slabs - 1)]
 
@@ -505,51 +622,68 @@
     def swap(to_core, to_near):
         return lax.ppermute(to_core, "slab", with_core), lax.ppermute(to_near, "slab", with_near)
 
-    mob, core, near, pay = call(
+    mob, core, near, rs, sub, fac, cou, pay = call(
         begin,
-        (grid, sds(384, 128), sds(384, 128), sds(4, 128, 128)),
+        (grid, sds(384, 128), sds(384, 128), grid, jax.ShapeDtypeStruct((4, 16, 1024), jnp.int32))
+        + (sds(64, 256), sds(32, 128), sds(4, 128, 128)),
         [pltpu.VMEM((64, 128), F32)],
-        (0, 1, 2, 3, 4),
-        (-4,),
-    )(right_side, phase_label, density_gain, subdomain, fac)
+        (3, 0, 1, 2, 4, 5),
+        (-8,),
+    )(right_side, phase_label, density_gain, subdomain, fac, cou)
     core, near = swap(core, near)
     got = exchange(pay, "quad")
-    cols, pay = call(share, (sds(4, 64, 128), sds(32, 40, 128)), (), (1, 2), (1,))(got, fac, cou)
+    cols, pay = call(share, (sds(2, 64, 128), sds(GROUP // 2, 40, 128)), (), (), (1,))(got, fac, cou)
     pay, core, near = lax.optimization_barrier((pay, core, near))
-    own = exchange(pay, "slab", cores)
-    kz, ky, kyt, kx, kxe, inv, bj, to_core, to_near, ups, downs, zsub, ysub, beside = call(
+    own = exchange(pay, "slab", within)
+    kz, ky, kyt, kx, kxe, inv, to_core, to_near, ups, downs, zsub, ysub, beside = call(
         setup,
-        (sds(5, 16, 1024), grid, edge, grid, sds(4, 16, 128), grid, grid, plane, plane, edge, edge)
+        (sds(5, 16, 1024), grid, edge, grid, sds(4, 16, 128), grid, plane, plane, edge, edge)
         + (jax.ShapeDtypeStruct((2, 16, 1024), jnp.int32), jax.ShapeDtypeStruct((8, 1024), jnp.int32), sds(2, 64, 256)),
         (),
+        (),
+        (-9, -10),
+    )(rs, mob, core, near, got)
+    own, to_core, to_near = lax.optimization_barrier((own, to_core, to_near))
+    other = lax.ppermute(own, "slab", with_core)
+    mats = pltpu.VMEM((GROUP, 64, 128), F32)
+    pay, rhs = call(
+        condense_first,
+        (sds(4, 104, 128), sds(GROUP, 128)),
+        [mats, pltpu.VMEM((64, GROUP * 64), F32)],
+        (),
         (0,),
-        (-10, -11),
-    )(right_side, mob, core, near, got)
-    own, bj_core, bj_near = lax.optimization_barrier((own, *swap(to_core, to_near)))
-    other = lax.ppermute(own, "slab", with_core)
+    )(own, other)
+    pay, to_core, to_near = lax.optimization_barrier((pay, to_core, to_near))
+    bj_core, bj_near = swap(to_core, to_near)
+    bounds = exchange(pay, "slab", between)
+    bounds, bj_core, bj_near = lax.optimization_barrier((bounds, bj_core, bj_near))
     work = [
-        pltpu.VMEM((64, 64, 128), F32),
-        pltpu.VMEM((64, 128), F32),
-        pltpu.VMEM((64, 64, 128), F32),
-        pltpu.VMEM((64, 128), F32),
-        pltpu.VMEM((66, 64, 128), F32),
-        pltpu.VMEM((64, 128), F32),
+        mats,
+        pltpu.VMEM((8, 128), F32),
+        pltpu.VMEM((8, 128), F32),
+        pltpu.VMEM((5, 64, 128), F32),
+        pltpu.VMEM((GROUP + 8, 128), F32),
+        pltpu.VMEM((GROUP + 2, 64, 128), F32),
     ]
-    part = call(chain_first, sds(4, 40, 128), work, (2, 4, 5), (-1,))(own, other, fac, beside, ups, downs)
-    coarse = exchange(part, "quad")
-    stencil = (subdomain, zsub, ysub, kz, ky, kyt, kx, kxe, right_side)
-    z0, q0, pay = call(
-        first, (grid, grid, sds(32, 8, 128)), [pltpu.VMEM((64, 128), F32)], (4, 12), (2,)
-    )(coarse, bj, bj_core, bj_near, *stencil, cols)
-    everyone = exchange(pay.reshape(256, 1, 128), BOTH).reshape(256, 128)
-    bj1, to_core, to_near, ups, downs = call(smooth, (grid, plane, plane, edge, edge), (), (), (-4, -5))(q0, kz, inv)
-    bj_core, bj_near = swap(to_core, to_near)
-    part, dots = call(chain_second, (sds(4, 40, 128), sds(8, 128)), work, (0, 1, 3, 5, 6), (-1,))(
-        own, other, everyone, fac, beside, ups, downs
+    part = call(chain_first, sds(4, 40, 128), work, (6, 7), (-1,))(
+        bounds, own, other, rhs, fac, beside, ups, downs
     )
     coarse = exchange(part, "quad")
-    z1, g1, r1, pay = call(second, (grid, grid, grid, sds(32, 8, 128)), (), (4, 12), (3,))(
-        coarse, bj1, bj_core, bj_near, *stencil, z0, q0, dots
+    stencil = (sub, zsub, ysub, kz, ky, kyt, kx, kxe, inv, rs)
+    z0, q0, pay = call(
+        first, (grid, grid, sds(8, 8, 128)), [pltpu.VMEM((64, 128), F32)], (), (2,)
+    )(coarse, bj_core, bj_near, *stencil, cols)
+    plane_rows = exchange(pay.reshape(64, 1, 128), BOTH, planes).reshape(64, 128)
+    to_core, to_near, ups, downs = call(smooth, (plane, plane, edge, edge), (), (), (-3, -4))(q0, kz, inv)
+    bj_core, bj_near = swap(to_core, to_near)
+    pay, rhs = call(condense_second, (sds(4, 8, 128), sds(GROUP, 128)), [mats], (), (0,))(plane_rows, own, other)
+    vecs = exchange(pay, "slab", between)
+    part, dots = call(chain_second, (sds(4, 40, 128), sds(8, 128)), work, (7, 8), (-1,))(
+        bounds, vecs, own, other, rhs, fac, beside, ups, downs
+    )
+    coarse = exchange(part, "quad")
+    z1, g1, r1, pay = call(second, (grid, grid, grid, sds(32, 8, 128)), (), (), (3,))(
+        coarse, bj_core, bj_near, *stencil, z0, q0, dots
     )
     everyone = exchange(pay.reshape(256, 1, 128), BOTH).reshape(256, 128)
     return tuple(call(last, (grid, grid))(everyone, dots, z0, q0, z1, g1, r1))

time: 138 us -> 135 us (0.978)
  blocking collectives: 30.2 us -> 46.9 us
  Pallas kernels: 35.4 us -> 27 us
  waiting for transfers between devices: 26.8 us -> 19.9 us
  starting transfers between devices: 44.3 us -> 39.1 us
    all_to_all x2 -> x3, blocking collectives: 30.2 us -> 46.9 us  [exchange(): lax.all_to_all(value, axis, 0, 0, tiled=True, axis_index_groups=groups)]
    pallas_call x9 -> x11, Pallas kernels: 35.4 us -> 27 us  [run(): pl.pallas_call(wrapped, in_specs=[hbm if i in far else vmem for i in rang...]
    ppermute x3, waiting for transfers between devices: 11.5 us -> 5.86 us  [swap(): lax.ppermute(to_near, 'slab', with_near)]
    ppermute x1, starting transfers between devices: 4.47 us -> 2.25 us  [body(): other = lax.ppermute(own, 'slab', with_core)]
    ppermute x3, starting transfers between devices: 5.77 us -> 3.64 us  [swap(): lax.ppermute(to_core, 'slab', with_core)]
    all_to_all x4 -> x5, waiting for transfers between devices: 13.5 us -> 13 us  [exchange(): lax.all_to_all(value, axis, 0, 0, tiled=True, axis_index_groups=groups)]
    all_to_all x4 -> x5, starting transfers between devices: 26.2 us -> 26.3 us  [exchange(): lax.all_to_all(value, axis, 0, 0, tiled=True, axis_index_groups=groups)]
  transfers between devices with their start and end apart: 11 -> 12, of which waited for: 6 -> 7; matrix products, arithmetic and copies ran while one was open for 0% -> 0% of each run, Pallas kernels for 10% -> 5%
where the time goes in v5:
time: 135 us; the launch traced here: 134 us
  blocking collectives  46.9 us (35%)
  starting transfers between devices  39.1 us (29%)
  Pallas kernels  27 us (20%)
  waiting for transfers between devices  19.9 us (15%)
    all_to_all x3, blocking collectives, exchange(): lax.all_to_all(value, axis, 0, 0, tiled=True, axis_index_groups=groups)  46.9 us
    pallas_call x11, Pallas kernels, run(): pl.pallas_call(wrapped, in_specs=[hbm if i in far else vmem for i in rang...  27 us
    all_to_all x5, starting transfers between devices, exchange(): lax.all_to_all(value, axis, 0, 0, tiled=True, axis_index_groups=groups)  26.3 us
    all_to_all x5, waiting for transfers between devices, exchange(): lax.all_to_all(value, axis, 0, 0, tiled=True, axis_index_groups=groups)  13 us
    ppermute x3, starting transfers between devices, swap(): lax.ppermute(to_near, 'slab', with_near)  6.87 us
    ppermute x3, waiting for transfers between devices, swap(): lax.ppermute(to_near, 'slab', with_near)  5.86 us
    ppermute x3, starting transfers between devices, swap(): lax.ppermute(to_core, 'slab', with_core)  3.64 us
  transfers between devices with their start and end apart: 12, of which 7 were waited for; matrix products, arithmetic and copies ran while one was open for 0% of the time, Pallas kernels for 5%

profile of v5, /device:TPU:1, one launch (start us, length us, event | category | flops | bytes accessed | tf_op | source)
XLA Modules:
  0.0 133.8 jit_solution(9567578023380740148)
XLA Ops:
  0.6 4.8 %begin.1 = (f32[4,16,1024]{2,1,0:T(8,128)S(1)}, f32[384,128]{1,0:T(8,128)S(1)}, f32[384,128]{1,0:T(8,128)S(1)}, f32[4,16,1024]{2,1,0:T(8,128)S(1)}, s32[4,16,102...) custom-call(f32[4,16,1024]{2,1,0:T(8,128)} %refs_0_.1, ...), custom_call_target="tpu_custom_call" | custom-call | tf_op jit(solution)/shard_map/begin/pallas_call | solution.py:83
  5.4 5.0 %all-to-all-start = ((f32[4,128,128]{2,1,0:T(8,128)}), f32[4,128,128]{2,1,0:T(8,128)S(1)}, u32[]{:S(2)}, u32[]{:S(2)}) async-start(f32[4,128,128]{2,1,0:T(8,128)} %get-tuple-element.54), calls=%async_computation | async-start | bytes 524288 | tf_op jit(solution)/shard_map/all_to_all | solution.py:620
  10.5 1.7 %collective-permute-start = (f32[384,128]{1,0:T(8,128)S(1)}, f32[384,128]{1,0:T(8,128)S(1)}, u32[]{:S(2)}, u32[]{:S(2)}) collective-permute-start(f32[384,128]{1,0:T(8,128)S(1)} %get-tuple-element.58), channel_id=1, source_target_pairs={{0,4},{4,0},{8,12},{12,8},{16,20},{20,16},{24,28},{28,24},{32,36},... | collective-permute-start | bytes 589832 | tf_op jit(solution)/shard_map/ppermute | solution.py:623
  12.2 2.6 %collective-permute-start.1 = (f32[384,128]{1,0:T(8,128)S(1)}, f32[384,128]{1,0:T(8,128)S(1)}, u32[]{:S(2)}, u32[]{:S(2)}) collective-permute-start(f32[384,128]{1,0:T(8,128)S(1)} %get-tuple-element.59), channel_id=1, source_target_pairs={{4,8},{8,4},{12,16},{16,12},{20,24},{24,20},{28,32},{32,28},{36,40... | collective-permute-start | bytes 589832 | tf_op jit(solution)/shard_map/ppermute | solution.py:623
  14.9 1.1 all-to-all-done.refs_0_.refs_4_
  16.0 1.1 share.1
  17.1 2.1 %collective-permute-done.1.refs_3_ = f32[384,128]{1,0:T(8,128)S(1)} collective-permute-done((f32[384,128]{1,0:T(8,128)S(1)}, f32[384,128]{1,0:T(8,128)S(1)}, u32[]{:S(2)}, u32[]{:S(2)}) %collective-permute-start.1) | collective-permute-done | bytes 196640 | tf_op jit(solution)/shard_map/ppermute | solution.py:623
  19.2 8.2 %all-to-all-start.1 = ((f32[8,40,128]{2,1,0:T(8,128)}), f32[8,40,128]{2,1,0:T(8,128)S(1)}, u32[]{:S(2)}, u32[]{:S(2)}) async-start(f32[8,40,128]{2,1,0:T(8,128)} %get-tuple-element.60), calls=%async_computation.1 | async-start | bytes 327680 | tf_op jit(solution)/shard_map/all_to_all | solution.py:620
  27.4 1.2 setup.1
  28.6 7.3 %all-to-all-done.1.refs_0_.refs_1_.refs_2_ = f32[8,40,128]{2,1,0:T(8,128)S(1)} async-done(((f32[8,40,128]{2,1,0:T(8,128)}), f32[8,40,128]{2,1,0:T(8,128)S(1)}, u32[]{:S(2)}, u32[]{:S(2)}) %all-to-all-start.1) | async-done | bytes 163872 | tf_op jit(solution)/shard_map/all_to_all | solution.py:620
  35.8 2.2 %collective-permute-start.2 = (f32[8,40,128]{2,1,0:T(8,128)S(1)}, f32[8,40,128]{2,1,0:T(8,128)S(1)}, u32[]{:S(2)}, u32[]{:S(2)}) collective-permute-start(f32[8,40,128]{2,1,0:T(8,128)S(1)} %all-to-all-done.1.refs_0_.refs_1_.refs_2_), channel_id=1, source_target_pairs={{0,4},{4,0},{8,12},{12,8},{16,20},{20,16},{24,28},{28,24},{32,36},... | collective-permute-start | bytes 491528 | tf_op jit(solution)/shard_map/ppermute | solution.py:647
  38.1 1.0 collective-permute-done.2.refs_1_.refs_2_.refs_3_
  39.1 3.4 %condense_first.1 = (f32[4,104,128]{2,1,0:T(8,128)}, f32[16,128]{1,0:T(8,128)S(1)}) custom-call(f32[8,40,128]{2,1,0:T(8,128)S(1)} %all-to-all-done.1.refs_0_.refs_1_.refs_2_, f32[8,40,128]{2,1,0:T(8,128)S(1)} %collective-permute-done.2.refs_1_.refs_2_.refs_3_), custom_call_target="tpu_custom_call" | custom-call | tf_op jit(solution)/shard_map/condense_first/pallas_call | solution.py:83
  42.5 4.0 %all-to-all-start.2 = ((f32[4,104,128]{2,1,0:T(8,128)}), f32[4,104,128]{2,1,0:T(8,128)S(1)}, u32[]{:S(2)}, u32[]{:S(2)}) async-start(f32[4,104,128]{2,1,0:T(8,128)} %get-tuple-element.71), calls=%async_computation.2 | async-start | bytes 425984 | tf_op jit(solution)/shard_map/all_to_all | solution.py:620
  46.6 0.6 collective-permute-start.3
  47.2 2.1 %collective-permute-start.4 = (f32[16,1024]{1,0:T(8,128)S(1)}, f32[16,1024]{1,0:T(8,128)S(1)}, u32[]{:S(2)}, u32[]{:S(2)}) collective-permute-start(f32[16,1024]{1,0:T(8,128)S(1)} %get-tuple-element.73), channel_id=1, source_target_pairs={{4,8},{8,4},{12,16},{16,12},{20,24},{24,20},{28,32},{32,28},{36,40... | collective-permute-start | bytes 196616 | tf_op jit(solution)/shard_map/ppermute | solution.py:623
  49.3 3.8 %collective-permute-done.4.refs_2_ = f32[16,1024]{1,0:T(8,128)S(1)} collective-permute-done((f32[16,1024]{1,0:T(8,128)S(1)}, f32[16,1024]{1,0:T(8,128)S(1)}, u32[]{:S(2)}, u32[]{:S(2)}) %collective-permute-start.4) | collective-permute-done | bytes 65568 | tf_op jit(solution)/shard_map/ppermute | solution.py:623
  53.1 3.1 %chain_first.1 = f32[4,40,128]{2,1,0:T(8,128)} custom-call(f32[4,104,128]{2,1,0:T(8,128)S(1)} %all-to-all-done.2.refs_0_, f32[8,40,128]{2,1,0:T(8,128)S(1)} %all-to-all-done.1.refs_0_.refs_1_.refs_2_, f32[8,40,128]{2,1,0:T(8,128)S(1)} %collective-permute-done.2.refs_1_.refs_2_.refs_3_, f32[16,128]{1,0:T(8,128)S(1)} %get-tuple-element.75.refs_3_, ...), custom_call_target="tpu_custom_call" | custom-call | tf_op jit(solution)/shard_map/chain_first/pallas_call | solution.py:83
  56.2 9.1 %all_to_all.40.refs_0_ = f32[4,40,128]{2,1,0:T(8,128)S(1)} all-to-all(f32[4,40,128]{2,1,0:T(8,128)} %chain_first.1), channel_id=1, replica_groups=mesh['slab'=64,'quad'=4] {'quad'}, dimensions={0} | all-to-all | bytes 163840 | tf_op jit(solution)/shard_map/all_to_all | solution.py:620
  65.3 4.6 %first.1 = (f32[4,16,1024]{2,1,0:T(8,128)S(1)}, f32[4,16,1024]{2,1,0:T(8,128)S(1)}, f32[8,8,128]{2,1,0:T(8,128)}) custom-call(f32[4,40,128]{2,1,0:T(8,128)S(1)} %all_to_all.40.refs_0_, f32[16,1024]{1,0:T(8,128)S(1)} %collective-permute-done.3.refs_1_, f32[16,1024]{1,0:T(8,128)S(1)} %collective-permute-done.4.refs_2_, ...), custom_call_target="tpu_custom_call" | custom-call | tf_op jit(solution)/shard_map/first/pallas_call | solution.py:83
  69.9 15.3 %all_to_all.41 = f32[64,1,128]{2,1,0:T(1,128)S(1)} all-to-all(f32[64,1,128]{2,1,0:T(1,128)} %bitcast.15), channel_id=1, replica_groups={{0,1,2,3,4,5,6,7,8,9,10,11,12,13,14,15,16,17,18,19,20,21,22,23,24,25,26..., dimensions={0} | all-to-all | bytes 65536 | tf_op jit(solution)/shard_map/all_to_all | solution.py:620
  85.2 2.2 %condense_second.1 = (f32[4,8,128]{2,1,0:T(8,128)}, f32[16,128]{1,0:T(8,128)S(1)}) custom-call(f32[64,128]{1,0:T(8,128)S(1)} %bitcast.11, f32[8,40,128]{2,1,0:T(8,128)S(1)} %all-to-all-done.1.refs_0_.refs_1_.refs_2_, f32[8,40,128]{2,1,0:T(8,128)S(1)} %collective-permute-done.2.refs_1_.refs_2_.refs_3_), custom_call_target="tpu_custom_call" | custom-call | tf_op jit(solution)/shard_map/condense_second/pallas_call | solution.py:83
  87.4 5.8 %all-to-all-start.5 = ((f32[4,8,128]{2,1,0:T(8,128)}), f32[4,8,128]{2,1,0:T(8,128)S(1)}, u32[]{:S(2)}, u32[]{:S(2)}) async-start(f32[4,8,128]{2,1,0:T(8,128)} %get-tuple-element.92), calls=%async_computation.5 | async-start | bytes 32768 | tf_op jit(solution)/shard_map/all_to_all | solution.py:620
  93.1 0.7 smooth.1
  93.8 1.3 collective-permute-start.5
  95.1 2.1 %collective-permute-start.6 = (f32[16,1024]{1,0:T(8,128)S(1)}, f32[16,1024]{1,0:T(8,128)S(1)}, u32[]{:S(2)}, u32[]{:S(2)}) collective-permute-start(f32[16,1024]{1,0:T(8,128)S(1)} %get-tuple-element.99), channel_id=1, source_target_pairs={{4,8},{8,4},{12,16},{16,12},{20,24},{24,20},{28,32},{32,28},{36,40... | collective-permute-start | bytes 196616 | tf_op jit(solution)/shard_map/ppermute | solution.py:623
  97.3 3.1 %chain_second.1 = (f32[4,40,128]{2,1,0:T(8,128)}, f32[8,128]{1,0:T(8,128)S(1)}) custom-call(f32[4,104,128]{2,1,0:T(8,128)S(1)} %all-to-all-done.2.refs_0_, f32[4,8,128]{2,1,0:T(8,128)S(1)} %all-to-all-done.5.refs_1_, f32[8,40,128]{2,1,0:T(8,128)S(1)} %all-to-all-done.1.refs_0_.refs_1_.refs_2_, ...), custom_call_target="tpu_custom_call" | custom-call | tf_op jit(solution)/shard_map/chain_second/pallas_call | solution.py:83
  100.4 3.3 %all-to-all-start.6 = ((f32[4,40,128]{2,1,0:T(8,128)}), f32[4,40,128]{2,1,0:T(8,128)S(1)}, u32[]{:S(2)}, u32[]{:S(2)}) async-start(f32[4,40,128]{2,1,0:T(8,128)} %get-tuple-element.97), calls=%async_computation.6 | async-start | bytes 163840 | tf_op jit(solution)/shard_map/all_to_all | solution.py:620
  103.8 4.5 %all-to-all-done.6.refs_0_ = f32[4,40,128]{2,1,0:T(8,128)S(1)} async-done(((f32[4,40,128]{2,1,0:T(8,128)}), f32[4,40,128]{2,1,0:T(8,128)S(1)}, u32[]{:S(2)}, u32[]{:S(2)}) %all-to-all-start.6) | async-done | bytes 81952 | tf_op jit(solution)/shard_map/all_to_all | solution.py:620
  108.3 1.8 %second.1 = (f32[4,16,1024]{2,1,0:T(8,128)S(1)}, f32[4,16,1024]{2,1,0:T(8,128)S(1)}, f32[4,16,1024]{2,1,0:T(8,128)S(1)}, f32[32,8,128]{2,1,0:T(8,128)}) custom-call(f32[4,40,128]{2,1,0:T(8,128)S(1)} %all-to-all-done.6.refs_0_, f32[16,1024]{1,0:T(8,128)S(1)} %collective-permute-done.5.refs_1_, f32[16,1024]{1,0:T(8,128)S(1)} %collective-permute-done.6.refs_2_, ...), custom_call_target="tpu_custom_call" | custom-call | tf_op jit(solution)/shard_map/second/pallas_call | solution.py:83
  110.1 22.5 %all_to_all.42 = f32[256,1,128]{2,1,0:T(1,128)S(1)} all-to-all(f32[256,1,128]{2,1,0:T(1,128)} %bitcast.12), channel_id=1, replica_groups=mesh['slab'=64,'quad'=4] {'slab','quad'}, dimensions={0} | all-to-all | bytes 262144 | tf_op jit(solution)/shard_map/all_to_all | solution.py:620
  132.6 1.1 last.1
  (6 shorter events, 0.1 us)
Async XLA Ops:
  5.4 10.6 %all-to-all-start = ((f32[4,128,128]{2,1,0:T(8,128)}), f32[4,128,128]{2,1,0:T(8,128)S(1)}, u32[]{:S(2)}, u32[]{:S(2)}) async-start(f32[4,128,128]{2,1,0:T(8,128)} %get-tuple-element.54), calls=%async_computation | async-start | bytes 524288 | tf_op jit(solution)/shard_map/all_to_all | solution.py:620
  10.5 6.6 %collective-permute-start = (f32[384,128]{1,0:T(8,128)S(1)}, f32[384,128]{1,0:T(8,128)S(1)}, u32[]{:S(2)}, u32[]{:S(2)}) collective-permute-start(f32[384,128]{1,0:T(8,128)S(1)} %get-tuple-element.58), channel_id=1, source_target_pairs={{0,4},{4,0},{8,12},{12,8},{16,20},{20,16},{24,28},{28,24},{32,36},... | collective-permute-start | bytes 589832 | tf_op jit(solution)/shard_map/ppermute | solution.py:623
  12.2 7.0 %collective-permute-start.1 = (f32[384,128]{1,0:T(8,128)S(1)}, f32[384,128]{1,0:T(8,128)S(1)}, u32[]{:S(2)}, u32[]{:S(2)}) collective-permute-start(f32[384,128]{1,0:T(8,128)S(1)} %get-tuple-element.59), channel_id=1, source_target_pairs={{4,8},{8,4},{12,16},{16,12},{20,24},{24,20},{28,32},{32,28},{36,40... | collective-permute-start | bytes 589832 | tf_op jit(solution)/shard_map/ppermute | solution.py:623
  19.2 16.7 %all-to-all-start.1 = ((f32[8,40,128]{2,1,0:T(8,128)}), f32[8,40,128]{2,1,0:T(8,128)S(1)}, u32[]{:S(2)}, u32[]{:S(2)}) async-start(f32[8,40,128]{2,1,0:T(8,128)} %get-tuple-element.60), calls=%async_computation.1 | async-start | bytes 327680 | tf_op jit(solution)/shard_map/all_to_all | solution.py:620
  35.8 3.3 %collective-permute-start.2 = (f32[8,40,128]{2,1,0:T(8,128)S(1)}, f32[8,40,128]{2,1,0:T(8,128)S(1)}, u32[]{:S(2)}, u32[]{:S(2)}) collective-permute-start(f32[8,40,128]{2,1,0:T(8,128)S(1)} %all-to-all-done.1.refs_0_.refs_1_.refs_2_), channel_id=1, source_target_pairs={{0,4},{4,0},{8,12},{12,8},{16,20},{20,16},{24,28},{28,24},{32,36},... | collective-permute-start | bytes 491528 | tf_op jit(solution)/shard_map/ppermute | solution.py:647
  42.5 10.5 %all-to-all-start.2 = ((f32[4,104,128]{2,1,0:T(8,128)}), f32[4,104,128]{2,1,0:T(8,128)S(1)}, u32[]{:S(2)}, u32[]{:S(2)}) async-start(f32[4,104,128]{2,1,0:T(8,128)} %get-tuple-element.71), calls=%async_computation.2 | async-start | bytes 425984 | tf_op jit(solution)/shard_map/all_to_all | solution.py:620
  46.6 2.7 %collective-permute-start.3 = (f32[16,1024]{1,0:T(8,128)S(1)}, f32[16,1024]{1,0:T(8,128)S(1)}, u32[]{:S(2)}, u32[]{:S(2)}) collective-permute-start(f32[16,1024]{1,0:T(8,128)S(1)} %get-tuple-element.72), channel_id=1, source_target_pairs={{0,4},{4,0},{8,12},{12,8},{16,20},{20,16},{24,28},{28,24},{32,36},... | collective-permute-start | bytes 196616 | tf_op jit(solution)/shard_map/ppermute | solution.py:623
  47.2 5.9 %collective-permute-start.4 = (f32[16,1024]{1,0:T(8,128)S(1)}, f32[16,1024]{1,0:T(8,128)S(1)}, u32[]{:S(2)}, u32[]{:S(2)}) collective-permute-start(f32[16,1024]{1,0:T(8,128)S(1)} %get-tuple-element.73), channel_id=1, source_target_pairs={{4,8},{8,4},{12,16},{16,12},{20,24},{24,20},{28,32},{32,28},{36,40... | collective-permute-start | bytes 196616 | tf_op jit(solution)/shard_map/ppermute | solution.py:623
  87.4 10.0 %all-to-all-start.5 = ((f32[4,8,128]{2,1,0:T(8,128)}), f32[4,8,128]{2,1,0:T(8,128)S(1)}, u32[]{:S(2)}, u32[]{:S(2)}) async-start(f32[4,8,128]{2,1,0:T(8,128)} %get-tuple-element.92), calls=%async_computation.5 | async-start | bytes 32768 | tf_op jit(solution)/shard_map/all_to_all | solution.py:620
  93.8 9.9 %collective-permute-start.5 = (f32[16,1024]{1,0:T(8,128)S(1)}, f32[16,1024]{1,0:T(8,128)S(1)}, u32[]{:S(2)}, u32[]{:S(2)}) collective-permute-start(f32[16,1024]{1,0:T(8,128)S(1)} %get-tuple-element.98), channel_id=1, source_target_pairs={{0,4},{4,0},{8,12},{12,8},{16,20},{20,16},{24,28},{28,24},{32,36},... | collective-permute-start | bytes 196616 | tf_op jit(solution)/shard_map/ppermute | solution.py:623
  95.1 8.7 %collective-permute-start.6 = (f32[16,1024]{1,0:T(8,128)S(1)}, f32[16,1024]{1,0:T(8,128)S(1)}, u32[]{:S(2)}, u32[]{:S(2)}) collective-permute-start(f32[16,1024]{1,0:T(8,128)S(1)} %get-tuple-element.99), channel_id=1, source_target_pairs={{4,8},{8,4},{12,16},{16,12},{20,24},{24,20},{28,32},{32,28},{36,40... | collective-permute-start | bytes 196616 | tf_op jit(solution)/shard_map/ppermute | solution.py:623
  100.4 7.8 %all-to-all-start.6 = ((f32[4,40,128]{2,1,0:T(8,128)}), f32[4,40,128]{2,1,0:T(8,128)S(1)}, u32[]{:S(2)}, u32[]{:S(2)}) async-start(f32[4,40,128]{2,1,0:T(8,128)} %get-tuple-element.97), calls=%async_computation.6 | async-start | bytes 163840 | tf_op jit(solution)/shard_map/all_to_all | solution.py:620

commit v6 on v5

--- a/solution.py
+++ b/solution.py
@@ -125,26 +125,25 @@
 
 
 def restrict(sub_ref, field_ref, rows_ref, least=0):
-    def group(g, unused):
+    for base in range(0, 64, 16):
+
         def tile(t, totals):
-            rows = pl.ds(pl.multiple_of((t % 2) * 8, 8), 8)
-            sub = sub_ref[t // 2, rows, :]
-            field = field_ref[t // 2, rows, :]
+            at = t // 2
+            rows = pl.ds(pl.multiple_of((at % 2) * 8, 8), 8)
+            lanes = pl.ds(pl.multiple_of((t % 2) * 512, 512), 512)
+            sub = sub_ref[at // 2, rows, lanes]
+            field = field_ref[at // 2, rows, lanes]
             out = []
-            for label in range(8):
-                picked = jnp.where(sub == g * 8 + (label + least), field, 0.0)
-                total = totals[label]
-                for j in range(8):
-                    total = total + picked[:, j * 128 : (j + 1) * 128]
-                out.append(total)
+            for label in range(16):
+                picked = jnp.where(sub == base + label + least, field, 0.0)
+                parts = [picked[:, j * 128 : (j + 1) * 128] for j in range(4)]
+                out.append(totals[label] + ((parts[0] + parts[1]) + (parts[2] + parts[3])))
             return tuple(out)
 
-        totals = lax.fori_loop(0, 8, tile, tuple(jnp.zeros((8, 128), F32) for _ in range(8)))
-        stacked = jnp.concatenate([jnp.sum(t, axis=0, keepdims=True) for t in totals], axis=0)
-        rows_ref[pl.ds(pl.multiple_of(g * 8, 8), 8), :] = stacked
-        return unused
-
-    lax.fori_loop(0, 8, group, 0)
+        totals = lax.fori_loop(0, 16, tile, tuple(jnp.zeros((8, 128), F32) for _ in range(16)), unroll=4)
+        for half in range(0, 16, 8):
+            sums = [jnp.sum(t, axis=0, keepdims=True) for t in totals[half : half + 8]]
+            rows_ref[base + half : base + half + 8, :] = jnp.concatenate(sums, axis=0)
     return jnp.sum(rows_ref[...].T, axis=0, keepdims=True)
 
 
@@ -217,16 +216,11 @@
         part[320:384, :] = fac[:, 128:]
     upward = jnp.concatenate([m[15:16, :] for m in ms] + [s[15:16, :] for s in ss], axis=0)
     downward = jnp.concatenate([m[0:1, :] for m in ms] + [s[0:1, :] for s in ss], axis=0)
-    both = jnp.concatenate([cin, cin], axis=1)
-    lane = lane_of((64, 128))
-    row = lax.broadcasted_iota(jnp.int32, (64, 128), 0)
-    tail = jnp.where(row == 0, both, 0.0)
+    both = jnp.broadcast_to(jnp.concatenate([cin, cin], axis=1), (8, 128))
     for q in range(4):
-        block = fac[:, (q // 2) * 128 : (q // 2 + 1) * 128]
-        if q % 2:
-            block = pltpu.roll(block, 64, 1)
-        pay[q, 0:64, :] = jnp.where(lane < 64, block, tail)
-        spread(pay.at[q], 64, face_for(q, upward, downward))
+        pay[q, 0:32, :] = pack(fac[:, q * 64 : (q + 1) * 64])
+        pay[q, 32:40, :] = both
+        spread(pay.at[q], 40, face_for(q, upward, downward))
 
 
 def send_faces(out, to_core, to_near, ups, downs):
@@ -239,10 +233,9 @@
 
 
 def share(ready, got, fac, cou, cols, pay):
-    low = lane_of((64, 128)) < 64
-    for h in range(2):
-        cols[h] = jnp.where(low, got[2 * h, 0:64, :], pltpu.roll(got[2 * h + 1, 0:64, :], 64, 1))
-    cins = [pltpu.roll(got[q, 0:8, :], 64, 1)[0:1, :64] for q in range(4)]
+    for q in range(4):
+        cols[q] = got[q, 0:32, :]
+    cins = [got[q, 32:33, :64] for q in range(4)]
     cin = jnp.concatenate(cins, axis=1)
     rhs = lax.dot_general(
         jnp.broadcast_to(cin, (8, 256)), fac[...], (((1,), (1,)), ((), ())), precision=HIGH, preferred_element_type=F32
@@ -267,8 +260,8 @@
     n_fac = jnp.concatenate([near[256:320, :], near[320:384, :]], axis=1)
     beside[0] = choose(odd, c_fac, n_fac)
     beside[1] = choose(odd, n_fac, c_fac)
-    before = gather_rows(got[jnp.maximum(quad - 1, 0)], 64, 8)
-    after = gather_rows(got[jnp.minimum(quad + 1, 3)], 64, 8)
+    before = gather_rows(got[jnp.maximum(quad - 1, 0)], 40, 8)
+    after = gather_rows(got[jnp.minimum(quad + 1, 3)], 40, 8)
     ylo = jnp.where(jnp.broadcast_to(quad, before.shape) > 0, before, 0.0)
     yhi = jnp.where(jnp.broadcast_to(quad, after.shape) < 3, after, 0.0)
     ysub[...] = jnp.concatenate([ylo[4:8, :], yhi[4:8, :]], axis=0).astype(jnp.int32)
@@ -563,7 +556,7 @@
     parts = []
     for q in range(4):
         part = lax.dot_general(
-            cin, cols[q // 2][:, q % 2 * 64 : q % 2 * 64 + 64], (((1,), (1,)), ((), ())), precision=HIGH, preferred_element_type=F32
+            cin, jnp.concatenate([cols[q, :, :64], cols[q, :, 64:]], axis=0), (((1,), (1,)), ((), ())), precision=HIGH, preferred_element_type=F32
         )[0:1, :]
         part = jnp.concatenate([part, part], axis=1)
         parts.append(jnp.where(lane < 64, part, jnp.where(lane == 64, rz, jnp.where(lane == 65, pq, 0.0))))
@@ -625,14 +618,14 @@
     mob, core, near, rs, sub, fac, cou, pay = call(
         begin,
         (grid, sds(384, 128), sds(384, 128), grid, jax.ShapeDtypeStruct((4, 16, 1024), jnp.int32))
-        + (sds(64, 256), sds(32, 128), sds(4, 128, 128)),
+        + (sds(64, 256), sds(32, 128), sds(4, 104, 128)),
         [pltpu.VMEM((64, 128), F32)],
         (3, 0, 1, 2, 4, 5),
         (-8,),
     )(right_side, phase_label, density_gain, subdomain, fac, cou)
     core, near = swap(core, near)
     got = exchange(pay, "quad")
-    cols, pay = call(share, (sds(2, 64, 128), sds(GROUP // 2, 40, 128)), (), (), (1,))(got, fac, cou)
+    cols, pay = call(share, (sds(4, 32, 128), sds(GROUP // 2, 40, 128)), (), (), (1,))(got, fac, cou)
     pay, core, near = lax.optimization_barrier((pay, core, near))
     own = exchange(pay, "slab", within)
     kz, ky, kyt, kx, kxe, inv, to_core, to_near, ups, downs, zsub, ysub, beside = call(

time: 135 us -> 134 us (level)
  blocking collectives: 46.9 us -> 54.7 us
  starting transfers between devices: 39.1 us -> 35.3 us
  waiting for transfers between devices: 19.9 us -> 16.3 us
  Pallas kernels: 27 us -> 25.6 us
    all_to_all x3 -> x4, blocking collectives: 46.9 us -> 54.7 us  [exchange(): lax.all_to_all(value, axis, 0, 0, tiled=True, axis_index_groups=groups)]
    all_to_all x5 -> x4, starting transfers between devices: 26.3 us -> 21.3 us  [exchange(): lax.all_to_all(value, axis, 0, 0, tiled=True, axis_index_groups=groups)]
    ppermute x3, waiting for transfers between devices: 5.86 us -> 3.78 us  [swap(): lax.ppermute(to_near, 'slab', with_near)]
    ppermute x3, starting transfers between devices: 3.64 us -> 5.24 us  [swap(): lax.ppermute(to_core, 'slab', with_core)]
    all_to_all x5 -> x4, waiting for transfers between devices: 13 us -> 11.5 us  [exchange(): lax.all_to_all(value, axis, 0, 0, tiled=True, axis_index_groups=groups)]
    pallas_call x11, Pallas kernels: 27 us -> 25.6 us  [run(): pl.pallas_call(wrapped, in_specs=[hbm if i in far else vmem for i in rang...]
  transfers between devices with their start and end apart: 12 -> 11, of which waited for: 7 -> 5; matrix products, arithmetic and copies ran while one was open for 0% -> 0% of each run, Pallas kernels for 5% -> 5%
where the time goes in v6:
time: 134 us; the launch traced here: 133 us
  blocking collectives  54.7 us (41%)
  starting transfers between devices  35.3 us (26%)
  Pallas kernels  25.6 us (19%)
  waiting for transfers between devices  16.3 us (12%)
    all_to_all x4, blocking collectives, exchange(): lax.all_to_all(value, axis, 0, 0, tiled=True, axis_index_groups=groups)  54.7 us
    pallas_call x11, Pallas kernels, run(): pl.pallas_call(wrapped, in_specs=[hbm if i in far else vmem for i in rang...  25.6 us
    all_to_all x4, starting transfers between devices, exchange(): lax.all_to_all(value, axis, 0, 0, tiled=True, axis_index_groups=groups)  21.3 us
    all_to_all x4, waiting for transfers between devices, exchange(): lax.all_to_all(value, axis, 0, 0, tiled=True, axis_index_groups=groups)  11.5 us
    ppermute x3, starting transfers between devices, swap(): lax.ppermute(to_near, 'slab', with_near)  6.13 us
    ppermute x3, starting transfers between devices, swap(): lax.ppermute(to_core, 'slab', with_core)  5.24 us
    ppermute x3, waiting for transfers between devices, swap(): lax.ppermute(to_near, 'slab', with_near)  3.78 us
  transfers between devices with their start and end apart: 11, of which 5 were waited for; matrix products, arithmetic and copies ran while one was open for 0% of the time, Pallas kernels for 5%

profile of v6, /device:TPU:1, one launch (start us, length us, event | category | flops | bytes accessed | tf_op | source)
XLA Modules:
  0.0 132.6 jit_solution(4052537355771803687)
XLA Ops:
  0.6 4.1 %begin.1 = (f32[4,16,1024]{2,1,0:T(8,128)S(1)}, f32[384,128]{1,0:T(8,128)S(1)}, f32[384,128]{1,0:T(8,128)S(1)}, f32[4,16,1024]{2,1,0:T(8,128)S(1)}, s32[4,16,102...) custom-call(f32[4,16,1024]{2,1,0:T(8,128)} %refs_0_.1, ...), custom_call_target="tpu_custom_call" | custom-call | tf_op jit(solution)/shard_map/begin/pallas_call | solution.py:83
  4.7 3.3 %collective-permute-start = (f32[384,128]{1,0:T(8,128)S(1)}, f32[384,128]{1,0:T(8,128)S(1)}, u32[]{:S(2)}, u32[]{:S(2)}) collective-permute-start(f32[384,128]{1,0:T(8,128)S(1)} %get-tuple-element.58), channel_id=1, source_target_pairs={{0,4},{4,0},{8,12},{12,8},{16,20},{20,16},{24,28},{28,24},{32,36},... | collective-permute-start | bytes 589832 | tf_op jit(solution)/shard_map/ppermute | solution.py:616
  8.1 1.9 %collective-permute-start.1 = (f32[384,128]{1,0:T(8,128)S(1)}, f32[384,128]{1,0:T(8,128)S(1)}, u32[]{:S(2)}, u32[]{:S(2)}) collective-permute-start(f32[384,128]{1,0:T(8,128)S(1)} %get-tuple-element.59), channel_id=1, source_target_pairs={{4,8},{8,4},{12,16},{16,12},{20,24},{24,20},{28,32},{32,28},{36,40... | collective-permute-start | bytes 589832 | tf_op jit(solution)/shard_map/ppermute | solution.py:616
  10.0 9.3 %all_to_all.40.refs_0_.refs_4_ = f32[4,104,128]{2,1,0:T(8,128)S(1)} all-to-all(f32[4,104,128]{2,1,0:T(8,128)} %get-tuple-element.54), channel_id=1, replica_groups=mesh['slab'=64,'quad'=4] {'quad'}, dimensions={0} | all-to-all | bytes 425984 | tf_op jit(solution)/shard_map/all_to_all | solution.py:613
  19.2 1.0 share.1
  20.3 0.0 collective-permute-done.refs_2_
  20.3 8.2 %all-to-all-start.1 = ((f32[8,40,128]{2,1,0:T(8,128)}), f32[8,40,128]{2,1,0:T(8,128)S(1)}, u32[]{:S(2)}, u32[]{:S(2)}) async-start(f32[8,40,128]{2,1,0:T(8,128)} %get-tuple-element.60), calls=%async_computation.1 | async-start | bytes 327680 | tf_op jit(solution)/shard_map/all_to_all | solution.py:613
  28.4 1.2 setup.1
  29.6 6.9 %all-to-all-done.1.refs_0_.refs_1_.refs_2_ = f32[8,40,128]{2,1,0:T(8,128)S(1)} async-done(((f32[8,40,128]{2,1,0:T(8,128)}), f32[8,40,128]{2,1,0:T(8,128)S(1)}, u32[]{:S(2)}, u32[]{:S(2)}) %all-to-all-start.1) | async-done | bytes 163872 | tf_op jit(solution)/shard_map/all_to_all | solution.py:613
  36.5 2.7 %collective-permute-start.2 = (f32[8,40,128]{2,1,0:T(8,128)S(1)}, f32[8,40,128]{2,1,0:T(8,128)S(1)}, u32[]{:S(2)}, u32[]{:S(2)}) collective-permute-start(f32[8,40,128]{2,1,0:T(8,128)S(1)} %all-to-all-done.1.refs_0_.refs_1_.refs_2_), channel_id=1, source_target_pairs={{0,4},{4,0},{8,12},{12,8},{16,20},{20,16},{24,28},{28,24},{32,36},... | collective-permute-start | bytes 491528 | tf_op jit(solution)/shard_map/ppermute | solution.py:640
  39.2 1.0 collective-permute-done.2.refs_1_.refs_2_.refs_3_
  40.2 3.4 %condense_first.1 = (f32[4,104,128]{2,1,0:T(8,128)}, f32[16,128]{1,0:T(8,128)S(1)}) custom-call(f32[8,40,128]{2,1,0:T(8,128)S(1)} %all-to-all-done.1.refs_0_.refs_1_.refs_2_, f32[8,40,128]{2,1,0:T(8,128)S(1)} %collective-permute-done.2.refs_1_.refs_2_.refs_3_), custom_call_target="tpu_custom_call" | custom-call | tf_op jit(solution)/shard_map/condense_first/pallas_call | solution.py:83
  43.6 4.0 %all-to-all-start.2 = ((f32[4,104,128]{2,1,0:T(8,128)}), f32[4,104,128]{2,1,0:T(8,128)S(1)}, u32[]{:S(2)}, u32[]{:S(2)}) async-start(f32[4,104,128]{2,1,0:T(8,128)} %get-tuple-element.71), calls=%async_computation.2 | async-start | bytes 425984 | tf_op jit(solution)/shard_map/all_to_all | solution.py:613
  47.7 0.6 collective-permute-start.3
  48.3 2.1 %collective-permute-start.4 = (f32[16,1024]{1,0:T(8,128)S(1)}, f32[16,1024]{1,0:T(8,128)S(1)}, u32[]{:S(2)}, u32[]{:S(2)}) collective-permute-start(f32[16,1024]{1,0:T(8,128)S(1)} %get-tuple-element.73), channel_id=1, source_target_pairs={{4,8},{8,4},{12,16},{16,12},{20,24},{24,20},{28,32},{32,28},{36,40... | collective-permute-start | bytes 196616 | tf_op jit(solution)/shard_map/ppermute | solution.py:616
  50.4 3.8 %collective-permute-done.4.refs_2_ = f32[16,1024]{1,0:T(8,128)S(1)} collective-permute-done((f32[16,1024]{1,0:T(8,128)S(1)}, f32[16,1024]{1,0:T(8,128)S(1)}, u32[]{:S(2)}, u32[]{:S(2)}) %collective-permute-start.4) | collective-permute-done | bytes 65568 | tf_op jit(solution)/shard_map/ppermute | solution.py:616
  54.2 3.1 %chain_first.1 = f32[4,40,128]{2,1,0:T(8,128)} custom-call(f32[4,104,128]{2,1,0:T(8,128)S(1)} %all-to-all-done.2.refs_0_, f32[8,40,128]{2,1,0:T(8,128)S(1)} %all-to-all-done.1.refs_0_.refs_1_.refs_2_, f32[8,40,128]{2,1,0:T(8,128)S(1)} %collective-permute-done.2.refs_1_.refs_2_.refs_3_, f32[16,128]{1,0:T(8,128)S(1)} %get-tuple-element.75.refs_3_, ...), custom_call_target="tpu_custom_call" | custom-call | tf_op jit(solution)/shard_map/chain_first/pallas_call | solution.py:83
  57.3 7.8 %all_to_all.41.refs_0_ = f32[4,40,128]{2,1,0:T(8,128)S(1)} all-to-all(f32[4,40,128]{2,1,0:T(8,128)} %chain_first.1), channel_id=1, replica_groups=mesh['slab'=64,'quad'=4] {'quad'}, dimensions={0} | all-to-all | bytes 163840 | tf_op jit(solution)/shard_map/all_to_all | solution.py:613
  65.1 3.9 %first.1 = (f32[4,16,1024]{2,1,0:T(8,128)S(1)}, f32[4,16,1024]{2,1,0:T(8,128)S(1)}, f32[8,8,128]{2,1,0:T(8,128)}) custom-call(f32[4,40,128]{2,1,0:T(8,128)S(1)} %all_to_all.41.refs_0_, f32[16,1024]{1,0:T(8,128)S(1)} %collective-permute-done.3.refs_1_, f32[16,1024]{1,0:T(8,128)S(1)} %collective-permute-done.4.refs_2_, ...), custom_call_target="tpu_custom_call" | custom-call | tf_op jit(solution)/shard_map/first/pallas_call | solution.py:83
  69.0 15.0 %all_to_all.42 = f32[64,1,128]{2,1,0:T(1,128)S(1)} all-to-all(f32[64,1,128]{2,1,0:T(1,128)} %bitcast.15), channel_id=1, replica_groups={{0,1,2,3,4,5,6,7,8,9,10,11,12,13,14,15,16,17,18,19,20,21,22,23,24,25,26..., dimensions={0} | all-to-all | bytes 65536 | tf_op jit(solution)/shard_map/all_to_all | solution.py:613
  84.0 2.2 %condense_second.1 = (f32[4,8,128]{2,1,0:T(8,128)}, f32[16,128]{1,0:T(8,128)S(1)}) custom-call(f32[64,128]{1,0:T(8,128)S(1)} %bitcast.11, f32[8,40,128]{2,1,0:T(8,128)S(1)} %all-to-all-done.1.refs_0_.refs_1_.refs_2_, f32[8,40,128]{2,1,0:T(8,128)S(1)} %collective-permute-done.2.refs_1_.refs_2_.refs_3_), custom_call_target="tpu_custom_call" | custom-call | tf_op jit(solution)/shard_map/condense_second/pallas_call | solution.py:83
  86.2 5.8 %all-to-all-start.5 = ((f32[4,8,128]{2,1,0:T(8,128)}), f32[4,8,128]{2,1,0:T(8,128)S(1)}, u32[]{:S(2)}, u32[]{:S(2)}) async-start(f32[4,8,128]{2,1,0:T(8,128)} %get-tuple-element.92), calls=%async_computation.5 | async-start | bytes 32768 | tf_op jit(solution)/shard_map/all_to_all | solution.py:613
  92.0 0.7 smooth.1
  92.7 1.3 collective-permute-start.5
  93.9 2.1 %collective-permute-start.6 = (f32[16,1024]{1,0:T(8,128)S(1)}, f32[16,1024]{1,0:T(8,128)S(1)}, u32[]{:S(2)}, u32[]{:S(2)}) collective-permute-start(f32[16,1024]{1,0:T(8,128)S(1)} %get-tuple-element.99), channel_id=1, source_target_pairs={{4,8},{8,4},{12,16},{16,12},{20,24},{24,20},{28,32},{32,28},{36,40... | collective-permute-start | bytes 196616 | tf_op jit(solution)/shard_map/ppermute | solution.py:616
  96.1 0.1 all-to-all-done.5.refs_1_
  96.2 3.1 %chain_second.1 = (f32[4,40,128]{2,1,0:T(8,128)}, f32[8,128]{1,0:T(8,128)S(1)}) custom-call(f32[4,104,128]{2,1,0:T(8,128)S(1)} %all-to-all-done.2.refs_0_, f32[4,8,128]{2,1,0:T(8,128)S(1)} %all-to-all-done.5.refs_1_, f32[8,40,128]{2,1,0:T(8,128)S(1)} %all-to-all-done.1.refs_0_.refs_1_.refs_2_, ...), custom_call_target="tpu_custom_call" | custom-call | tf_op jit(solution)/shard_map/chain_second/pallas_call | solution.py:83
  99.3 3.3 %all-to-all-start.6 = ((f32[4,40,128]{2,1,0:T(8,128)}), f32[4,40,128]{2,1,0:T(8,128)S(1)}, u32[]{:S(2)}, u32[]{:S(2)}) async-start(f32[4,40,128]{2,1,0:T(8,128)} %get-tuple-element.97), calls=%async_computation.6 | async-start | bytes 163840 | tf_op jit(solution)/shard_map/all_to_all | solution.py:613
  102.6 4.5 %all-to-all-done.6.refs_0_ = f32[4,40,128]{2,1,0:T(8,128)S(1)} async-done(((f32[4,40,128]{2,1,0:T(8,128)}), f32[4,40,128]{2,1,0:T(8,128)S(1)}, u32[]{:S(2)}, u32[]{:S(2)}) %all-to-all-start.6) | async-done | bytes 81952 | tf_op jit(solution)/shard_map/all_to_all | solution.py:613
  107.1 1.8 %second.1 = (f32[4,16,1024]{2,1,0:T(8,128)S(1)}, f32[4,16,1024]{2,1,0:T(8,128)S(1)}, f32[4,16,1024]{2,1,0:T(8,128)S(1)}, f32[32,8,128]{2,1,0:T(8,128)}) custom-call(f32[4,40,128]{2,1,0:T(8,128)S(1)} %all-to-all-done.6.refs_0_, f32[16,1024]{1,0:T(8,128)S(1)} %collective-permute-done.5.refs_1_, f32[16,1024]{1,0:T(8,128)S(1)} %collective-permute-done.6.refs_2_, ...), custom_call_target="tpu_custom_call" | custom-call | tf_op jit(solution)/shard_map/second/pallas_call | solution.py:83
  109.0 22.5 %all_to_all.43 = f32[256,1,128]{2,1,0:T(1,128)S(1)} all-to-all(f32[256,1,128]{2,1,0:T(1,128)} %bitcast.12), channel_id=1, replica_groups=mesh['slab'=64,'quad'=4] {'slab','quad'}, dimensions={0} | all-to-all | bytes 262144 | tf_op jit(solution)/shard_map/all_to_all | solution.py:613
  131.5 1.1 last.1
  (5 shorter events, 0.0 us)
Async XLA Ops:
  4.7 15.5 %collective-permute-start = (f32[384,128]{1,0:T(8,128)S(1)}, f32[384,128]{1,0:T(8,128)S(1)}, u32[]{:S(2)}, u32[]{:S(2)}) collective-permute-start(f32[384,128]{1,0:T(8,128)S(1)} %get-tuple-element.58), channel_id=1, source_target_pairs={{0,4},{4,0},{8,12},{12,8},{16,20},{20,16},{24,28},{28,24},{32,36},... | collective-permute-start | bytes 589832 | tf_op jit(solution)/shard_map/ppermute | solution.py:616
  8.1 12.2 %collective-permute-start.1 = (f32[384,128]{1,0:T(8,128)S(1)}, f32[384,128]{1,0:T(8,128)S(1)}, u32[]{:S(2)}, u32[]{:S(2)}) collective-permute-start(f32[384,128]{1,0:T(8,128)S(1)} %get-tuple-element.59), channel_id=1, source_target_pairs={{4,8},{8,4},{12,16},{16,12},{20,24},{24,20},{28,32},{32,28},{36,40... | collective-permute-start | bytes 589832 | tf_op jit(solution)/shard_map/ppermute | solution.py:616
  20.3 16.2 %all-to-all-start.1 = ((f32[8,40,128]{2,1,0:T(8,128)}), f32[8,40,128]{2,1,0:T(8,128)S(1)}, u32[]{:S(2)}, u32[]{:S(2)}) async-start(f32[8,40,128]{2,1,0:T(8,128)} %get-tuple-element.60), calls=%async_computation.1 | async-start | bytes 327680 | tf_op jit(solution)/shard_map/all_to_all | solution.py:613
  36.5 3.7 %collective-permute-start.2 = (f32[8,40,128]{2,1,0:T(8,128)S(1)}, f32[8,40,128]{2,1,0:T(8,128)S(1)}, u32[]{:S(2)}, u32[]{:S(2)}) collective-permute-start(f32[8,40,128]{2,1,0:T(8,128)S(1)} %all-to-all-done.1.refs_0_.refs_1_.refs_2_), channel_id=1, source_target_pairs={{0,4},{4,0},{8,12},{12,8},{16,20},{20,16},{24,28},{28,24},{32,36},... | collective-permute-start | bytes 491528 | tf_op jit(solution)/shard_map/ppermute | solution.py:640
  43.6 10.5 %all-to-all-start.2 = ((f32[4,104,128]{2,1,0:T(8,128)}), f32[4,104,128]{2,1,0:T(8,128)S(1)}, u32[]{:S(2)}, u32[]{:S(2)}) async-start(f32[4,104,128]{2,1,0:T(8,128)} %get-tuple-element.71), calls=%async_computation.2 | async-start | bytes 425984 | tf_op jit(solution)/shard_map/all_to_all | solution.py:613
  47.7 2.7 %collective-permute-start.3 = (f32[16,1024]{1,0:T(8,128)S(1)}, f32[16,1024]{1,0:T(8,128)S(1)}, u32[]{:S(2)}, u32[]{:S(2)}) collective-permute-start(f32[16,1024]{1,0:T(8,128)S(1)} %get-tuple-element.72), channel_id=1, source_target_pairs={{0,4},{4,0},{8,12},{12,8},{16,20},{20,16},{24,28},{28,24},{32,36},... | collective-permute-start | bytes 196616 | tf_op jit(solution)/shard_map/ppermute | solution.py:616
  48.3 5.9 %collective-permute-start.4 = (f32[16,1024]{1,0:T(8,128)S(1)}, f32[16,1024]{1,0:T(8,128)S(1)}, u32[]{:S(2)}, u32[]{:S(2)}) collective-permute-start(f32[16,1024]{1,0:T(8,128)S(1)} %get-tuple-element.73), channel_id=1, source_target_pairs={{4,8},{8,4},{12,16},{16,12},{20,24},{24,20},{28,32},{32,28},{36,40... | collective-permute-start | bytes 196616 | tf_op jit(solution)/shard_map/ppermute | solution.py:616
  86.2 10.0 %all-to-all-start.5 = ((f32[4,8,128]{2,1,0:T(8,128)}), f32[4,8,128]{2,1,0:T(8,128)S(1)}, u32[]{:S(2)}, u32[]{:S(2)}) async-start(f32[4,8,128]{2,1,0:T(8,128)} %get-tuple-element.92), calls=%async_computation.5 | async-start | bytes 32768 | tf_op jit(solution)/shard_map/all_to_all | solution.py:613
  92.7 9.9 %collective-permute-start.5 = (f32[16,1024]{1,0:T(8,128)S(1)}, f32[16,1024]{1,0:T(8,128)S(1)}, u32[]{:S(2)}, u32[]{:S(2)}) collective-permute-start(f32[16,1024]{1,0:T(8,128)S(1)} %get-tuple-element.98), channel_id=1, source_target_pairs={{0,4},{4,0},{8,12},{12,8},{16,20},{20,16},{24,28},{28,24},{32,36},... | collective-permute-start | bytes 196616 | tf_op jit(solution)/shard_map/ppermute | solution.py:616
  93.9 8.7 %collective-permute-start.6 = (f32[16,1024]{1,0:T(8,128)S(1)}, f32[16,1024]{1,0:T(8,128)S(1)}, u32[]{:S(2)}, u32[]{:S(2)}) collective-permute-start(f32[16,1024]{1,0:T(8,128)S(1)} %get-tuple-element.99), channel_id=1, source_target_pairs={{4,8},{8,4},{12,16},{16,12},{20,24},{24,20},{28,32},{32,28},{36,40... | collective-permute-start | bytes 196616 | tf_op jit(solution)/shard_map/ppermute | solution.py:616
  99.3 7.8 %all-to-all-start.6 = ((f32[4,40,128]{2,1,0:T(8,128)}), f32[4,40,128]{2,1,0:T(8,128)S(1)}, u32[]{:S(2)}, u32[]{:S(2)}) async-start(f32[4,40,128]{2,1,0:T(8,128)} %get-tuple-element.97), calls=%async_computation.6 | async-start | bytes 163840 | tf_op jit(solution)/shard_map/all_to_all | solution.py:613

commit v7 on v5

--- a/solution.py
+++ b/solution.py
@@ -125,26 +125,25 @@
 
 
 def restrict(sub_ref, field_ref, rows_ref, least=0):
-    def group(g, unused):
+    for base in range(0, 64, 16):
+
         def tile(t, totals):
-            rows = pl.ds(pl.multiple_of((t % 2) * 8, 8), 8)
-            sub = sub_ref[t // 2, rows, :]
-            field = field_ref[t // 2, rows, :]
+            at = t // 2
+            rows = pl.ds(pl.multiple_of((at % 2) * 8, 8), 8)
+            lanes = pl.ds(pl.multiple_of((t % 2) * 512, 512), 512)
+            sub = sub_ref[at // 2, rows, lanes]
+            field = field_ref[at // 2, rows, lanes]
             out = []
-            for label in range(8):
-                picked = jnp.where(sub == g * 8 + (label + least), field, 0.0)
-                total = totals[label]
-                for j in range(8):
-                    total = total + picked[:, j * 128 : (j + 1) * 128]
-                out.append(total)
+            for label in range(16):
+                picked = jnp.where(sub == base + label + least, field, 0.0)
+                parts = [picked[:, j * 128 : (j + 1) * 128] for j in range(4)]
+                out.append(totals[label] + ((parts[0] + parts[1]) + (parts[2] + parts[3])))
             return tuple(out)
 
-        totals = lax.fori_loop(0, 8, tile, tuple(jnp.zeros((8, 128), F32) for _ in range(8)))
-        stacked = jnp.concatenate([jnp.sum(t, axis=0, keepdims=True) for t in totals], axis=0)
-        rows_ref[pl.ds(pl.multiple_of(g * 8, 8), 8), :] = stacked
-        return unused
-
-    lax.fori_loop(0, 8, group, 0)
+        totals = lax.fori_loop(0, 16, tile, tuple(jnp.zeros((8, 128), F32) for _ in range(16)), unroll=4)
+        for half in range(0, 16, 8):
+            sums = [jnp.sum(t, axis=0, keepdims=True) for t in totals[half : half + 8]]
+            rows_ref[base + half : base + half + 8, :] = jnp.concatenate(sums, axis=0)
     return jnp.sum(rows_ref[...].T, axis=0, keepdims=True)
 
 

time: 135 us -> 133 us (0.985)
    pallas_call x11, Pallas kernels: 27 us -> 25.7 us  [run(): pl.pallas_call(wrapped, in_specs=[hbm if i in far else vmem for i in rang...]
where the time goes in v7:
time: 133 us; the launch traced here: 132 us
  blocking collectives  46.9 us (35%)
  starting transfers between devices  39.1 us (29%)
  Pallas kernels  25.7 us (19%)
  waiting for transfers between devices  19.9 us (15%)
    all_to_all x3, blocking collectives, exchange(): lax.all_to_all(value, axis, 0, 0, tiled=True, axis_index_groups=groups)  46.9 us
    all_to_all x5, starting transfers between devices, exchange(): lax.all_to_all(value, axis, 0, 0, tiled=True, axis_index_groups=groups)  26.3 us
    pallas_call x11, Pallas kernels, run(): pl.pallas_call(wrapped, in_specs=[hbm if i in far else vmem for i in rang...  25.7 us
    all_to_all x5, waiting for transfers between devices, exchange(): lax.all_to_all(value, axis, 0, 0, tiled=True, axis_index_groups=groups)  13 us
    ppermute x3, starting transfers between devices, swap(): lax.ppermute(to_near, 'slab', with_near)  6.87 us
    ppermute x3, waiting for transfers between devices, swap(): lax.ppermute(to_near, 'slab', with_near)  5.86 us
    ppermute x3, starting transfers between devices, swap(): lax.ppermute(to_core, 'slab', with_core)  3.64 us
  transfers between devices with their start and end apart: 12, of which 7 were waited for; matrix products, arithmetic and copies ran while one was open for 0% of the time, Pallas kernels for 5%

profile of v7, /device:TPU:1, one launch (start us, length us, event | category | flops | bytes accessed | tf_op | source)
XLA Modules:
  0.0 132.4 jit_solution(8277309313606772175)
XLA Ops:
  0.6 4.1 %begin.1 = (f32[4,16,1024]{2,1,0:T(8,128)S(1)}, f32[384,128]{1,0:T(8,128)S(1)}, f32[384,128]{1,0:T(8,128)S(1)}, f32[4,16,1024]{2,1,0:T(8,128)S(1)}, s32[4,16,102...) custom-call(f32[4,16,1024]{2,1,0:T(8,128)} %refs_0_.1, ...), custom_call_target="tpu_custom_call" | custom-call | tf_op jit(solution)/shard_map/begin/pallas_call | solution.py:83
  4.7 5.0 %all-to-all-start = ((f32[4,128,128]{2,1,0:T(8,128)}), f32[4,128,128]{2,1,0:T(8,128)S(1)}, u32[]{:S(2)}, u32[]{:S(2)}) async-start(f32[4,128,128]{2,1,0:T(8,128)} %get-tuple-element.54), calls=%async_computation | async-start | bytes 524288 | tf_op jit(solution)/shard_map/all_to_all | solution.py:619
  9.8 1.7 %collective-permute-start = (f32[384,128]{1,0:T(8,128)S(1)}, f32[384,128]{1,0:T(8,128)S(1)}, u32[]{:S(2)}, u32[]{:S(2)}) collective-permute-start(f32[384,128]{1,0:T(8,128)S(1)} %get-tuple-element.58), channel_id=1, source_target_pairs={{0,4},{4,0},{8,12},{12,8},{16,20},{20,16},{24,28},{28,24},{32,36},... | collective-permute-start | bytes 589832 | tf_op jit(solution)/shard_map/ppermute | solution.py:622
  11.5 2.6 %collective-permute-start.1 = (f32[384,128]{1,0:T(8,128)S(1)}, f32[384,128]{1,0:T(8,128)S(1)}, u32[]{:S(2)}, u32[]{:S(2)}) collective-permute-start(f32[384,128]{1,0:T(8,128)S(1)} %get-tuple-element.59), channel_id=1, source_target_pairs={{4,8},{8,4},{12,16},{16,12},{20,24},{24,20},{28,32},{32,28},{36,40... | collective-permute-start | bytes 589832 | tf_op jit(solution)/shard_map/ppermute | solution.py:622
  14.2 1.1 all-to-all-done.refs_0_.refs_4_
  15.3 1.1 share.1
  16.4 2.1 %collective-permute-done.1.refs_3_ = f32[384,128]{1,0:T(8,128)S(1)} collective-permute-done((f32[384,128]{1,0:T(8,128)S(1)}, f32[384,128]{1,0:T(8,128)S(1)}, u32[]{:S(2)}, u32[]{:S(2)}) %collective-permute-start.1) | collective-permute-done | bytes 196640 | tf_op jit(solution)/shard_map/ppermute | solution.py:622
  18.5 8.2 %all-to-all-start.1 = ((f32[8,40,128]{2,1,0:T(8,128)}), f32[8,40,128]{2,1,0:T(8,128)S(1)}, u32[]{:S(2)}, u32[]{:S(2)}) async-start(f32[8,40,128]{2,1,0:T(8,128)} %get-tuple-element.60), calls=%async_computation.1 | async-start | bytes 327680 | tf_op jit(solution)/shard_map/all_to_all | solution.py:619
  26.7 1.2 setup.1
  27.9 7.3 %all-to-all-done.1.refs_0_.refs_1_.refs_2_ = f32[8,40,128]{2,1,0:T(8,128)S(1)} async-done(((f32[8,40,128]{2,1,0:T(8,128)}), f32[8,40,128]{2,1,0:T(8,128)S(1)}, u32[]{:S(2)}, u32[]{:S(2)}) %all-to-all-start.1) | async-done | bytes 163872 | tf_op jit(solution)/shard_map/all_to_all | solution.py:619
  35.1 2.2 %collective-permute-start.2 = (f32[8,40,128]{2,1,0:T(8,128)S(1)}, f32[8,40,128]{2,1,0:T(8,128)S(1)}, u32[]{:S(2)}, u32[]{:S(2)}) collective-permute-start(f32[8,40,128]{2,1,0:T(8,128)S(1)} %all-to-all-done.1.refs_0_.refs_1_.refs_2_), channel_id=1, source_target_pairs={{0,4},{4,0},{8,12},{12,8},{16,20},{20,16},{24,28},{28,24},{32,36},... | collective-permute-start | bytes 491528 | tf_op jit(solution)/shard_map/ppermute | solution.py:646
  37.4 1.0 collective-permute-done.2.refs_1_.refs_2_.refs_3_
  38.4 3.4 %condense_first.1 = (f32[4,104,128]{2,1,0:T(8,128)}, f32[16,128]{1,0:T(8,128)S(1)}) custom-call(f32[8,40,128]{2,1,0:T(8,128)S(1)} %all-to-all-done.1.refs_0_.refs_1_.refs_2_, f32[8,40,128]{2,1,0:T(8,128)S(1)} %collective-permute-done.2.refs_1_.refs_2_.refs_3_), custom_call_target="tpu_custom_call" | custom-call | tf_op jit(solution)/shard_map/condense_first/pallas_call | solution.py:83
  41.8 4.0 %all-to-all-start.2 = ((f32[4,104,128]{2,1,0:T(8,128)}), f32[4,104,128]{2,1,0:T(8,128)S(1)}, u32[]{:S(2)}, u32[]{:S(2)}) async-start(f32[4,104,128]{2,1,0:T(8,128)} %get-tuple-element.71), calls=%async_computation.2 | async-start | bytes 425984 | tf_op jit(solution)/shard_map/all_to_all | solution.py:619
  45.9 0.6 collective-permute-start.3
  46.5 2.1 %collective-permute-start.4 = (f32[16,1024]{1,0:T(8,128)S(1)}, f32[16,1024]{1,0:T(8,128)S(1)}, u32[]{:S(2)}, u32[]{:S(2)}) collective-permute-start(f32[16,1024]{1,0:T(8,128)S(1)} %get-tuple-element.73), channel_id=1, source_target_pairs={{4,8},{8,4},{12,16},{16,12},{20,24},{24,20},{28,32},{32,28},{36,40... | collective-permute-start | bytes 196616 | tf_op jit(solution)/shard_map/ppermute | solution.py:622
  48.6 3.8 %collective-permute-done.4.refs_2_ = f32[16,1024]{1,0:T(8,128)S(1)} collective-permute-done((f32[16,1024]{1,0:T(8,128)S(1)}, f32[16,1024]{1,0:T(8,128)S(1)}, u32[]{:S(2)}, u32[]{:S(2)}) %collective-permute-start.4) | collective-permute-done | bytes 65568 | tf_op jit(solution)/shard_map/ppermute | solution.py:622
  52.4 3.1 %chain_first.1 = f32[4,40,128]{2,1,0:T(8,128)} custom-call(f32[4,104,128]{2,1,0:T(8,128)S(1)} %all-to-all-done.2.refs_0_, f32[8,40,128]{2,1,0:T(8,128)S(1)} %all-to-all-done.1.refs_0_.refs_1_.refs_2_, f32[8,40,128]{2,1,0:T(8,128)S(1)} %collective-permute-done.2.refs_1_.refs_2_.refs_3_, f32[16,128]{1,0:T(8,128)S(1)} %get-tuple-element.75.refs_3_, ...), custom_call_target="tpu_custom_call" | custom-call | tf_op jit(solution)/shard_map/chain_first/pallas_call | solution.py:83
  55.5 9.1 %all_to_all.40.refs_0_ = f32[4,40,128]{2,1,0:T(8,128)S(1)} all-to-all(f32[4,40,128]{2,1,0:T(8,128)} %chain_first.1), channel_id=1, replica_groups=mesh['slab'=64,'quad'=4] {'quad'}, dimensions={0} | all-to-all | bytes 163840 | tf_op jit(solution)/shard_map/all_to_all | solution.py:619
  64.6 3.9 %first.1 = (f32[4,16,1024]{2,1,0:T(8,128)S(1)}, f32[4,16,1024]{2,1,0:T(8,128)S(1)}, f32[8,8,128]{2,1,0:T(8,128)}) custom-call(f32[4,40,128]{2,1,0:T(8,128)S(1)} %all_to_all.40.refs_0_, f32[16,1024]{1,0:T(8,128)S(1)} %collective-permute-done.3.refs_1_, f32[16,1024]{1,0:T(8,128)S(1)} %collective-permute-done.4.refs_2_, ...), custom_call_target="tpu_custom_call" | custom-call | tf_op jit(solution)/shard_map/first/pallas_call | solution.py:83
  68.5 15.3 %all_to_all.41 = f32[64,1,128]{2,1,0:T(1,128)S(1)} all-to-all(f32[64,1,128]{2,1,0:T(1,128)} %bitcast.15), channel_id=1, replica_groups={{0,1,2,3,4,5,6,7,8,9,10,11,12,13,14,15,16,17,18,19,20,21,22,23,24,25,26..., dimensions={0} | all-to-all | bytes 65536 | tf_op jit(solution)/shard_map/all_to_all | solution.py:619
  83.8 2.2 %condense_second.1 = (f32[4,8,128]{2,1,0:T(8,128)}, f32[16,128]{1,0:T(8,128)S(1)}) custom-call(f32[64,128]{1,0:T(8,128)S(1)} %bitcast.11, f32[8,40,128]{2,1,0:T(8,128)S(1)} %all-to-all-done.1.refs_0_.refs_1_.refs_2_, f32[8,40,128]{2,1,0:T(8,128)S(1)} %collective-permute-done.2.refs_1_.refs_2_.refs_3_), custom_call_target="tpu_custom_call" | custom-call | tf_op jit(solution)/shard_map/condense_second/pallas_call | solution.py:83
  86.0 5.8 %all-to-all-start.5 = ((f32[4,8,128]{2,1,0:T(8,128)}), f32[4,8,128]{2,1,0:T(8,128)S(1)}, u32[]{:S(2)}, u32[]{:S(2)}) async-start(f32[4,8,128]{2,1,0:T(8,128)} %get-tuple-element.92), calls=%async_computation.5 | async-start | bytes 32768 | tf_op jit(solution)/shard_map/all_to_all | solution.py:619
  91.8 0.7 smooth.1
  92.5 1.3 collective-permute-start.5
  93.7 2.1 %collective-permute-start.6 = (f32[16,1024]{1,0:T(8,128)S(1)}, f32[16,1024]{1,0:T(8,128)S(1)}, u32[]{:S(2)}, u32[]{:S(2)}) collective-permute-start(f32[16,1024]{1,0:T(8,128)S(1)} %get-tuple-element.99), channel_id=1, source_target_pairs={{4,8},{8,4},{12,16},{16,12},{20,24},{24,20},{28,32},{32,28},{36,40... | collective-permute-start | bytes 196616 | tf_op jit(solution)/shard_map/ppermute | solution.py:622
  96.0 3.1 %chain_second.1 = (f32[4,40,128]{2,1,0:T(8,128)}, f32[8,128]{1,0:T(8,128)S(1)}) custom-call(f32[4,104,128]{2,1,0:T(8,128)S(1)} %all-to-all-done.2.refs_0_, f32[4,8,128]{2,1,0:T(8,128)S(1)} %all-to-all-done.5.refs_1_, f32[8,40,128]{2,1,0:T(8,128)S(1)} %all-to-all-done.1.refs_0_.refs_1_.refs_2_, ...), custom_call_target="tpu_custom_call" | custom-call | tf_op jit(solution)/shard_map/chain_second/pallas_call | solution.py:83
  99.1 3.3 %all-to-all-start.6 = ((f32[4,40,128]{2,1,0:T(8,128)}), f32[4,40,128]{2,1,0:T(8,128)S(1)}, u32[]{:S(2)}, u32[]{:S(2)}) async-start(f32[4,40,128]{2,1,0:T(8,128)} %get-tuple-element.97), calls=%async_computation.6 | async-start | bytes 163840 | tf_op jit(solution)/shard_map/all_to_all | solution.py:619
  102.4 4.5 %all-to-all-done.6.refs_0_ = f32[4,40,128]{2,1,0:T(8,128)S(1)} async-done(((f32[4,40,128]{2,1,0:T(8,128)}), f32[4,40,128]{2,1,0:T(8,128)S(1)}, u32[]{:S(2)}, u32[]{:S(2)}) %all-to-all-start.6) | async-done | bytes 81952 | tf_op jit(solution)/shard_map/all_to_all | solution.py:619
  106.9 1.8 %second.1 = (f32[4,16,1024]{2,1,0:T(8,128)S(1)}, f32[4,16,1024]{2,1,0:T(8,128)S(1)}, f32[4,16,1024]{2,1,0:T(8,128)S(1)}, f32[32,8,128]{2,1,0:T(8,128)}) custom-call(f32[4,40,128]{2,1,0:T(8,128)S(1)} %all-to-all-done.6.refs_0_, f32[16,1024]{1,0:T(8,128)S(1)} %collective-permute-done.5.refs_1_, f32[16,1024]{1,0:T(8,128)S(1)} %collective-permute-done.6.refs_2_, ...), custom_call_target="tpu_custom_call" | custom-call | tf_op jit(solution)/shard_map/second/pallas_call | solution.py:83
  108.7 22.5 %all_to_all.42 = f32[256,1,128]{2,1,0:T(1,128)S(1)} all-to-all(f32[256,1,128]{2,1,0:T(1,128)} %bitcast.12), channel_id=1, replica_groups=mesh['slab'=64,'quad'=4] {'slab','quad'}, dimensions={0} | all-to-all | bytes 262144 | tf_op jit(solution)/shard_map/all_to_all | solution.py:619
  131.3 1.1 last.1
  (6 shorter events, 0.1 us)
Async XLA Ops:
  4.7 10.6 %all-to-all-start = ((f32[4,128,128]{2,1,0:T(8,128)}), f32[4,128,128]{2,1,0:T(8,128)S(1)}, u32[]{:S(2)}, u32[]{:S(2)}) async-start(f32[4,128,128]{2,1,0:T(8,128)} %get-tuple-element.54), calls=%async_computation | async-start | bytes 524288 | tf_op jit(solution)/shard_map/all_to_all | solution.py:619
  9.8 6.6 %collective-permute-start = (f32[384,128]{1,0:T(8,128)S(1)}, f32[384,128]{1,0:T(8,128)S(1)}, u32[]{:S(2)}, u32[]{:S(2)}) collective-permute-start(f32[384,128]{1,0:T(8,128)S(1)} %get-tuple-element.58), channel_id=1, source_target_pairs={{0,4},{4,0},{8,12},{12,8},{16,20},{20,16},{24,28},{28,24},{32,36},... | collective-permute-start | bytes 589832 | tf_op jit(solution)/shard_map/ppermute | solution.py:622
  11.5 7.0 %collective-permute-start.1 = (f32[384,128]{1,0:T(8,128)S(1)}, f32[384,128]{1,0:T(8,128)S(1)}, u32[]{:S(2)}, u32[]{:S(2)}) collective-permute-start(f32[384,128]{1,0:T(8,128)S(1)} %get-tuple-element.59), channel_id=1, source_target_pairs={{4,8},{8,4},{12,16},{16,12},{20,24},{24,20},{28,32},{32,28},{36,40... | collective-permute-start | bytes 589832 | tf_op jit(solution)/shard_map/ppermute | solution.py:622
  18.5 16.7 %all-to-all-start.1 = ((f32[8,40,128]{2,1,0:T(8,128)}), f32[8,40,128]{2,1,0:T(8,128)S(1)}, u32[]{:S(2)}, u32[]{:S(2)}) async-start(f32[8,40,128]{2,1,0:T(8,128)} %get-tuple-element.60), calls=%async_computation.1 | async-start | bytes 327680 | tf_op jit(solution)/shard_map/all_to_all | solution.py:619
  35.1 3.3 %collective-permute-start.2 = (f32[8,40,128]{2,1,0:T(8,128)S(1)}, f32[8,40,128]{2,1,0:T(8,128)S(1)}, u32[]{:S(2)}, u32[]{:S(2)}) collective-permute-start(f32[8,40,128]{2,1,0:T(8,128)S(1)} %all-to-all-done.1.refs_0_.refs_1_.refs_2_), channel_id=1, source_target_pairs={{0,4},{4,0},{8,12},{12,8},{16,20},{20,16},{24,28},{28,24},{32,36},... | collective-permute-start | bytes 491528 | tf_op jit(solution)/shard_map/ppermute | solution.py:646
  41.8 10.5 %all-to-all-start.2 = ((f32[4,104,128]{2,1,0:T(8,128)}), f32[4,104,128]{2,1,0:T(8,128)S(1)}, u32[]{:S(2)}, u32[]{:S(2)}) async-start(f32[4,104,128]{2,1,0:T(8,128)} %get-tuple-element.71), calls=%async_computation.2 | async-start | bytes 425984 | tf_op jit(solution)/shard_map/all_to_all | solution.py:619
  45.9 2.7 %collective-permute-start.3 = (f32[16,1024]{1,0:T(8,128)S(1)}, f32[16,1024]{1,0:T(8,128)S(1)}, u32[]{:S(2)}, u32[]{:S(2)}) collective-permute-start(f32[16,1024]{1,0:T(8,128)S(1)} %get-tuple-element.72), channel_id=1, source_target_pairs={{0,4},{4,0},{8,12},{12,8},{16,20},{20,16},{24,28},{28,24},{32,36},... | collective-permute-start | bytes 196616 | tf_op jit(solution)/shard_map/ppermute | solution.py:622
  46.5 5.9 %collective-permute-start.4 = (f32[16,1024]{1,0:T(8,128)S(1)}, f32[16,1024]{1,0:T(8,128)S(1)}, u32[]{:S(2)}, u32[]{:S(2)}) collective-permute-start(f32[16,1024]{1,0:T(8,128)S(1)} %get-tuple-element.73), channel_id=1, source_target_pairs={{4,8},{8,4},{12,16},{16,12},{20,24},{24,20},{28,32},{32,28},{36,40... | collective-permute-start | bytes 196616 | tf_op jit(solution)/shard_map/ppermute | solution.py:622
  86.0 10.0 %all-to-all-start.5 = ((f32[4,8,128]{2,1,0:T(8,128)}), f32[4,8,128]{2,1,0:T(8,128)S(1)}, u32[]{:S(2)}, u32[]{:S(2)}) async-start(f32[4,8,128]{2,1,0:T(8,128)} %get-tuple-element.92), calls=%async_computation.5 | async-start | bytes 32768 | tf_op jit(solution)/shard_map/all_to_all | solution.py:619
  92.5 9.9 %collective-permute-start.5 = (f32[16,1024]{1,0:T(8,128)S(1)}, f32[16,1024]{1,0:T(8,128)S(1)}, u32[]{:S(2)}, u32[]{:S(2)}) collective-permute-start(f32[16,1024]{1,0:T(8,128)S(1)} %get-tuple-element.98), channel_id=1, source_target_pairs={{0,4},{4,0},{8,12},{12,8},{16,20},{20,16},{24,28},{28,24},{32,36},... | collective-permute-start | bytes 196616 | tf_op jit(solution)/shard_map/ppermute | solution.py:622
  93.7 8.7 %collective-permute-start.6 = (f32[16,1024]{1,0:T(8,128)S(1)}, f32[16,1024]{1,0:T(8,128)S(1)}, u32[]{:S(2)}, u32[]{:S(2)}) collective-permute-start(f32[16,1024]{1,0:T(8,128)S(1)} %get-tuple-element.99), channel_id=1, source_target_pairs={{4,8},{8,4},{12,16},{16,12},{20,24},{24,20},{28,32},{32,28},{36,40... | collective-permute-start | bytes 196616 | tf_op jit(solution)/shard_map/ppermute | solution.py:622
  99.1 7.8 %all-to-all-start.6 = ((f32[4,40,128]{2,1,0:T(8,128)}), f32[4,40,128]{2,1,0:T(8,128)S(1)}, u32[]{:S(2)}, u32[]{:S(2)}) async-start(f32[4,40,128]{2,1,0:T(8,128)} %get-tuple-element.97), calls=%async_computation.6 | async-start | bytes 163840 | tf_op jit(solution)/shard_map/all_to_all | solution.py:619

commit v8 on v7

--- a/solution.py
+++ b/solution.py
@@ -297,11 +297,6 @@
     send_faces(out, to_core, to_near, ups, downs)
 
 
-def smooth(ready, field, kz, inv, to_core, to_near, ups, downs):
-    out = solve_lines([kz[z] for z in range(5)], [inv[z] for z in range(4)], [field[z] for z in range(4)])
-    send_faces(out, to_core, to_near, ups, downs)
-
-
 def unpack(packed):
     low = lane_of((32, 128)) < 64
     return jnp.concatenate([jnp.where(low, packed, 0.0), jnp.where(low, pltpu.roll(packed, 64, 1), 0.0)], axis=0)
@@ -352,16 +347,15 @@
     return choose(parity(), at_odd[k // 2, rows, :], at_even[k // 2, rows, :])
 
 
-def local_mats(own, other, mats):
-    for k in range(GROUP):
-        mats[k] = unpack(of_slab(own, other, k, slice(0, 32)))
-
-
-def condense_first(ready, own, other, out, rhs_out, mats, tall):
+def local_mats(own, other):
+    return [unpack(of_slab(own, other, k, slice(0, 32))) for k in range(GROUP)]
+
+
+def condense_first(ready, own, other, out, rhs_out, tall):
     rows = [of_slab(own, other, k, slice(32, 33)) for k in range(GROUP)]
     rhs = jnp.where(lane_of((GROUP, 128)) < 64, jnp.concatenate(rows, axis=0), 0.0)
     rhs_out[...] = rhs
-    local_mats(own, other, mats)
+    mats = local_mats(own, other)
     eye = lax.broadcasted_iota(jnp.int32, (64, 64), 0) == lax.broadcasted_iota(jnp.int32, (64, 64), 1)
     one = jnp.where(eye, 1.0, 0.0)
     runs = [[mats[b][:, :64] if b else one] for b in range(0, GROUP, 4)]
@@ -386,8 +380,8 @@
     out[96:104, :] = jnp.concatenate([end, start, rhs[0:1, :], jnp.zeros((5, 128), F32)], axis=0)
 
 
-def condense_second(ready, got, own, other, out, rhs_out, mats):
-    local_mats(own, other, mats)
+def condense_second(ready, got, own, other, out, rhs_out):
+    mats = local_mats(own, other)
     total = got[pl.ds(0, GROUP, 4), :]
     for q in range(1, 4):
         total = total + got[pl.ds(q, GROUP, 4), :]
@@ -473,14 +467,14 @@
         spread(out.at[q], 8, face_for(q, ups[...], downs[...]))
 
 
-def chain_first(ready, bounds, own, other, rhs, fac, beside, ups, downs, out, mats, *work):
-    local_mats(own, other, mats)
+def chain_first(ready, bounds, own, other, rhs, fac, beside, ups, downs, out, *work):
+    mats = local_mats(own, other)
     vecs = [bounds[g, 96:104, :] for g in range(4)]
     chain(ready, bounds, vecs, mats, rhs, fac, beside, ups, downs, out, *work)
 
 
-def chain_second(ready, bounds, got, own, other, rhs, fac, beside, ups, downs, out, dots, mats, *work):
-    local_mats(own, other, mats)
+def chain_second(ready, bounds, got, own, other, rhs, fac, beside, ups, downs, out, dots, *work):
+    mats = local_mats(own, other)
     vecs = [got[g] for g in range(4)]
     total = vecs[0][3:4, :] + vecs[1][3:4, :] + vecs[2][3:4, :] + vecs[3][3:4, :]
     dots[...] = jnp.broadcast_to(total, (8, 128))
@@ -547,13 +541,16 @@
 
 def first(
     ready, got, core, near, sub, zsub, ysub, kz, ky, kyt, kx, kxe, inv, rs, cols,
-    z_out, q_out, pay, rows,
+    z_out, q_out, to_core, to_near, ups, downs, pay, rows,
 ):
     ready(4)
     planes, images = apply(got, rs, core, near, sub, zsub, ysub, kz, ky, kyt, kx, kxe, inv)
     for z in range(4):
         z_out[z] = planes[z]
         q_out[z] = images[z]
+    send_faces(
+        solve_lines([kz[z] for z in range(5)], [inv[z] for z in range(4)], images), to_core, to_near, ups, downs
+    )
     cin = jnp.broadcast_to(restrict(sub, q_out, rows, 1), (8, 64))
     ready(12)
     rz = total_of([rs[z] for z in range(4)], planes)
@@ -644,11 +641,10 @@
     )(rs, mob, core, near, got)
     own, to_core, to_near = lax.optimization_barrier((own, to_core, to_near))
     other = lax.ppermute(own, "slab", with_core)
-    mats = pltpu.VMEM((GROUP, 64, 128), F32)
     pay, rhs = call(
         condense_first,
         (sds(4, 104, 128), sds(GROUP, 128)),
-        [mats, pltpu.VMEM((64, GROUP * 64), F32)],
+        [pltpu.VMEM((64, GROUP * 64), F32)],
         (),
         (0,),
     )(own, other)
@@ -657,7 +653,6 @@
     bounds = exchange(pay, "slab", between)
     bounds, bj_core, bj_near = lax.optimization_barrier((bounds, bj_core, bj_near))
     work = [
-        mats,
         pltpu.VMEM((8, 128), F32),
         pltpu.VMEM((8, 128), F32),
         pltpu.VMEM((5, 64, 128), F32),
@@ -669,13 +664,16 @@
     )
     coarse = exchange(part, "quad")
     stencil = (sub, zsub, ysub, kz, ky, kyt, kx, kxe, inv, rs)
-    z0, q0, pay = call(
-        first, (grid, grid, sds(8, 8, 128)), [pltpu.VMEM((64, 128), F32)], (), (2,)
+    z0, q0, to_core, to_near, ups, downs, pay = call(
+        first,
+        (grid, grid, plane, plane, edge, edge, sds(8, 8, 128)),
+        [pltpu.VMEM((64, 128), F32)],
+        (),
+        (-5, -6, 6),
     )(coarse, bj_core, bj_near, *stencil, cols)
     plane_rows = exchange(pay.reshape(64, 1, 128), BOTH, planes).reshape(64, 128)
-    to_core, to_near, ups, downs = call(smooth, (plane, plane, edge, edge), (), (), (-3, -4))(q0, kz, inv)
     bj_core, bj_near = swap(to_core, to_near)
-    pay, rhs = call(condense_second, (sds(4, 8, 128), sds(GROUP, 128)), [mats], (), (0,))(plane_rows, own, other)
+    pay, rhs = call(condense_second, (sds(4, 8, 128), sds(GROUP, 128)), (), (), (0,))(plane_rows, own, other)
     vecs = exchange(pay, "slab", between)
     part, dots = call(chain_second, (sds(4, 40, 128), sds(8, 128)), work, (7, 8), (-1,))(
         bounds, vecs, own, other, rhs, fac, beside, ups, downs

time: 133 us -> 133 us (level)
    pallas_call x11 -> x10, Pallas kernels: 25.7 us -> 25 us  [run(): pl.pallas_call(wrapped, in_specs=[hbm if i in far else vmem for i in rang...]
  transfers between devices with their start and end apart: 12 -> 12, of which waited for: 7 -> 7; matrix products, arithmetic and copies ran while one was open for 0% -> 0% of each run, Pallas kernels for 5% -> 4%
where the time goes in v8:
time: 133 us; the launch traced here: 132 us
  blocking collectives  46.3 us (35%)
  starting transfers between devices  39 us (29%)
  Pallas kernels  25 us (19%)
  waiting for transfers between devices  20.7 us (16%)
    all_to_all x3, blocking collectives, exchange(): lax.all_to_all(value, axis, 0, 0, tiled=True, axis_index_groups=groups)  46.3 us
    all_to_all x5, starting transfers between devices, exchange(): lax.all_to_all(value, axis, 0, 0, tiled=True, axis_index_groups=groups)  26.3 us
    pallas_call x10, Pallas kernels, run(): pl.pallas_call(wrapped, in_specs=[hbm if i in far else vmem for i in rang...  25 us
    all_to_all x5, waiting for transfers between devices, exchange(): lax.all_to_all(value, axis, 0, 0, tiled=True, axis_index_groups=groups)  13.8 us
    ppermute x3, starting transfers between devices, swap(): lax.ppermute(to_near, 'slab', with_near)  6.84 us
    ppermute x3, waiting for transfers between devices, swap(): lax.ppermute(to_near, 'slab', with_near)  5.86 us
    ppermute x3, starting transfers between devices, swap(): lax.ppermute(to_core, 'slab', with_core)  3.55 us
  transfers between devices with their start and end apart: 12, of which 7 were waited for; matrix products, arithmetic and copies ran while one was open for 0% of the time, Pallas kernels for 4%

profile of v8, /device:TPU:1, one launch (start us, length us, event | category | flops | bytes accessed | tf_op | source)
XLA Modules:
  0.0 131.8 jit_solution(4904676724123550830)
XLA Ops:
  0.6 4.1 %begin.1 = (f32[4,16,1024]{2,1,0:T(8,128)S(1)}, f32[384,128]{1,0:T(8,128)S(1)}, f32[384,128]{1,0:T(8,128)S(1)}, f32[4,16,1024]{2,1,0:T(8,128)S(1)}, s32[4,16,102...) custom-call(f32[4,16,1024]{2,1,0:T(8,128)} %refs_0_.1, ...), custom_call_target="tpu_custom_call" | custom-call | tf_op jit(solution)/shard_map/begin/pallas_call | solution.py:83
  4.7 5.0 %all-to-all-start = ((f32[4,128,128]{2,1,0:T(8,128)}), f32[4,128,128]{2,1,0:T(8,128)S(1)}, u32[]{:S(2)}, u32[]{:S(2)}) async-start(f32[4,128,128]{2,1,0:T(8,128)} %get-tuple-element.54), calls=%async_computation | async-start | bytes 524288 | tf_op jit(solution)/shard_map/all_to_all | solution.py:616
  9.8 1.7 %collective-permute-start = (f32[384,128]{1,0:T(8,128)S(1)}, f32[384,128]{1,0:T(8,128)S(1)}, u32[]{:S(2)}, u32[]{:S(2)}) collective-permute-start(f32[384,128]{1,0:T(8,128)S(1)} %get-tuple-element.58), channel_id=1, source_target_pairs={{0,4},{4,0},{8,12},{12,8},{16,20},{20,16},{24,28},{28,24},{32,36},... | collective-permute-start | bytes 589832 | tf_op jit(solution)/shard_map/ppermute | solution.py:619
  11.5 2.6 %collective-permute-start.1 = (f32[384,128]{1,0:T(8,128)S(1)}, f32[384,128]{1,0:T(8,128)S(1)}, u32[]{:S(2)}, u32[]{:S(2)}) collective-permute-start(f32[384,128]{1,0:T(8,128)S(1)} %get-tuple-element.59), channel_id=1, source_target_pairs={{4,8},{8,4},{12,16},{16,12},{20,24},{24,20},{28,32},{32,28},{36,40... | collective-permute-start | bytes 589832 | tf_op jit(solution)/shard_map/ppermute | solution.py:619
  14.2 1.1 all-to-all-done.refs_0_.refs_4_
  15.3 1.1 share.1
  16.4 2.1 %collective-permute-done.1.refs_3_ = f32[384,128]{1,0:T(8,128)S(1)} collective-permute-done((f32[384,128]{1,0:T(8,128)S(1)}, f32[384,128]{1,0:T(8,128)S(1)}, u32[]{:S(2)}, u32[]{:S(2)}) %collective-permute-start.1) | collective-permute-done | bytes 196640 | tf_op jit(solution)/shard_map/ppermute | solution.py:619
  18.5 8.2 %all-to-all-start.1 = ((f32[8,40,128]{2,1,0:T(8,128)}), f32[8,40,128]{2,1,0:T(8,128)S(1)}, u32[]{:S(2)}, u32[]{:S(2)}) async-start(f32[8,40,128]{2,1,0:T(8,128)} %get-tuple-element.60), calls=%async_computation.1 | async-start | bytes 327680 | tf_op jit(solution)/shard_map/all_to_all | solution.py:616
  26.7 1.2 setup.1
  27.9 7.3 %all-to-all-done.1.refs_0_.refs_1_.refs_2_ = f32[8,40,128]{2,1,0:T(8,128)S(1)} async-done(((f32[8,40,128]{2,1,0:T(8,128)}), f32[8,40,128]{2,1,0:T(8,128)S(1)}, u32[]{:S(2)}, u32[]{:S(2)}) %all-to-all-start.1) | async-done | bytes 163872 | tf_op jit(solution)/shard_map/all_to_all | solution.py:616
  35.1 2.2 %collective-permute-start.2 = (f32[8,40,128]{2,1,0:T(8,128)S(1)}, f32[8,40,128]{2,1,0:T(8,128)S(1)}, u32[]{:S(2)}, u32[]{:S(2)}) collective-permute-start(f32[8,40,128]{2,1,0:T(8,128)S(1)} %all-to-all-done.1.refs_0_.refs_1_.refs_2_), channel_id=1, source_target_pairs={{0,4},{4,0},{8,12},{12,8},{16,20},{20,16},{24,28},{28,24},{32,36},... | collective-permute-start | bytes 491528 | tf_op jit(solution)/shard_map/ppermute | solution.py:643
  37.4 1.0 collective-permute-done.2.refs_1_.refs_2_.refs_3_
  38.4 3.4 %condense_first.1 = (f32[4,104,128]{2,1,0:T(8,128)}, f32[16,128]{1,0:T(8,128)S(1)}) custom-call(f32[8,40,128]{2,1,0:T(8,128)S(1)} %all-to-all-done.1.refs_0_.refs_1_.refs_2_, f32[8,40,128]{2,1,0:T(8,128)S(1)} %collective-permute-done.2.refs_1_.refs_2_.refs_3_), custom_call_target="tpu_custom_call" | custom-call | tf_op jit(solution)/shard_map/condense_first/pallas_call | solution.py:83
  41.8 4.0 %all-to-all-start.2 = ((f32[4,104,128]{2,1,0:T(8,128)}), f32[4,104,128]{2,1,0:T(8,128)S(1)}, u32[]{:S(2)}, u32[]{:S(2)}) async-start(f32[4,104,128]{2,1,0:T(8,128)} %get-tuple-element.71), calls=%async_computation.2 | async-start | bytes 425984 | tf_op jit(solution)/shard_map/all_to_all | solution.py:616
  45.9 0.6 collective-permute-start.3
  46.5 2.1 %collective-permute-start.4 = (f32[16,1024]{1,0:T(8,128)S(1)}, f32[16,1024]{1,0:T(8,128)S(1)}, u32[]{:S(2)}, u32[]{:S(2)}) collective-permute-start(f32[16,1024]{1,0:T(8,128)S(1)} %get-tuple-element.73), channel_id=1, source_target_pairs={{4,8},{8,4},{12,16},{16,12},{20,24},{24,20},{28,32},{32,28},{36,40... | collective-permute-start | bytes 196616 | tf_op jit(solution)/shard_map/ppermute | solution.py:619
  48.6 3.8 %collective-permute-done.4.refs_2_ = f32[16,1024]{1,0:T(8,128)S(1)} collective-permute-done((f32[16,1024]{1,0:T(8,128)S(1)}, f32[16,1024]{1,0:T(8,128)S(1)}, u32[]{:S(2)}, u32[]{:S(2)}) %collective-permute-start.4) | collective-permute-done | bytes 65568 | tf_op jit(solution)/shard_map/ppermute | solution.py:619
  52.4 3.1 %chain_first.1 = f32[4,40,128]{2,1,0:T(8,128)} custom-call(f32[4,104,128]{2,1,0:T(8,128)S(1)} %all-to-all-done.2.refs_0_, f32[8,40,128]{2,1,0:T(8,128)S(1)} %all-to-all-done.1.refs_0_.refs_1_.refs_2_, f32[8,40,128]{2,1,0:T(8,128)S(1)} %collective-permute-done.2.refs_1_.refs_2_.refs_3_, f32[16,128]{1,0:T(8,128)S(1)} %get-tuple-element.75.refs_3_, ...), custom_call_target="tpu_custom_call" | custom-call | tf_op jit(solution)/shard_map/chain_first/pallas_call | solution.py:83
  55.5 9.1 %all_to_all.40.refs_0_ = f32[4,40,128]{2,1,0:T(8,128)S(1)} all-to-all(f32[4,40,128]{2,1,0:T(8,128)} %chain_first.1), channel_id=1, replica_groups=mesh['slab'=64,'quad'=4] {'quad'}, dimensions={0} | all-to-all | bytes 163840 | tf_op jit(solution)/shard_map/all_to_all | solution.py:616
  64.6 4.0 %first.1 = (f32[4,16,1024]{2,1,0:T(8,128)S(1)}, f32[4,16,1024]{2,1,0:T(8,128)S(1)}, f32[16,1024]{1,0:T(8,128)S(1)}, f32[16,1024]{1,0:T(8,128)S(1)}, f32[4,1024]{...) custom-call(f32[4,40,128]{2,1,0:T(8,128)S(1)} %all_to_all.40.refs_0_, ...), custom_call_target="tpu_custom_call" | custom-call | tf_op jit(solution)/shard_map/first/pallas_call | solution.py:83
  68.6 15.3 %all_to_all.41 = f32[64,1,128]{2,1,0:T(1,128)S(1)} all-to-all(f32[64,1,128]{2,1,0:T(1,128)} %bitcast.15), channel_id=1, replica_groups={{0,1,2,3,4,5,6,7,8,9,10,11,12,13,14,15,16,17,18,19,20,21,22,23,24,25,26..., dimensions={0} | all-to-all | bytes 65536 | tf_op jit(solution)/shard_map/all_to_all | solution.py:616
  83.9 2.2 %condense_second.1 = (f32[4,8,128]{2,1,0:T(8,128)}, f32[16,128]{1,0:T(8,128)S(1)}) custom-call(f32[64,128]{1,0:T(8,128)S(1)} %bitcast.11, f32[8,40,128]{2,1,0:T(8,128)S(1)} %all-to-all-done.1.refs_0_.refs_1_.refs_2_, f32[8,40,128]{2,1,0:T(8,128)S(1)} %collective-permute-done.2.refs_1_.refs_2_.refs_3_), custom_call_target="tpu_custom_call" | custom-call | tf_op jit(solution)/shard_map/condense_second/pallas_call | solution.py:83
  86.1 5.8 %all-to-all-start.5 = ((f32[4,8,128]{2,1,0:T(8,128)}), f32[4,8,128]{2,1,0:T(8,128)S(1)}, u32[]{:S(2)}, u32[]{:S(2)}) async-start(f32[4,8,128]{2,1,0:T(8,128)} %get-tuple-element.92), calls=%async_computation.5 | async-start | bytes 32768 | tf_op jit(solution)/shard_map/all_to_all | solution.py:616
  91.8 1.2 collective-permute-start.5
  93.0 2.1 %collective-permute-start.6 = (f32[16,1024]{1,0:T(8,128)S(1)}, f32[16,1024]{1,0:T(8,128)S(1)}, u32[]{:S(2)}, u32[]{:S(2)}) collective-permute-start(f32[16,1024]{1,0:T(8,128)S(1)} %get-tuple-element.98), channel_id=1, source_target_pairs={{4,8},{8,4},{12,16},{16,12},{20,24},{24,20},{28,32},{32,28},{36,40... | collective-permute-start | bytes 196616 | tf_op jit(solution)/shard_map/ppermute | solution.py:619
  95.1 0.9 all-to-all-done.5.refs_1_
  96.0 3.1 %chain_second.1 = (f32[4,40,128]{2,1,0:T(8,128)}, f32[8,128]{1,0:T(8,128)S(1)}) custom-call(f32[4,104,128]{2,1,0:T(8,128)S(1)} %all-to-all-done.2.refs_0_, f32[4,8,128]{2,1,0:T(8,128)S(1)} %all-to-all-done.5.refs_1_, f32[8,40,128]{2,1,0:T(8,128)S(1)} %all-to-all-done.1.refs_0_.refs_1_.refs_2_, ...), custom_call_target="tpu_custom_call" | custom-call | tf_op jit(solution)/shard_map/chain_second/pallas_call | solution.py:83
  99.1 3.3 %all-to-all-start.6 = ((f32[4,40,128]{2,1,0:T(8,128)}), f32[4,40,128]{2,1,0:T(8,128)S(1)}, u32[]{:S(2)}, u32[]{:S(2)}) async-start(f32[4,40,128]{2,1,0:T(8,128)} %get-tuple-element.96), calls=%async_computation.6 | async-start | bytes 163840 | tf_op jit(solution)/shard_map/all_to_all | solution.py:616
  102.5 4.5 %all-to-all-done.6.refs_0_ = f32[4,40,128]{2,1,0:T(8,128)S(1)} async-done(((f32[4,40,128]{2,1,0:T(8,128)}), f32[4,40,128]{2,1,0:T(8,128)S(1)}, u32[]{:S(2)}, u32[]{:S(2)}) %all-to-all-start.6) | async-done | bytes 81952 | tf_op jit(solution)/shard_map/all_to_all | solution.py:616
  107.0 1.8 %second.1 = (f32[4,16,1024]{2,1,0:T(8,128)S(1)}, f32[4,16,1024]{2,1,0:T(8,128)S(1)}, f32[4,16,1024]{2,1,0:T(8,128)S(1)}, f32[32,8,128]{2,1,0:T(8,128)}) custom-call(f32[4,40,128]{2,1,0:T(8,128)S(1)} %all-to-all-done.6.refs_0_, f32[16,1024]{1,0:T(8,128)S(1)} %collective-permute-done.5.refs_1_, f32[16,1024]{1,0:T(8,128)S(1)} %collective-permute-done.6.refs_2_, ...), custom_call_target="tpu_custom_call" | custom-call | tf_op jit(solution)/shard_map/second/pallas_call | solution.py:83
  108.8 21.9 %all_to_all.42 = f32[256,1,128]{2,1,0:T(1,128)S(1)} all-to-all(f32[256,1,128]{2,1,0:T(1,128)} %bitcast.12), channel_id=1, replica_groups=mesh['slab'=64,'quad'=4] {'slab','quad'}, dimensions={0} | all-to-all | bytes 262144 | tf_op jit(solution)/shard_map/all_to_all | solution.py:616
  130.7 1.1 last.1
  (5 shorter events, 0.0 us)
Async XLA Ops:
  4.7 10.6 %all-to-all-start = ((f32[4,128,128]{2,1,0:T(8,128)}), f32[4,128,128]{2,1,0:T(8,128)S(1)}, u32[]{:S(2)}, u32[]{:S(2)}) async-start(f32[4,128,128]{2,1,0:T(8,128)} %get-tuple-element.54), calls=%async_computation | async-start | bytes 524288 | tf_op jit(solution)/shard_map/all_to_all | solution.py:616
  9.8 6.6 %collective-permute-start = (f32[384,128]{1,0:T(8,128)S(1)}, f32[384,128]{1,0:T(8,128)S(1)}, u32[]{:S(2)}, u32[]{:S(2)}) collective-permute-start(f32[384,128]{1,0:T(8,128)S(1)} %get-tuple-element.58), channel_id=1, source_target_pairs={{0,4},{4,0},{8,12},{12,8},{16,20},{20,16},{24,28},{28,24},{32,36},... | collective-permute-start | bytes 589832 | tf_op jit(solution)/shard_map/ppermute | solution.py:619
  11.5 7.0 %collective-permute-start.1 = (f32[384,128]{1,0:T(8,128)S(1)}, f32[384,128]{1,0:T(8,128)S(1)}, u32[]{:S(2)}, u32[]{:S(2)}) collective-permute-start(f32[384,128]{1,0:T(8,128)S(1)} %get-tuple-element.59), channel_id=1, source_target_pairs={{4,8},{8,4},{12,16},{16,12},{20,24},{24,20},{28,32},{32,28},{36,40... | collective-permute-start | bytes 589832 | tf_op jit(solution)/shard_map/ppermute | solution.py:619
  18.5 16.7 %all-to-all-start.1 = ((f32[8,40,128]{2,1,0:T(8,128)}), f32[8,40,128]{2,1,0:T(8,128)S(1)}, u32[]{:S(2)}, u32[]{:S(2)}) async-start(f32[8,40,128]{2,1,0:T(8,128)} %get-tuple-element.60), calls=%async_computation.1 | async-start | bytes 327680 | tf_op jit(solution)/shard_map/all_to_all | solution.py:616
  35.1 3.3 %collective-permute-start.2 = (f32[8,40,128]{2,1,0:T(8,128)S(1)}, f32[8,40,128]{2,1,0:T(8,128)S(1)}, u32[]{:S(2)}, u32[]{:S(2)}) collective-permute-start(f32[8,40,128]{2,1,0:T(8,128)S(1)} %all-to-all-done.1.refs_0_.refs_1_.refs_2_), channel_id=1, source_target_pairs={{0,4},{4,0},{8,12},{12,8},{16,20},{20,16},{24,28},{28,24},{32,36},... | collective-permute-start | bytes 491528 | tf_op jit(solution)/shard_map/ppermute | solution.py:643
  41.8 10.5 %all-to-all-start.2 = ((f32[4,104,128]{2,1,0:T(8,128)}), f32[4,104,128]{2,1,0:T(8,128)S(1)}, u32[]{:S(2)}, u32[]{:S(2)}) async-start(f32[4,104,128]{2,1,0:T(8,128)} %get-tuple-element.71), calls=%async_computation.2 | async-start | bytes 425984 | tf_op jit(solution)/shard_map/all_to_all | solution.py:616
  45.9 2.7 %collective-permute-start.3 = (f32[16,1024]{1,0:T(8,128)S(1)}, f32[16,1024]{1,0:T(8,128)S(1)}, u32[]{:S(2)}, u32[]{:S(2)}) collective-permute-start(f32[16,1024]{1,0:T(8,128)S(1)} %get-tuple-element.72), channel_id=1, source_target_pairs={{0,4},{4,0},{8,12},{12,8},{16,20},{20,16},{24,28},{28,24},{32,36},... | collective-permute-start | bytes 196616 | tf_op jit(solution)/shard_map/ppermute | solution.py:619
  46.5 5.9 %collective-permute-start.4 = (f32[16,1024]{1,0:T(8,128)S(1)}, f32[16,1024]{1,0:T(8,128)S(1)}, u32[]{:S(2)}, u32[]{:S(2)}) collective-permute-start(f32[16,1024]{1,0:T(8,128)S(1)} %get-tuple-element.73), channel_id=1, source_target_pairs={{4,8},{8,4},{12,16},{16,12},{20,24},{24,20},{28,32},{32,28},{36,40... | collective-permute-start | bytes 196616 | tf_op jit(solution)/shard_map/ppermute | solution.py:619
  86.1 10.0 %all-to-all-start.5 = ((f32[4,8,128]{2,1,0:T(8,128)}), f32[4,8,128]{2,1,0:T(8,128)S(1)}, u32[]{:S(2)}, u32[]{:S(2)}) async-start(f32[4,8,128]{2,1,0:T(8,128)} %get-tuple-element.92), calls=%async_computation.5 | async-start | bytes 32768 | tf_op jit(solution)/shard_map/all_to_all | solution.py:616
  91.8 10.6 %collective-permute-start.5 = (f32[16,1024]{1,0:T(8,128)S(1)}, f32[16,1024]{1,0:T(8,128)S(1)}, u32[]{:S(2)}, u32[]{:S(2)}) collective-permute-start(f32[16,1024]{1,0:T(8,128)S(1)} %get-tuple-element.97), channel_id=1, source_target_pairs={{0,4},{4,0},{8,12},{12,8},{16,20},{20,16},{24,28},{28,24},{32,36},... | collective-permute-start | bytes 196616 | tf_op jit(solution)/shard_map/ppermute | solution.py:619
  93.0 9.5 %collective-permute-start.6 = (f32[16,1024]{1,0:T(8,128)S(1)}, f32[16,1024]{1,0:T(8,128)S(1)}, u32[]{:S(2)}, u32[]{:S(2)}) collective-permute-start(f32[16,1024]{1,0:T(8,128)S(1)} %get-tuple-element.98), channel_id=1, source_target_pairs={{4,8},{8,4},{12,16},{16,12},{20,24},{24,20},{28,32},{32,28},{36,40... | collective-permute-start | bytes 196616 | tf_op jit(solution)/shard_map/ppermute | solution.py:619
  99.1 7.8 %all-to-all-start.6 = ((f32[4,40,128]{2,1,0:T(8,128)}), f32[4,40,128]{2,1,0:T(8,128)S(1)}, u32[]{:S(2)}, u32[]{:S(2)}) async-start(f32[4,40,128]{2,1,0:T(8,128)} %get-tuple-element.96), calls=%async_computation.6 | async-start | bytes 163840 | tf_op jit(solution)/shard_map/all_to_all | solution.py:616

commit v9 on v8

--- a/solution.py
+++ b/solution.py
@@ -651,7 +651,6 @@
     pay, to_core, to_near = lax.optimization_barrier((pay, to_core, to_near))
     bj_core, bj_near = swap(to_core, to_near)
     bounds = exchange(pay, "slab", between)
-    bounds, bj_core, bj_near = lax.optimization_barrier((bounds, bj_core, bj_near))
     work = [
         pltpu.VMEM((8, 128), F32),
         pltpu.VMEM((8, 128), F32),

time: 133 us -> 130 us (0.977)
  blocking collectives: 46.3 us -> 38.2 us
  waiting for transfers between devices: 20.7 us -> 24.2 us
  starting transfers between devices: 39 us -> 40.8 us
    all_to_all x3 -> x2, blocking collectives: 46.3 us -> 38.2 us  [exchange(): lax.all_to_all(value, axis, 0, 0, tiled=True, axis_index_groups=groups)]
    all_to_all x5 -> x6, waiting for transfers between devices: 13.8 us -> 21.1 us  [exchange(): lax.all_to_all(value, axis, 0, 0, tiled=True, axis_index_groups=groups)]
    ppermute x3, waiting for transfers between devices: 5.86 us -> 2.08 us  [swap(): lax.ppermute(to_near, 'slab', with_near)]
    all_to_all x5 -> x6, starting transfers between devices: 26.3 us -> 28.3 us  [exchange(): lax.all_to_all(value, axis, 0, 0, tiled=True, axis_index_groups=groups)]
  transfers between devices with their start and end apart: 12 -> 13, of which waited for: 7 -> 8; matrix products, arithmetic and copies ran while one was open for 0% -> 0% of each run, Pallas kernels for 4% -> 7%
where the time goes in v9:
time: 130 us; the launch traced here: 129 us
  starting transfers between devices  40.8 us (31%)
  blocking collectives  38.2 us (29%)
  Pallas kernels  25 us (19%)
  waiting for transfers between devices  24.2 us (19%)
    all_to_all x2, blocking collectives, exchange(): lax.all_to_all(value, axis, 0, 0, tiled=True, axis_index_groups=groups)  38.2 us
    all_to_all x6, starting transfers between devices, exchange(): lax.all_to_all(value, axis, 0, 0, tiled=True, axis_index_groups=groups)  28.3 us
    pallas_call x10, Pallas kernels, run(): pl.pallas_call(wrapped, in_specs=[hbm if i in far else vmem for i in rang...  25 us
    all_to_all x6, waiting for transfers between devices, exchange(): lax.all_to_all(value, axis, 0, 0, tiled=True, axis_index_groups=groups)  21.1 us
    ppermute x3, starting transfers between devices, swap(): lax.ppermute(to_near, 'slab', with_near)  6.87 us
    ppermute x3, starting transfers between devices, swap(): lax.ppermute(to_core, 'slab', with_core)  3.36 us
  transfers between devices with their start and end apart: 13, of which 8 were waited for; matrix products, arithmetic and copies ran while one was open for 0% of the time, Pallas kernels for 7%

profile of v9, /device:TPU:1, one launch (start us, length us, event | category | flops | bytes accessed | tf_op | source)
XLA Modules:
  0.0 129.0 jit_solution(8415538566532587386)
XLA Ops:
  0.6 4.1 %begin.1 = (f32[4,16,1024]{2,1,0:T(8,128)S(1)}, f32[384,128]{1,0:T(8,128)S(1)}, f32[384,128]{1,0:T(8,128)S(1)}, f32[4,16,1024]{2,1,0:T(8,128)S(1)}, s32[4,16,102...) custom-call(f32[4,16,1024]{2,1,0:T(8,128)} %refs_0_.1, ...), custom_call_target="tpu_custom_call" | custom-call | tf_op jit(solution)/shard_map/begin/pallas_call | solution.py:83
  4.7 5.0 %all-to-all-start = ((f32[4,128,128]{2,1,0:T(8,128)}), f32[4,128,128]{2,1,0:T(8,128)S(1)}, u32[]{:S(2)}, u32[]{:S(2)}) async-start(f32[4,128,128]{2,1,0:T(8,128)} %get-tuple-element.51), calls=%async_computation | async-start | bytes 524288 | tf_op jit(solution)/shard_map/all_to_all | solution.py:616
  9.8 1.7 %collective-permute-start = (f32[384,128]{1,0:T(8,128)S(1)}, f32[384,128]{1,0:T(8,128)S(1)}, u32[]{:S(2)}, u32[]{:S(2)}) collective-permute-start(f32[384,128]{1,0:T(8,128)S(1)} %get-tuple-element.55), channel_id=1, source_target_pairs={{0,4},{4,0},{8,12},{12,8},{16,20},{20,16},{24,28},{28,24},{32,36},... | collective-permute-start | bytes 589832 | tf_op jit(solution)/shard_map/ppermute | solution.py:619
  11.5 2.6 %collective-permute-start.1 = (f32[384,128]{1,0:T(8,128)S(1)}, f32[384,128]{1,0:T(8,128)S(1)}, u32[]{:S(2)}, u32[]{:S(2)}) collective-permute-start(f32[384,128]{1,0:T(8,128)S(1)} %get-tuple-element.56), channel_id=1, source_target_pairs={{4,8},{8,4},{12,16},{16,12},{20,24},{24,20},{28,32},{32,28},{36,40... | collective-permute-start | bytes 589832 | tf_op jit(solution)/shard_map/ppermute | solution.py:619
  14.2 1.1 all-to-all-done.refs_0_.refs_4_
  15.3 1.1 share.1
  16.4 2.1 %collective-permute-done.1.refs_3_ = f32[384,128]{1,0:T(8,128)S(1)} collective-permute-done((f32[384,128]{1,0:T(8,128)S(1)}, f32[384,128]{1,0:T(8,128)S(1)}, u32[]{:S(2)}, u32[]{:S(2)}) %collective-permute-start.1) | collective-permute-done | bytes 196640 | tf_op jit(solution)/shard_map/ppermute | solution.py:619
  18.5 8.2 %all-to-all-start.1 = ((f32[8,40,128]{2,1,0:T(8,128)}), f32[8,40,128]{2,1,0:T(8,128)S(1)}, u32[]{:S(2)}, u32[]{:S(2)}) async-start(f32[8,40,128]{2,1,0:T(8,128)} %get-tuple-element.57), calls=%async_computation.1 | async-start | bytes 327680 | tf_op jit(solution)/shard_map/all_to_all | solution.py:616
  26.7 1.2 setup.1
  27.9 7.3 %all-to-all-done.1.refs_0_.refs_1_.refs_2_ = f32[8,40,128]{2,1,0:T(8,128)S(1)} async-done(((f32[8,40,128]{2,1,0:T(8,128)}), f32[8,40,128]{2,1,0:T(8,128)S(1)}, u32[]{:S(2)}, u32[]{:S(2)}) %all-to-all-start.1) | async-done | bytes 163872 | tf_op jit(solution)/shard_map/all_to_all | solution.py:616
  35.1 2.2 %collective-permute-start.2 = (f32[8,40,128]{2,1,0:T(8,128)S(1)}, f32[8,40,128]{2,1,0:T(8,128)S(1)}, u32[]{:S(2)}, u32[]{:S(2)}) collective-permute-start(f32[8,40,128]{2,1,0:T(8,128)S(1)} %all-to-all-done.1.refs_0_.refs_1_.refs_2_), channel_id=1, source_target_pairs={{0,4},{4,0},{8,12},{12,8},{16,20},{20,16},{24,28},{28,24},{32,36},... | collective-permute-start | bytes 491528 | tf_op jit(solution)/shard_map/ppermute | solution.py:643
  37.4 1.0 collective-permute-done.2.refs_1_.refs_2_.refs_3_
  38.4 3.4 %condense_first.1 = (f32[4,104,128]{2,1,0:T(8,128)}, f32[16,128]{1,0:T(8,128)S(1)}) custom-call(f32[8,40,128]{2,1,0:T(8,128)S(1)} %all-to-all-done.1.refs_0_.refs_1_.refs_2_, f32[8,40,128]{2,1,0:T(8,128)S(1)} %collective-permute-done.2.refs_1_.refs_2_.refs_3_), custom_call_target="tpu_custom_call" | custom-call | tf_op jit(solution)/shard_map/condense_first/pallas_call | solution.py:83
  41.8 4.0 %all-to-all-start.2 = ((f32[4,104,128]{2,1,0:T(8,128)}), f32[4,104,128]{2,1,0:T(8,128)S(1)}, u32[]{:S(2)}, u32[]{:S(2)}) async-start(f32[4,104,128]{2,1,0:T(8,128)} %get-tuple-element.68), calls=%async_computation.2 | async-start | bytes 425984 | tf_op jit(solution)/shard_map/all_to_all | solution.py:616
  46.5 2.1 %collective-permute-start.4 = (f32[16,1024]{1,0:T(8,128)S(1)}, f32[16,1024]{1,0:T(8,128)S(1)}, u32[]{:S(2)}, u32[]{:S(2)}) collective-permute-start(f32[16,1024]{1,0:T(8,128)S(1)} %get-tuple-element.74), channel_id=1, source_target_pairs={{4,8},{8,4},{12,16},{16,12},{20,24},{24,20},{28,32},{32,28},{36,40... | collective-permute-start | bytes 196616 | tf_op jit(solution)/shard_map/ppermute | solution.py:619
  48.6 2.6 %all-to-all-done.2.refs_0_ = f32[4,104,128]{2,1,0:T(8,128)S(1)} async-done(((f32[4,104,128]{2,1,0:T(8,128)}), f32[4,104,128]{2,1,0:T(8,128)S(1)}, u32[]{:S(2)}, u32[]{:S(2)}) %all-to-all-start.2) | async-done | bytes 213024 | tf_op jit(solution)/shard_map/all_to_all | solution.py:616
  51.2 3.1 %chain_first.1 = f32[4,40,128]{2,1,0:T(8,128)} custom-call(f32[4,104,128]{2,1,0:T(8,128)S(1)} %all-to-all-done.2.refs_0_, f32[8,40,128]{2,1,0:T(8,128)S(1)} %all-to-all-done.1.refs_0_.refs_1_.refs_2_, f32[8,40,128]{2,1,0:T(8,128)S(1)} %collective-permute-done.2.refs_1_.refs_2_.refs_3_, f32[16,128]{1,0:T(8,128)S(1)} %get-tuple-element.69.refs_3_, ...), custom_call_target="tpu_custom_call" | custom-call | tf_op jit(solution)/shard_map/chain_first/pallas_call | solution.py:83
  54.3 4.5 %all-to-all-start.3 = ((f32[4,40,128]{2,1,0:T(8,128)}), f32[4,40,128]{2,1,0:T(8,128)S(1)}, u32[]{:S(2)}, u32[]{:S(2)}) async-start(f32[4,40,128]{2,1,0:T(8,128)} %chain_first.1), calls=%async_computation.3 | async-start | bytes 163840 | tf_op jit(solution)/shard_map/all_to_all | solution.py:616
  58.8 4.6 %all-to-all-done.3.refs_0_ = f32[4,40,128]{2,1,0:T(8,128)S(1)} async-done(((f32[4,40,128]{2,1,0:T(8,128)}), f32[4,40,128]{2,1,0:T(8,128)S(1)}, u32[]{:S(2)}, u32[]{:S(2)}) %all-to-all-start.3) | async-done | bytes 81952 | tf_op jit(solution)/shard_map/all_to_all | solution.py:616
  63.4 4.0 %first.1 = (f32[4,16,1024]{2,1,0:T(8,128)S(1)}, f32[4,16,1024]{2,1,0:T(8,128)S(1)}, f32[16,1024]{1,0:T(8,128)S(1)}, f32[16,1024]{1,0:T(8,128)S(1)}, f32[4,1024]{...) custom-call(f32[4,40,128]{2,1,0:T(8,128)S(1)} %all-to-all-done.3.refs_0_, ...), custom_call_target="tpu_custom_call" | custom-call | tf_op jit(solution)/shard_map/first/pallas_call | solution.py:83
  67.4 16.5 %all_to_all.40 = f32[64,1,128]{2,1,0:T(1,128)S(1)} all-to-all(f32[64,1,128]{2,1,0:T(1,128)} %bitcast.15), channel_id=1, replica_groups={{0,1,2,3,4,5,6,7,8,9,10,11,12,13,14,15,16,17,18,19,20,21,22,23,24,25,26..., dimensions={0} | all-to-all | bytes 65536 | tf_op jit(solution)/shard_map/all_to_all | solution.py:616
  83.9 2.2 %condense_second.1 = (f32[4,8,128]{2,1,0:T(8,128)}, f32[16,128]{1,0:T(8,128)S(1)}) custom-call(f32[64,128]{1,0:T(8,128)S(1)} %bitcast.11, f32[8,40,128]{2,1,0:T(8,128)S(1)} %all-to-all-done.1.refs_0_.refs_1_.refs_2_, f32[8,40,128]{2,1,0:T(8,128)S(1)} %collective-permute-done.2.refs_1_.refs_2_.refs_3_), custom_call_target="tpu_custom_call" | custom-call | tf_op jit(solution)/shard_map/condense_second/pallas_call | solution.py:83
  86.1 3.3 %all-to-all-start.5 = ((f32[4,8,128]{2,1,0:T(8,128)}), f32[4,8,128]{2,1,0:T(8,128)S(1)}, u32[]{:S(2)}, u32[]{:S(2)}) async-start(f32[4,8,128]{2,1,0:T(8,128)} %get-tuple-element.86), calls=%async_computation.5 | async-start | bytes 32768 | tf_op jit(solution)/shard_map/all_to_all | solution.py:616
  89.3 1.0 collective-permute-start.5
  90.3 2.1 %collective-permute-start.6 = (f32[16,1024]{1,0:T(8,128)S(1)}, f32[16,1024]{1,0:T(8,128)S(1)}, u32[]{:S(2)}, u32[]{:S(2)}) collective-permute-start(f32[16,1024]{1,0:T(8,128)S(1)} %get-tuple-element.92), channel_id=1, source_target_pairs={{4,8},{8,4},{12,16},{16,12},{20,24},{24,20},{28,32},{32,28},{36,40... | collective-permute-start | bytes 196616 | tf_op jit(solution)/shard_map/ppermute | solution.py:619
  92.5 1.0 all-to-all-done.5.refs_1_
  93.5 3.1 %chain_second.1 = (f32[4,40,128]{2,1,0:T(8,128)}, f32[8,128]{1,0:T(8,128)S(1)}) custom-call(f32[4,104,128]{2,1,0:T(8,128)S(1)} %all-to-all-done.2.refs_0_, f32[4,8,128]{2,1,0:T(8,128)S(1)} %all-to-all-done.5.refs_1_, f32[8,40,128]{2,1,0:T(8,128)S(1)} %all-to-all-done.1.refs_0_.refs_1_.refs_2_, ...), custom_call_target="tpu_custom_call" | custom-call | tf_op jit(solution)/shard_map/chain_second/pallas_call | solution.py:83
  96.6 3.3 %all-to-all-start.6 = ((f32[4,40,128]{2,1,0:T(8,128)}), f32[4,40,128]{2,1,0:T(8,128)S(1)}, u32[]{:S(2)}, u32[]{:S(2)}) async-start(f32[4,40,128]{2,1,0:T(8,128)} %get-tuple-element.90), calls=%async_computation.6 | async-start | bytes 163840 | tf_op jit(solution)/shard_map/all_to_all | solution.py:616
  100.0 4.5 %all-to-all-done.6.refs_0_ = f32[4,40,128]{2,1,0:T(8,128)S(1)} async-done(((f32[4,40,128]{2,1,0:T(8,128)}), f32[4,40,128]{2,1,0:T(8,128)S(1)}, u32[]{:S(2)}, u32[]{:S(2)}) %all-to-all-start.6) | async-done | bytes 81952 | tf_op jit(solution)/shard_map/all_to_all | solution.py:616
  104.5 1.8 %second.1 = (f32[4,16,1024]{2,1,0:T(8,128)S(1)}, f32[4,16,1024]{2,1,0:T(8,128)S(1)}, f32[4,16,1024]{2,1,0:T(8,128)S(1)}, f32[32,8,128]{2,1,0:T(8,128)}) custom-call(f32[4,40,128]{2,1,0:T(8,128)S(1)} %all-to-all-done.6.refs_0_, f32[16,1024]{1,0:T(8,128)S(1)} %collective-permute-done.5.refs_1_, f32[16,1024]{1,0:T(8,128)S(1)} %collective-permute-done.6.refs_2_, ...), custom_call_target="tpu_custom_call" | custom-call | tf_op jit(solution)/shard_map/second/pallas_call | solution.py:83
  106.3 21.6 %all_to_all.41 = f32[256,1,128]{2,1,0:T(1,128)S(1)} all-to-all(f32[256,1,128]{2,1,0:T(1,128)} %bitcast.12), channel_id=1, replica_groups=mesh['slab'=64,'quad'=4] {'slab','quad'}, dimensions={0} | all-to-all | bytes 262144 | tf_op jit(solution)/shard_map/all_to_all | solution.py:616
  127.9 1.1 last.1
  (6 shorter events, 0.7 us)
Async XLA Ops:
  4.7 10.6 %all-to-all-start = ((f32[4,128,128]{2,1,0:T(8,128)}), f32[4,128,128]{2,1,0:T(8,128)S(1)}, u32[]{:S(2)}, u32[]{:S(2)}) async-start(f32[4,128,128]{2,1,0:T(8,128)} %get-tuple-element.51), calls=%async_computation | async-start | bytes 524288 | tf_op jit(solution)/shard_map/all_to_all | solution.py:616
  9.8 6.6 %collective-permute-start = (f32[384,128]{1,0:T(8,128)S(1)}, f32[384,128]{1,0:T(8,128)S(1)}, u32[]{:S(2)}, u32[]{:S(2)}) collective-permute-start(f32[384,128]{1,0:T(8,128)S(1)} %get-tuple-element.55), channel_id=1, source_target_pairs={{0,4},{4,0},{8,12},{12,8},{16,20},{20,16},{24,28},{28,24},{32,36},... | collective-permute-start | bytes 589832 | tf_op jit(solution)/shard_map/ppermute | solution.py:619
  11.5 7.0 %collective-permute-start.1 = (f32[384,128]{1,0:T(8,128)S(1)}, f32[384,128]{1,0:T(8,128)S(1)}, u32[]{:S(2)}, u32[]{:S(2)}) collective-permute-start(f32[384,128]{1,0:T(8,128)S(1)} %get-tuple-element.56), channel_id=1, source_target_pairs={{4,8},{8,4},{12,16},{16,12},{20,24},{24,20},{28,32},{32,28},{36,40... | collective-permute-start | bytes 589832 | tf_op jit(solution)/shard_map/ppermute | solution.py:619
  18.5 16.7 %all-to-all-start.1 = ((f32[8,40,128]{2,1,0:T(8,128)}), f32[8,40,128]{2,1,0:T(8,128)S(1)}, u32[]{:S(2)}, u32[]{:S(2)}) async-start(f32[8,40,128]{2,1,0:T(8,128)} %get-tuple-element.57), calls=%async_computation.1 | async-start | bytes 327680 | tf_op jit(solution)/shard_map/all_to_all | solution.py:616
  35.1 3.3 %collective-permute-start.2 = (f32[8,40,128]{2,1,0:T(8,128)S(1)}, f32[8,40,128]{2,1,0:T(8,128)S(1)}, u32[]{:S(2)}, u32[]{:S(2)}) collective-permute-start(f32[8,40,128]{2,1,0:T(8,128)S(1)} %all-to-all-done.1.refs_0_.refs_1_.refs_2_), channel_id=1, source_target_pairs={{0,4},{4,0},{8,12},{12,8},{16,20},{20,16},{24,28},{28,24},{32,36},... | collective-permute-start | bytes 491528 | tf_op jit(solution)/shard_map/ppermute | solution.py:643
  41.8 9.3 %all-to-all-start.2 = ((f32[4,104,128]{2,1,0:T(8,128)}), f32[4,104,128]{2,1,0:T(8,128)S(1)}, u32[]{:S(2)}, u32[]{:S(2)}) async-start(f32[4,104,128]{2,1,0:T(8,128)} %get-tuple-element.68), calls=%async_computation.2 | async-start | bytes 425984 | tf_op jit(solution)/shard_map/all_to_all | solution.py:616
  45.9 12.9 %collective-permute-start.3 = (f32[16,1024]{1,0:T(8,128)S(1)}, f32[16,1024]{1,0:T(8,128)S(1)}, u32[]{:S(2)}, u32[]{:S(2)}) collective-permute-start(f32[16,1024]{1,0:T(8,128)S(1)} %get-tuple-element.73), channel_id=1, source_target_pairs={{0,4},{4,0},{8,12},{12,8},{16,20},{20,16},{24,28},{28,24},{32,36},... | collective-permute-start | bytes 196616 | tf_op jit(solution)/shard_map/ppermute | solution.py:619
  46.5 12.3 %collective-permute-start.4 = (f32[16,1024]{1,0:T(8,128)S(1)}, f32[16,1024]{1,0:T(8,128)S(1)}, u32[]{:S(2)}, u32[]{:S(2)}) collective-permute-start(f32[16,1024]{1,0:T(8,128)S(1)} %get-tuple-element.74), channel_id=1, source_target_pairs={{4,8},{8,4},{12,16},{16,12},{20,24},{24,20},{28,32},{32,28},{36,40... | collective-permute-start | bytes 196616 | tf_op jit(solution)/shard_map/ppermute | solution.py:619
  54.3 9.1 %all-to-all-start.3 = ((f32[4,40,128]{2,1,0:T(8,128)}), f32[4,40,128]{2,1,0:T(8,128)S(1)}, u32[]{:S(2)}, u32[]{:S(2)}) async-start(f32[4,40,128]{2,1,0:T(8,128)} %chain_first.1), calls=%async_computation.3 | async-start | bytes 163840 | tf_op jit(solution)/shard_map/all_to_all | solution.py:616
  86.1 7.5 %all-to-all-start.5 = ((f32[4,8,128]{2,1,0:T(8,128)}), f32[4,8,128]{2,1,0:T(8,128)S(1)}, u32[]{:S(2)}, u32[]{:S(2)}) async-start(f32[4,8,128]{2,1,0:T(8,128)} %get-tuple-element.86), calls=%async_computation.5 | async-start | bytes 32768 | tf_op jit(solution)/shard_map/all_to_all | solution.py:616
  89.3 10.6 %collective-permute-start.5 = (f32[16,1024]{1,0:T(8,128)S(1)}, f32[16,1024]{1,0:T(8,128)S(1)}, u32[]{:S(2)}, u32[]{:S(2)}) collective-permute-start(f32[16,1024]{1,0:T(8,128)S(1)} %get-tuple-element.91), channel_id=1, source_target_pairs={{0,4},{4,0},{8,12},{12,8},{16,20},{20,16},{24,28},{28,24},{32,36},... | collective-permute-start | bytes 196616 | tf_op jit(solution)/shard_map/ppermute | solution.py:619
  90.3 9.6 %collective-permute-start.6 = (f32[16,1024]{1,0:T(8,128)S(1)}, f32[16,1024]{1,0:T(8,128)S(1)}, u32[]{:S(2)}, u32[]{:S(2)}) collective-permute-start(f32[16,1024]{1,0:T(8,128)S(1)} %get-tuple-element.92), channel_id=1, source_target_pairs={{4,8},{8,4},{12,16},{16,12},{20,24},{24,20},{28,32},{32,28},{36,40... | collective-permute-start | bytes 196616 | tf_op jit(solution)/shard_map/ppermute | solution.py:619
  96.6 7.8 %all-to-all-start.6 = ((f32[4,40,128]{2,1,0:T(8,128)}), f32[4,40,128]{2,1,0:T(8,128)S(1)}, u32[]{:S(2)}, u32[]{:S(2)}) async-start(f32[4,40,128]{2,1,0:T(8,128)} %get-tuple-element.90), calls=%async_computation.6 | async-start | bytes 163840 | tf_op jit(solution)/shard_map/all_to_all | solution.py:616
